TPU v7x, 768 devices: a whole 4x8x12 slice. The times are simulated.
768 devices in a mesh: dp: 32 (over y, x), tensor: 24 (over z, core).
Axes of the slice: x: 4, y: 8, z: 12, core: 2. Of those that a mesh axis runs over, the one named last changes fastest.
Arguments:
- kept_input: bfloat16 [18432, 4096], P(('dp', 'tensor')), may hold values from -6 to 6
- kept_grad: bfloat16 [18432, 4096], P(('dp', 'tensor')), may hold values from -6 to 6
- up_weight_t: bfloat16 [8256, 4096], P('tensor'), may hold values from -0.09375 to 0.09375
- up_bias: bfloat16 [8256], P('tensor'), may hold values from -4 to 4
- down_weight: bfloat16 [8256, 4096], P('tensor'), may hold values from -0.0625 to 0.0625
- kept_count: int32 [768], P(('dp', 'tensor')), may hold values from 8 to 24, as said below
Outputs:
- grad_kept: bfloat16 [18432, 4096], P(('dp', 'tensor'))
Inputs may be any that keep to these rules, and one draw needn't show every extreme that they name: `kept_count`: every block keeps at least 8 and at most 24 of its 24 slots, some block exactly 24. Among the 32 blocks of one tensor index taken in order of g, the blocks before block g keep g * 16 + e tokens together with e between -4 and 4, and e is 0 for g = 0 and for g = 32 (all 32 blocks together keep exactly 512 tokens).
All inputs are finite; a program needn't handle non-finite values.
Results may differ from a plain program's by a relative error of at most 0.014.
Values may be sent and summed in bfloat16 or wider, within the bound.
No kernel may reach another device: no remote copies, remote signals or barrier semaphores. Data moves between devices by JAX's collectives and lax.ppermute only.
A program may use at most 64 MiB of HBM per device.

v0:
```python
import jax
import jax.numpy as jnp
from jax import lax
from jax.sharding import PartitionSpec as P

CORES = 2

INV_SQRT_TWO = 0.7071067811865476
INV_SQRT_TWO_PI = 0.3989422804014327


def gelu_slope(values):
    return (
        0.5 * (1.0 + lax.erf(values * INV_SQRT_TWO))
        + values * jnp.exp(-0.5 * values * values) * INV_SQRT_TWO_PI
    )


def with_sibling(block, pairs):
    return jnp.concatenate([block, lax.ppermute(block, "tensor", pairs)], axis=0)


def body(kept_input, kept_grad, up_weight_t, up_bias, down_weight, kept_count):
    slots = kept_input.shape[0]
    members = lax.axis_size("tensor")
    pairs = [(i, i ^ 1) for i in range(members)]
    rings = [list(range(core, members, CORES)) for core in range(CORES)]
    contract = (((1,), (1,)), ((), ()))

    stacked = jnp.stack((kept_input, kept_grad), axis=1)
    stacked, up_weight_t, up_bias, down_weight = lax.optimization_barrier(
        (stacked, up_weight_t, up_bias, down_weight)
    )
    gathered = lax.all_gather(stacked, "tensor", axis=0, tiled=True, axis_index_groups=rings)

    up = with_sibling(up_weight_t, pairs)
    down = with_sibling(down_weight, pairs)
    bias = with_sibling(up_bias, pairs).astype(jnp.float32)

    inputs = gathered[:, 0]
    out_grads = gathered[:, 1]
    preact = lax.dot_general(inputs, up, contract, preferred_element_type=jnp.float32) + bias
    down_grad = lax.dot_general(out_grads, down, contract, preferred_element_type=jnp.float32)
    pre_grad = lax.optimization_barrier((gelu_slope(preact) * down_grad).astype(jnp.bfloat16))
    partials = jnp.dot(pre_grad, up, preferred_element_type=jnp.float32)
    branch = lax.psum_scatter(
        partials.astype(jnp.bfloat16),
        "tensor",
        scatter_dimension=0,
        axis_index_groups=rings,
        tiled=True,
    )
    usable = jnp.arange(slots, dtype=jnp.int32) < kept_count[0]
    summed = kept_grad.astype(jnp.float32) + branch.astype(jnp.float32)
    return jnp.where(usable[:, None], summed, jnp.float32(0.0)).astype(jnp.bfloat16)


def solution(mesh):
    placed = (
        P(("dp", "tensor"), None),
        P(("dp", "tensor"), None),
        P("tensor", None),
        P("tensor"),
        P("tensor", None),
        P(("dp", "tensor")),
    )
    return jax.shard_map(
        body, mesh=mesh, in_specs=placed, out_specs=P(("dp", "tensor"), None), check_vma=False
    )
```

profile of v0, /device:TPU:14, one launch (start us, length us, event | category | flops | bytes accessed | tf_op | source)
XLA Modules:
  0.0 170.8 jit_solution(1429394487622991099)
XLA Ops:
  6.5 0.0 copy-start.1
  6.5 0.0 all-gather.2.cloned.1.call-start
  6.5 1.8 %pad_maximum_fusion = bf16[24,2,4096]{2,0,1:T(8,128)(2,1)} fusion(bf16[24,1,4096]{2,0,1:T(8,128)(2,1)} %bitcast.19, bf16[24,1,4096]{2,0,1:T(8,128)(2,1)} %bitcast.20), kind=kLoop, calls=%fused_computation.16 | loop fusion | flops 196608 | bytes 786432 | tf_op jit(solution)/shard_map/stack | solution.py:30
  8.4 0.0 all-gather.2.cloned.1.call-update
  8.4 0.0 reduce-scatter.2.cloned.1.call-start
  8.4 1.9 %collective-permute-start = (bf16[344,4096]{1,0:T(8,128)(2,1)}, bf16[344,4096]{1,0:T(8,128)(2,1)S(1)}, u32[]{:S(2)}, u32[]{:S(2)}) collective-permute-start(bf16[344,4096]{1,0:T(8,128)(2,1)} %param.8), channel_id=1, source_target_pairs={{0,1},{1,0},{2,3},{3,2},{4,5},{5,4},{6,7},{7,6},{8,9},{9,8},{10,11... | collective-permute-start | bytes 8454152 | tf_op jit(solution)/shard_map/ppermute | solution.py:20
  10.4 2.4 %collective-permute-start.2 = (bf16[344,4096]{1,0:T(8,128)(2,1)}, bf16[344,4096]{1,0:T(8,128)(2,1)}, u32[]{:S(2)}, u32[]{:S(2)}) collective-permute-start(bf16[344,4096]{1,0:T(8,128)(2,1)} %param.10), channel_id=1, source_target_pairs={{0,1},{1,0},{2,3},{3,2},{4,5},{5,4},{6,7},{7,6},{8,9},{9,8},{10,11... | collective-permute-start | bytes 8454152 | tf_op jit(solution)/shard_map/ppermute | solution.py:20
  12.8 1.9 %collective-permute-start.1 = (bf16[344]{0:T(512)(128)(2,1)}, bf16[344]{0:T(512)(128)(2,1)S(1)}, u32[]{:S(2)}, u32[]{:S(2)}) collective-permute-start(bf16[344]{0:T(512)(128)(2,1)} %param.9), channel_id=1, source_target_pairs={{0,1},{1,0},{2,3},{3,2},{4,5},{5,4},{6,7},{7,6},{8,9},{9,8},{10,11... | collective-permute-start | bytes 2072 | tf_op jit(solution)/shard_map/ppermute | solution.py:20
  14.7 3.7 %constant_dynamic-update-slice_fusion.1 = bf16[688,4096]{1,0:T(8,128)(2,1)} fusion(bf16[344,4096]{1,0:T(8,128)(2,1)} %param.8), kind=kLoop, calls=%fused_computation.19 | loop fusion | bytes 5636096
  18.4 1.5 collective-permute-done.1
  19.9 0.0 copy-done.1
  19.9 0.1 maximum_convert_fusion
  20.0 0.0 collective-permute-done
  20.0 1.8 %constant_dynamic-update-slice_fusion = bf16[688,4096]{1,0:T(8,128)(2,1)} fusion(bf16[688,4096]{1,0:T(8,128)(2,1)} %constant_dynamic-update-slice_fusion.1, bf16[344,4096]{1,0:T(8,128)(2,1)S(1)} %collective-permute-done), kind=kLoop, calls=%fused_computation.18 | loop fusion | bytes 5636096 | tf_op jit(solution)/shard_map/concatenate | solution.py:20
  21.8 0.0 copy-start.3
  21.8 63.9 %all-gather.2.cloned.1.call-done = bf16[288,2,4096]{2,0,1:T(8,128)(2,1)} async-done(((bf16[24,2,4096]{2,0,1:T(8,128)(2,1)}), bf16[288,2,4096]{2,0,1:T(8,128)(2,1)}) %all-gather.2.cloned.1.call-update) | async-done | bytes 4718608 | tf_op jit(solution)/shard_map/all_gather | solution.py:34
  85.7 0.0 copy-start.2
  85.7 5.5 %fusion.8 = f32[288,688]{1,0:T(8,128)S(1)} fusion(bf16[688,4096]{1,0:T(8,128)(2,1)} %constant_dynamic-update-slice_fusion, bf16[288,2,4096]{2,0,1:T(8,128)(2,1)} %all-gather.2.cloned.1.call-done, f32[688]{0:T(1024)S(1)} %maximum_convert_fusion), kind=kOutput, calls=%fused_computation.10 | convolution fusion | flops 1623393792 | bytes 8790720 | tf_op jit(solution)/shard_map/dot_general | solution.py:42
  91.2 0.0 collective-permute-done.2
  91.2 0.0 copy-done.3
  91.2 0.0 copy-done.2
  91.2 4.0 %fusion.9 = bf16[288,688]{1,0:T(8,128)(2,1)S(1)} fusion(bf16[344,4096]{1,0:T(8,128)(2,1)} %collective-permute-done.2, bf16[344,4096]{1,0:T(8,128)(2,1)S(1)} %copy-done.3, bf16[288,2,4096]{2,0,1:T(8,128)(2,1)S(1)} %copy-done.2, f32[288,688]{1,0:T(8,128)S(1)} %fusion.8), kind=kOutput, calls=%fused_computation.11 | convolution fusion | flops 1636449280 | bytes 9276416 | tf_op jit(solution)/shard_map/dot_general | solution.py:43
  95.2 0.0 copy-start
  95.2 6.1 %convolution_convert_fusion = bf16[288,4096]{1,0:T(8,128)(2,1)} fusion(bf16[288,688]{1,0:T(8,128)(2,1)S(1)} %fusion.9, bf16[688,4096]{1,0:T(8,128)(2,1)} %constant_dynamic-update-slice_fusion), kind=kOutput, calls=%fused_computation.4 | convolution fusion | flops 1624375296 | bytes 8391680 | tf_op jit(solution)/shard_map/dot_general | solution.py:45
  101.3 0.0 reduce-scatter.2.cloned.1.call-update
  101.9 60.3 %reduce-scatter.2.cloned.1.call-done = bf16[24,4096]{1,0:T(8,128)(2,1)} async-done(((bf16[288,4096]{1,0:T(8,128)(2,1)}), bf16[24,4096]{1,0:T(8,128)(2,1)}) %reduce-scatter.2.cloned.1.call-update) | async-done | bytes 196624 | tf_op jit(solution)/shard_map/reduce_scatter | solution.py:46
  162.3 0.0 copy-done
  162.3 1.7 select_convert_fusion
  (1 shorter events, 0.0 us)
Async XLA Ops:
  6.5 13.4 %copy-start.1 = (bf16[344]{0:T(512)(128)(2,1)S(1)}, bf16[344]{0:T(512)(128)(2,1)}, u32[]{:S(2)}) copy-start(bf16[344]{0:T(512)(128)(2,1)} %param.9) | copy-start | bytes 2068
  6.5 79.1 %all-gather.2.cloned.1.call-start = ((), (), s32[]{:S(2)}) async-start(), calls=%async_computation.1 | async-start | bytes 5111808 | tf_op jit(solution)/shard_map/all_gather | solution.py:34
  8.4 153.9 %reduce-scatter.2.cloned.1.call-start = ((), (), s32[]{:S(2)}) async-start(), calls=%async_computation.2 | async-start | bytes 2555904 | tf_op jit(solution)/shard_map/reduce_scatter | solution.py:46
  8.4 11.5 %collective-permute-start = (bf16[344,4096]{1,0:T(8,128)(2,1)}, bf16[344,4096]{1,0:T(8,128)(2,1)S(1)}, u32[]{:S(2)}, u32[]{:S(2)}) collective-permute-start(bf16[344,4096]{1,0:T(8,128)(2,1)} %param.8), channel_id=1, source_target_pairs={{0,1},{1,0},{2,3},{3,2},{4,5},{5,4},{6,7},{7,6},{8,9},{9,8},{10,11... | collective-permute-start | bytes 8454152 | tf_op jit(solution)/shard_map/ppermute | solution.py:20
  10.4 80.8 %collective-permute-start.2 = (bf16[344,4096]{1,0:T(8,128)(2,1)}, bf16[344,4096]{1,0:T(8,128)(2,1)}, u32[]{:S(2)}, u32[]{:S(2)}) collective-permute-start(bf16[344,4096]{1,0:T(8,128)(2,1)} %param.10), channel_id=1, source_target_pairs={{0,1},{1,0},{2,3},{3,2},{4,5},{5,4},{6,7},{7,6},{8,9},{9,8},{10,11... | collective-permute-start | bytes 8454152 | tf_op jit(solution)/shard_map/ppermute | solution.py:20
  12.8 7.1 %collective-permute-start.1 = (bf16[344]{0:T(512)(128)(2,1)}, bf16[344]{0:T(512)(128)(2,1)S(1)}, u32[]{:S(2)}, u32[]{:S(2)}) collective-permute-start(bf16[344]{0:T(512)(128)(2,1)} %param.9), channel_id=1, source_target_pairs={{0,1},{1,0},{2,3},{3,2},{4,5},{5,4},{6,7},{7,6},{8,9},{9,8},{10,11... | collective-permute-start | bytes 2072 | tf_op jit(solution)/shard_map/ppermute | solution.py:20
  21.8 69.4 %copy-start.3 = (bf16[344,4096]{1,0:T(8,128)(2,1)S(1)}, bf16[344,4096]{1,0:T(8,128)(2,1)}, u32[]{:S(2)}) copy-start(bf16[344,4096]{1,0:T(8,128)(2,1)} %param.10) | copy-start | bytes 8454148
  85.7 5.5 %copy-start.2 = (bf16[288,2,4096]{2,0,1:T(8,128)(2,1)S(1)}, bf16[288,2,4096]{2,0,1:T(8,128)(2,1)}, u32[]{:S(2)}) copy-start(bf16[288,2,4096]{2,0,1:T(8,128)(2,1)} %all-gather.2.cloned.1.call-done) | copy-start | bytes 14155780
  95.2 67.1 %copy-start = (bf16[24,4096]{1,0:T(8,128)(2,1)S(1)}, bf16[24,4096]{1,0:T(8,128)(2,1)}, u32[]{:S(2)}) copy-start(bf16[24,4096]{1,0:T(8,128)(2,1)} %param.7) | copy-start | bytes 589828
Sparse Core Ops, SparseCore 0:
  9.7 75.9 all-gather.1
  101.4 60.8 reduce-scatter.1
where the time goes:
time: 171 us
  waiting for transfers between devices  126 us (74%)
  matrix products  15.5 us (9%)
  between operations  14.1 us (8%)
  starting transfers between devices  6.3 us (4%)
  local copies, waits for them, and re-layouts  5.48 us (3%)
  other arithmetic  3.6 us (2%)
    all_gather x1, waiting for transfers between devices, body(): lax.all_gather(stacked, 'tensor', axis=0, tiled=True, axis_index_groups=r...  63.9 us
    reduce_scatter x1, waiting for transfers between devices, body(): lax.psum_scatter(partials.astype(jnp.bfloat16), 'tensor', scatter_dimensi...  60.3 us
    ppermute x3, starting transfers between devices, with_sibling(): lax.ppermute(block, 'tensor', pairs)  6.25 us
    dot_general x1, matrix products, body(): partials = jnp.dot(pre_grad, up, preferred_element_type=jnp.float32)  6.06 us
    dot_general x1, matrix products, body(): lax.dot_general(inputs, up, contract, preferred_element_type=jnp.float32)  5.49 us
    dot_general x1, matrix products, body(): lax.dot_general(out_grads, down, contract, preferred_element_type=jnp.flo...  3.97 us
    unnamed x9, local copies, waits for them, and re-layouts  3.68 us
  transfers between devices with their start and end apart: 5, of which 3 were waited for; matrix products, arithmetic and copies ran while one was open for 6% of the time, Pallas kernels for 0%

commit v1 on v0

v1 whole, which is shorter than its diff:
```python
import jax
import jax.numpy as jnp
from jax import lax
from jax.sharding import PartitionSpec as P


CORES = 2

INV_SQRT_TWO = 0.7071067811865476
INV_SQRT_TWO_PI = 0.3989422804014327


def gelu_slope(values):
    return (
        0.5 * (1.0 + lax.erf(values * INV_SQRT_TWO))
        + values * jnp.exp(-0.5 * values * values) * INV_SQRT_TWO_PI
    )


def hop(block, pairs):
    return lax.ppermute(block, "tensor", pairs)


def traced(kept_input, kept_grad, up_weight_t, up_bias, down_weight, kept_count):
    slots = kept_input.shape[0]
    members = lax.axis_size("tensor")
    chips = members // CORES
    steps = chips // 2
    core = lax.axis_index("tensor") % CORES
    contract = (((1,), (1,)), ((), ()))
    sibling = [(i, i ^ 1) for i in range(members)]
    out = [
        (i, (i + (CORES if i % CORES == 0 else -CORES)) % members) for i in range(members)
    ]
    home = [(target, source) for source, target in out]
    out_far = [(source, target) for source, target in out if source % CORES == 0]
    home_far = [(target, source) for source, target in out_far]

    mine = jnp.stack((kept_input, kept_grad), axis=0)
    other = hop(mine, sibling)

    def both(block):
        return jnp.concatenate([block, hop(block, sibling)], axis=0)

    up = both(up_weight_t)
    down = both(down_weight)
    bias = both(up_bias).astype(jnp.float32)

    def terms(pieces):
        inputs = jnp.concatenate([piece[0] for piece in pieces], axis=0)
        out_grads = jnp.concatenate([piece[1] for piece in pieces], axis=0)
        preact = lax.dot_general(inputs, up, contract, preferred_element_type=jnp.float32) + bias
        down_grad = lax.dot_general(out_grads, down, contract, preferred_element_type=jnp.float32)
        pre_grad = (gelu_slope(preact) * down_grad).astype(jnp.bfloat16)
        pre_grad = lax.optimization_barrier(pre_grad)
        partials = jnp.dot(pre_grad, up, preferred_element_type=jnp.float32)
        partials = partials.astype(jnp.bfloat16)
        return [partials[i * slots : (i + 1) * slots] for i in range(len(pieces))]

    chain_mine, chain_other = [mine], [other]
    for step in range(1, steps + 1):
        pairs = out if step < steps else out_far
        if step == steps - 1:
            up, down, bias, chain_other[-1] = lax.optimization_barrier(
                (up, down, bias, chain_other[-1])
            )
        chain_mine.append(hop(chain_mine[-1], pairs))
        chain_other.append(hop(chain_other[-1], pairs))
    chain_mine[steps] = jnp.where(core == 0, chain_mine[steps], mine)
    chain_other[steps] = jnp.where(core == 0, chain_other[steps], other)

    near = terms(chain_mine[1:steps] + chain_other[1:steps])
    far_pieces, near = lax.optimization_barrier(
        ([chain_mine[steps], chain_other[steps]], near)
    )
    far = terms(far_pieces)
    for_mine = near[: steps - 1] + far[:1]
    for_other = near[steps - 1 :] + far[1:]

    def add(moved, part):
        return (moved.astype(jnp.float32) + part.astype(jnp.float32)).astype(jnp.bfloat16)

    sum_other = hop(for_other[-1], home_far)
    sum_mine = hop(for_mine[-1], home_far)
    for step in range(2, steps + 1):
        sum_other = hop(add(sum_other, for_other[steps - step]), home)
        sum_mine = hop(add(sum_mine, for_mine[steps - step]), home)
    kept_here = core == 1
    sum_other = sum_other.astype(jnp.float32) + jnp.where(kept_here, for_other[-1], 0.0)
    from_sibling = hop(sum_other.astype(jnp.bfloat16), sibling)
    branch = (
        sum_mine.astype(jnp.float32)
        + jnp.where(kept_here, for_mine[-1], 0.0).astype(jnp.float32)
        + from_sibling.astype(jnp.float32)
    ).astype(jnp.bfloat16)
    usable = jnp.arange(slots, dtype=jnp.int32) < kept_count[0]
    summed = kept_grad.astype(jnp.float32) + branch.astype(jnp.float32)
    return jnp.where(usable[:, None], summed, jnp.float32(0.0)).astype(jnp.bfloat16)


def solution(mesh):
    placed = (
        P(("dp", "tensor"), None),
        P(("dp", "tensor"), None),
        P("tensor", None),
        P("tensor"),
        P("tensor", None),
        P(("dp", "tensor")),
    )
    return jax.shard_map(
        traced, mesh=mesh, in_specs=placed, out_specs=P(("dp", "tensor"), None), check_vma=False
    )
```

time: 171 us -> 183 us (1.070)
  the two profiles are of different devices: /device:TPU:14 before, /device:TPU:1 now
where the time goes in v1:
time: 183 us; the launch traced here: 182 us
  starting transfers between devices  116 us (63%)
  waiting for transfers between devices  32.8 us (18%)
  matrix products  13.1 us (7%)
  local copies, waits for them, and re-layouts  10.3 us (6%)
  other arithmetic  8.17 us (4%)
    ppermute x29, starting transfers between devices, hop(): return lax.ppermute(block, 'tensor', pairs)  116 us
    ppermute x29, waiting for transfers between devices, hop(): return lax.ppermute(block, 'tensor', pairs)  32.8 us
    unnamed x17, local copies, waits for them, and re-layouts  9.18 us
    dot_general x2, matrix products, terms(): lax.dot_general(out_grads, down, contract, preferred_element_type=jnp.flo...  5.21 us
    dot_general x2, matrix products, terms(): lax.dot_general(inputs, up, contract, preferred_element_type=jnp.float32)  5.08 us
  transfers between devices with their start and end apart: 29, of which 15 were waited for; matrix products, arithmetic and copies ran while one was open for 8% of the time, Pallas kernels for 0%

profile of v1, /device:TPU:1, one launch (start us, length us, event | category | flops | bytes accessed | tf_op | source)
XLA Modules:
  0.0 181.5 jit_solution(7121606732500867664)
XLA Ops:
  0.0 1.8 pad_maximum_fusion.2
  1.8 15.1 %collective-permute-start = (bf16[2,24,4096]{2,1,0:T(8,128)(2,1)}, bf16[2,24,4096]{2,1,0:T(8,128)(2,1)S(1)}, u32[]{:S(2)}, u32[]{:S(2)}) collective-permute-start(bf16[2,24,4096]{2,1,0:T(8,128)(2,1)} %pad_maximum_fusion.2), channel_id=1, source_target_pairs={{0,2},{1,23},{2,4},{3,1},{4,6},{5,3},{6,8},{7,5},{8,10},{9,7},{10,... | collective-permute-start | bytes 1179656 | tf_op jit(solution)/shard_map/ppermute | solution.py:21
  16.9 1.9 %collective-permute-start.9 = (bf16[2,24,4096]{2,1,0:T(8,128)(2,1)}, bf16[2,24,4096]{2,1,0:T(8,128)(2,1)}, u32[]{:S(2)}, u32[]{:S(2)}) collective-permute-start(bf16[2,24,4096]{2,1,0:T(8,128)(2,1)} %pad_maximum_fusion.2), channel_id=1, source_target_pairs={{0,1},{1,0},{2,3},{3,2},{4,5},{5,4},{6,7},{7,6},{8,9},{9,8},{10,11... | collective-permute-start | bytes 1179656 | tf_op jit(solution)/shard_map/ppermute | solution.py:21
  18.8 2.4 %collective-permute-start.6 = (bf16[344,4096]{1,0:T(8,128)(2,1)}, bf16[344,4096]{1,0:T(8,128)(2,1)}, u32[]{:S(2)}, u32[]{:S(2)}) collective-permute-start(bf16[344,4096]{1,0:T(8,128)(2,1)} %param.8), channel_id=1, source_target_pairs={{0,1},{1,0},{2,3},{3,2},{4,5},{5,4},{6,7},{7,6},{8,9},{9,8},{10,11... | collective-permute-start | bytes 8454152 | tf_op jit(solution)/shard_map/ppermute | solution.py:21
  21.3 1.9 %collective-permute-start.7 = (bf16[344,4096]{1,0:T(8,128)(2,1)}, bf16[344,4096]{1,0:T(8,128)(2,1)S(1)}, u32[]{:S(2)}, u32[]{:S(2)}) collective-permute-start(bf16[344,4096]{1,0:T(8,128)(2,1)} %param.10), channel_id=1, source_target_pairs={{0,1},{1,0},{2,3},{3,2},{4,5},{5,4},{6,7},{7,6},{8,9},{9,8},{10,11... | collective-permute-start | bytes 8454152 | tf_op jit(solution)/shard_map/ppermute | solution.py:21
  23.2 2.4 %collective-permute-start.8 = (bf16[344]{0:T(512)(128)(2,1)}, bf16[344]{0:T(512)(128)(2,1)S(1)}, u32[]{:S(2)}, u32[]{:S(2)}) collective-permute-start(bf16[344]{0:T(512)(128)(2,1)} %param.9), channel_id=1, source_target_pairs={{0,1},{1,0},{2,3},{3,2},{4,5},{5,4},{6,7},{7,6},{8,9},{9,8},{10,11... | collective-permute-start | bytes 2072 | tf_op jit(solution)/shard_map/ppermute | solution.py:21
  25.6 4.7 %collective-permute-done.8 = bf16[344]{0:T(512)(128)(2,1)S(1)} collective-permute-done((bf16[344]{0:T(512)(128)(2,1)}, bf16[344]{0:T(512)(128)(2,1)S(1)}, u32[]{:S(2)}, u32[]{:S(2)}) %collective-permute-start.8) | collective-permute-done | bytes 720 | tf_op jit(solution)/shard_map/ppermute | solution.py:21
  30.3 0.8 maximum_convert_fusion
  31.1 2.4 %collective-permute-start.1 = (bf16[2,24,4096]{2,1,0:T(8,128)(2,1)S(1)}, bf16[2,24,4096]{2,1,0:T(8,128)(2,1)S(1)}, u32[]{:S(2)}, u32[]{:S(2)}) collective-permute-start(bf16[2,24,4096]{2,1,0:T(8,128)(2,1)S(1)} %collective-permute-done), channel_id=1, source_target_pairs={{0,2},{1,23},{2,4},{3,1},{4,6},{5,3},{6,8},{7,5},{8,10},{9,7},{10,... | collective-permute-start | bytes 1179656 | tf_op jit(solution)/shard_map/ppermute | solution.py:21
  33.5 3.6 %collective-permute-start.10 = (bf16[2,24,4096]{2,1,0:T(8,128)(2,1)}, bf16[2,24,4096]{2,1,0:T(8,128)(2,1)S(1)}, u32[]{:S(2)}, u32[]{:S(2)}) collective-permute-start(bf16[2,24,4096]{2,1,0:T(8,128)(2,1)} %collective-permute-done.9), channel_id=1, source_target_pairs={{0,2},{1,23},{2,4},{3,1},{4,6},{5,3},{6,8},{7,5},{8,10},{9,7},{10,... | collective-permute-start | bytes 1179656 | tf_op jit(solution)/shard_map/ppermute | solution.py:21
  37.2 0.8 fusion.29
  38.0 1.9 %collective-permute-done.1 = bf16[2,24,4096]{2,1,0:T(8,128)(2,1)S(1)} collective-permute-done((bf16[2,24,4096]{2,1,0:T(8,128)(2,1)S(1)}, bf16[2,24,4096]{2,1,0:T(8,128)(2,1)S(1)}, u32[]{:S(2)}, u32[]{:S(2)}) %collective-permute-start.1) | collective-permute-done | bytes 393248 | tf_op jit(solution)/shard_map/ppermute | solution.py:21
  39.9 3.4 %collective-permute-start.2 = (bf16[2,24,4096]{2,1,0:T(8,128)(2,1)S(1)}, bf16[2,24,4096]{2,1,0:T(8,128)(2,1)S(1)}, u32[]{:S(2)}, u32[]{:S(2)}) collective-permute-start(bf16[2,24,4096]{2,1,0:T(8,128)(2,1)S(1)} %collective-permute-done.1), channel_id=1, source_target_pairs={{0,2},{1,23},{2,4},{3,1},{4,6},{5,3},{6,8},{7,5},{8,10},{9,7},{10,... | collective-permute-start | bytes 1179656 | tf_op jit(solution)/shard_map/ppermute | solution.py:21
  43.2 0.8 collective-permute-done.10
  44.1 3.4 %collective-permute-start.11 = (bf16[2,24,4096]{2,1,0:T(8,128)(2,1)S(1)}, bf16[2,24,4096]{2,1,0:T(8,128)(2,1)S(1)}, u32[]{:S(2)}, u32[]{:S(2)}) collective-permute-start(bf16[2,24,4096]{2,1,0:T(8,128)(2,1)S(1)} %collective-permute-done.10), channel_id=1, source_target_pairs={{0,2},{1,23},{2,4},{3,1},{4,6},{5,3},{6,8},{7,5},{8,10},{9,7},{10,... | collective-permute-start | bytes 1179656 | tf_op jit(solution)/shard_map/ppermute | solution.py:21
  47.4 0.8 fusion.28
  48.2 0.5 collective-permute-done.2
  48.7 4.3 %collective-permute-start.3 = (bf16[2,24,4096]{2,1,0:T(8,128)(2,1)S(1)}, bf16[2,24,4096]{2,1,0:T(8,128)(2,1)S(1)}, u32[]{:S(2)}, u32[]{:S(2)}) collective-permute-start(bf16[2,24,4096]{2,1,0:T(8,128)(2,1)S(1)} %collective-permute-done.2), channel_id=1, source_target_pairs={{0,2},{1,23},{2,4},{3,1},{4,6},{5,3},{6,8},{7,5},{8,10},{9,7},{10,... | collective-permute-start | bytes 1179656 | tf_op jit(solution)/shard_map/ppermute | solution.py:21
  53.0 4.2 %collective-permute-start.12 = (bf16[2,24,4096]{2,1,0:T(8,128)(2,1)S(1)}, bf16[2,24,4096]{2,1,0:T(8,128)(2,1)}, u32[]{:S(2)}, u32[]{:S(2)}) collective-permute-start(bf16[2,24,4096]{2,1,0:T(8,128)(2,1)S(1)} %collective-permute-done.11), channel_id=1, source_target_pairs={{0,2},{1,23},{2,4},{3,1},{4,6},{5,3},{6,8},{7,5},{8,10},{9,7},{10,... | collective-permute-start | bytes 1179656 | tf_op jit(solution)/shard_map/ppermute | solution.py:21
  57.2 0.8 fusion.27
  58.0 4.7 %collective-permute-start.4 = (bf16[2,24,4096]{2,1,0:T(8,128)(2,1)S(1)}, bf16[2,24,4096]{2,1,0:T(8,128)(2,1)S(1)}, u32[]{:S(2)}, u32[]{:S(2)}) collective-permute-start(bf16[2,24,4096]{2,1,0:T(8,128)(2,1)S(1)} %collective-permute-done.3), channel_id=1, source_target_pairs={{0,2},{1,23},{2,4},{3,1},{4,6},{5,3},{6,8},{7,5},{8,10},{9,7},{10,... | collective-permute-start | bytes 1179656 | tf_op jit(solution)/shard_map/ppermute | solution.py:21
  62.7 4.3 %collective-permute-start.13 = (bf16[2,24,4096]{2,1,0:T(8,128)(2,1)}, bf16[2,24,4096]{2,1,0:T(8,128)(2,1)}, u32[]{:S(2)}, u32[]{:S(2)}) collective-permute-start(bf16[2,24,4096]{2,1,0:T(8,128)(2,1)} %collective-permute-done.12), channel_id=1, source_target_pairs={{0,2},{1,23},{2,4},{3,1},{4,6},{5,3},{6,8},{7,5},{8,10},{9,7},{10,... | collective-permute-start | bytes 1179656 | tf_op jit(solution)/shard_map/ppermute | solution.py:21
  67.0 0.8 fusion.26
  67.8 0.7 collective-permute-start.5
  68.5 0.8 fusion.25
  69.2 0.8 fusion.24
  70.0 0.8 fusion.23
  70.8 1.9 %fusion.22 = (bf16[240,4096]{1,0:T(8,128)(2,1)}, bf16[240,4096]{1,0:T(8,128)(2,1)}) fusion(bf16[240,4096]{1,0:T(8,128)(2,1)} %get-tuple-element.59, bf16[2,24,4096]{2,1,0:T(8,128)(2,1)} %collective-permute-done.12, bf16[240,4096]{1,0:T(8,128)(2,1)} %get-tuple-element.60), kind=kLoop, calls=%fused_computation.59 | loop fusion | bytes 786432
  72.7 2.5 %pad_maximum_fusion = bf16[688,4096]{1,0:T(8,128)(2,1)S(1)} fusion(bf16[344,4096]{1,0:T(8,128)(2,1)} %collective-permute-done.6, bf16[344,4096]{1,0:T(8,128)(2,1)S(1)} %copy-done), kind=kLoop, calls=%fused_computation | loop fusion | flops 11272192 | bytes 11272192 | tf_op jit(solution)/shard_map/concatenate | solution.py:43
  75.3 0.6 pad_maximum_fusion.1
  76.0 4.6 %collective-permute-start.14 = (bf16[2,24,4096]{2,1,0:T(8,128)(2,1)}, bf16[2,24,4096]{2,1,0:T(8,128)(2,1)S(1)}, u32[]{:S(2)}, u32[]{:S(2)}) collective-permute-start(bf16[2,24,4096]{2,1,0:T(8,128)(2,1)} %collective-permute-done.13), channel_id=1, source_target_pairs={{0,2},{1,23},{2,4},{3,1},{4,6},{5,3},{6,8},{7,5},{8,10},{9,7},{10,... | collective-permute-start | bytes 1179656 | tf_op jit(solution)/shard_map/ppermute | solution.py:21
  80.6 1.8 %bitcast_dynamic-update-slice_fusion.1 = (bf16[240,4096]{1,0:T(8,128)(2,1)}, bf16[240,4096]{1,0:T(8,128)(2,1)}) fusion(bf16[240,4096]{1,0:T(8,128)(2,1)} %get-tuple-element.57, bf16[2,24,4096]{2,1,0:T(8,128)(2,1)} %collective-permute-done.13, bf16[240,4096]{1,0:T(8,128)(2,1)} %get-tuple-element.58), kind=kLoop, calls=%fused_computation.75 | loop fusion | bytes 786432
  82.4 3.2 %collective-permute-done.14 = bf16[2,24,4096]{2,1,0:T(8,128)(2,1)S(1)} collective-permute-done((bf16[2,24,4096]{2,1,0:T(8,128)(2,1)}, bf16[2,24,4096]{2,1,0:T(8,128)(2,1)S(1)}, u32[]{:S(2)}, u32[]{:S(2)}) %collective-permute-start.14) | collective-permute-done | bytes 393248 | tf_op jit(solution)/shard_map/ppermute | solution.py:21
  85.6 0.8 fusion.21
  86.5 3.3 %convolution_add_fusion = f32[240,688]{0,1:T(8,128)S(1)} fusion(bf16[240,4096]{1,0:T(8,128)(2,1)} %get-tuple-element.53, bf16[688,4096]{1,0:T(8,128)(2,1)S(1)} %pad_maximum_fusion, f32[688]{0:T(1024)S(1)} %maximum_convert_fusion), kind=kOutput, calls=%fused_computation.5 | convolution fusion | flops 1352828160 | bytes 8265408 | tf_op jit(solution)/shard_map/dot_general | solution.py:52
  89.8 3.5 %fusion = bf16[240,688]{0,1:T(8,128)(2,1)S(1)} fusion(bf16[240,4096]{1,0:T(8,128)(2,1)} %get-tuple-element.54, bf16[688,4096]{1,0:T(8,128)(2,1)S(1)} %pad_maximum_fusion.1, f32[240,688]{0,1:T(8,128)S(1)} %convolution_add_fusion), kind=kOutput, calls=%fused_computation.6 | convolution fusion | flops 1354314240 | bytes 8592896 | tf_op jit(solution)/shard_map/dot_general | solution.py:53
  93.3 1.8 convolution_convert_fusion
  95.1 0.7 collective-permute-start.15
  96.0 1.0 broadcast_select_fusion
  97.1 1.7 convolution_add_fusion.1
  98.8 1.7 fusion.1
  100.6 1.1 convolution_convert_fusion.1
  101.7 0.7 collective-permute-start.22
  102.4 0.7 collective-permute-start.16
  103.1 1.9 %collective-permute-start.23 = (bf16[24,4096]{1,0:T(8,128)(2,1)S(1)}, bf16[24,4096]{1,0:T(8,128)(2,1)S(1)}, u32[]{:S(2)}, u32[]{:S(2)}) collective-permute-start(bf16[24,4096]{1,0:T(8,128)(2,1)S(1)} %add_convert_fusion.6), channel_id=1, source_target_pairs={{2,0},{23,1},{4,2},{1,3},{6,4},{3,5},{8,6},{5,7},{10,8},{7,9},{12,... | collective-permute-start | bytes 589832 | tf_op jit(solution)/shard_map/ppermute | solution.py:21
  105.1 1.9 %collective-permute-start.17 = (bf16[24,4096]{1,0:T(8,128)(2,1)S(1)}, bf16[24,4096]{1,0:T(8,128)(2,1)S(1)}, u32[]{:S(2)}, u32[]{:S(2)}) collective-permute-start(bf16[24,4096]{1,0:T(8,128)(2,1)S(1)} %add_convert_fusion.11), channel_id=1, source_target_pairs={{2,0},{23,1},{4,2},{1,3},{6,4},{3,5},{8,6},{5,7},{10,8},{7,9},{12,... | collective-permute-start | bytes 589832 | tf_op jit(solution)/shard_map/ppermute | solution.py:21
  107.1 4.0 %collective-permute-done.23 = bf16[24,4096]{1,0:T(8,128)(2,1)S(1)} collective-permute-done((bf16[24,4096]{1,0:T(8,128)(2,1)S(1)}, bf16[24,4096]{1,0:T(8,128)(2,1)S(1)}, u32[]{:S(2)}, u32[]{:S(2)}) %collective-permute-start.23) | collective-permute-done | bytes 196640 | tf_op jit(solution)/shard_map/ppermute | solution.py:21
  111.2 1.9 %collective-permute-start.24 = (bf16[24,4096]{1,0:T(8,128)(2,1)S(1)}, bf16[24,4096]{1,0:T(8,128)(2,1)S(1)}, u32[]{:S(2)}, u32[]{:S(2)}) collective-permute-start(bf16[24,4096]{1,0:T(8,128)(2,1)S(1)} %add_convert_fusion.5), channel_id=1, source_target_pairs={{2,0},{23,1},{4,2},{1,3},{6,4},{3,5},{8,6},{5,7},{10,8},{7,9},{12,... | collective-permute-start | bytes 589832 | tf_op jit(solution)/shard_map/ppermute | solution.py:21
  113.3 1.9 %collective-permute-start.18 = (bf16[24,4096]{1,0:T(8,128)(2,1)S(1)}, bf16[24,4096]{1,0:T(8,128)(2,1)S(1)}, u32[]{:S(2)}, u32[]{:S(2)}) collective-permute-start(bf16[24,4096]{1,0:T(8,128)(2,1)S(1)} %add_convert_fusion.10), channel_id=1, source_target_pairs={{2,0},{23,1},{4,2},{1,3},{6,4},{3,5},{8,6},{5,7},{10,8},{7,9},{12,... | collective-permute-start | bytes 589832 | tf_op jit(solution)/shard_map/ppermute | solution.py:21
  115.2 6.0 %collective-permute-done.24 = bf16[24,4096]{1,0:T(8,128)(2,1)S(1)} collective-permute-done((bf16[24,4096]{1,0:T(8,128)(2,1)S(1)}, bf16[24,4096]{1,0:T(8,128)(2,1)S(1)}, u32[]{:S(2)}, u32[]{:S(2)}) %collective-permute-start.24) | collective-permute-done | bytes 196640 | tf_op jit(solution)/shard_map/ppermute | solution.py:21
  121.2 1.9 %collective-permute-start.25 = (bf16[24,4096]{1,0:T(8,128)(2,1)S(1)}, bf16[24,4096]{1,0:T(8,128)(2,1)S(1)}, u32[]{:S(2)}, u32[]{:S(2)}) collective-permute-start(bf16[24,4096]{1,0:T(8,128)(2,1)S(1)} %add_convert_fusion.4), channel_id=1, source_target_pairs={{2,0},{23,1},{4,2},{1,3},{6,4},{3,5},{8,6},{5,7},{10,8},{7,9},{12,... | collective-permute-start | bytes 589832 | tf_op jit(solution)/shard_map/ppermute | solution.py:21
  123.2 0.9 collective-permute-done.18
  124.1 1.9 %collective-permute-start.19 = (bf16[24,4096]{1,0:T(8,128)(2,1)S(1)}, bf16[24,4096]{1,0:T(8,128)(2,1)S(1)}, u32[]{:S(2)}, u32[]{:S(2)}) collective-permute-start(bf16[24,4096]{1,0:T(8,128)(2,1)S(1)} %add_convert_fusion.9), channel_id=1, source_target_pairs={{2,0},{23,1},{4,2},{1,3},{6,4},{3,5},{8,6},{5,7},{10,8},{7,9},{12,... | collective-permute-start | bytes 589832 | tf_op jit(solution)/shard_map/ppermute | solution.py:21
  126.0 2.8 %collective-permute-done.25 = bf16[24,4096]{1,0:T(8,128)(2,1)S(1)} collective-permute-done((bf16[24,4096]{1,0:T(8,128)(2,1)S(1)}, bf16[24,4096]{1,0:T(8,128)(2,1)S(1)}, u32[]{:S(2)}, u32[]{:S(2)}) %collective-permute-start.25) | collective-permute-done | bytes 196640 | tf_op jit(solution)/shard_map/ppermute | solution.py:21
  128.9 1.9 %collective-permute-start.26 = (bf16[24,4096]{1,0:T(8,128)(2,1)S(1)}, bf16[24,4096]{1,0:T(8,128)(2,1)S(1)}, u32[]{:S(2)}, u32[]{:S(2)}) collective-permute-start(bf16[24,4096]{1,0:T(8,128)(2,1)S(1)} %add_convert_fusion.3), channel_id=1, source_target_pairs={{2,0},{23,1},{4,2},{1,3},{6,4},{3,5},{8,6},{5,7},{10,8},{7,9},{12,... | collective-permute-start | bytes 589832 | tf_op jit(solution)/shard_map/ppermute | solution.py:21
  130.9 0.9 collective-permute-done.19
  131.8 1.9 %collective-permute-start.20 = (bf16[24,4096]{1,0:T(8,128)(2,1)S(1)}, bf16[24,4096]{1,0:T(8,128)(2,1)S(1)}, u32[]{:S(2)}, u32[]{:S(2)}) collective-permute-start(bf16[24,4096]{1,0:T(8,128)(2,1)S(1)} %add_convert_fusion.8), channel_id=1, source_target_pairs={{2,0},{23,1},{4,2},{1,3},{6,4},{3,5},{8,6},{5,7},{10,8},{7,9},{12,... | collective-permute-start | bytes 589832 | tf_op jit(solution)/shard_map/ppermute | solution.py:21
  133.7 2.8 %collective-permute-done.26 = bf16[24,4096]{1,0:T(8,128)(2,1)S(1)} collective-permute-done((bf16[24,4096]{1,0:T(8,128)(2,1)S(1)}, bf16[24,4096]{1,0:T(8,128)(2,1)S(1)}, u32[]{:S(2)}, u32[]{:S(2)}) %collective-permute-start.26) | collective-permute-done | bytes 196640 | tf_op jit(solution)/shard_map/ppermute | solution.py:21
  136.6 1.9 %collective-permute-start.27 = (bf16[24,4096]{1,0:T(8,128)(2,1)S(1)}, bf16[24,4096]{1,0:T(8,128)(2,1)S(1)}, u32[]{:S(2)}, u32[]{:S(2)}) collective-permute-start(bf16[24,4096]{1,0:T(8,128)(2,1)S(1)} %add_convert_fusion.2), channel_id=1, source_target_pairs={{2,0},{23,1},{4,2},{1,3},{6,4},{3,5},{8,6},{5,7},{10,8},{7,9},{12,... | collective-permute-start | bytes 589832 | tf_op jit(solution)/shard_map/ppermute | solution.py:21
  138.5 0.9 collective-permute-done.20
  139.5 1.9 %collective-permute-start.21 = (bf16[24,4096]{1,0:T(8,128)(2,1)S(1)}, bf16[24,4096]{1,0:T(8,128)(2,1)S(1)}, u32[]{:S(2)}, u32[]{:S(2)}) collective-permute-start(bf16[24,4096]{1,0:T(8,128)(2,1)S(1)} %add_convert_fusion.7), channel_id=1, source_target_pairs={{2,0},{23,1},{4,2},{1,3},{6,4},{3,5},{8,6},{5,7},{10,8},{7,9},{12,... | collective-permute-start | bytes 589832 | tf_op jit(solution)/shard_map/ppermute | solution.py:21
  141.4 2.8 %collective-permute-done.27 = bf16[24,4096]{1,0:T(8,128)(2,1)S(1)} collective-permute-done((bf16[24,4096]{1,0:T(8,128)(2,1)S(1)}, bf16[24,4096]{1,0:T(8,128)(2,1)S(1)}, u32[]{:S(2)}, u32[]{:S(2)}) %collective-permute-start.27) | collective-permute-done | bytes 196640 | tf_op jit(solution)/shard_map/ppermute | solution.py:21
  144.3 35.4 %collective-permute-start.28 = (bf16[24,4096]{1,0:T(8,128)(2,1)S(1)}, bf16[24,4096]{1,0:T(8,128)(2,1)S(1)}, u32[]{:S(2)}, u32[]{:S(2)}) collective-permute-start(bf16[24,4096]{1,0:T(8,128)(2,1)S(1)} %add_convert_fusion.1), channel_id=1, source_target_pairs={{0,1},{1,0},{2,3},{3,2},{4,5},{5,4},{6,7},{7,6},{8,9},{9,8},{10,11... | collective-permute-start | bytes 589832 | tf_op jit(solution)/shard_map/ppermute | solution.py:21
  180.7 0.8 select_convert_fusion
  (40 shorter events, 1.5 us)
Async XLA Ops:
  1.8 29.3 %collective-permute-start = (bf16[2,24,4096]{2,1,0:T(8,128)(2,1)}, bf16[2,24,4096]{2,1,0:T(8,128)(2,1)S(1)}, u32[]{:S(2)}, u32[]{:S(2)}) collective-permute-start(bf16[2,24,4096]{2,1,0:T(8,128)(2,1)} %pad_maximum_fusion.2), channel_id=1, source_target_pairs={{0,2},{1,23},{2,4},{3,1},{4,6},{5,3},{6,8},{7,5},{8,10},{9,7},{10,... | collective-permute-start | bytes 1179656 | tf_op jit(solution)/shard_map/ppermute | solution.py:21
  16.9 16.6 %collective-permute-start.9 = (bf16[2,24,4096]{2,1,0:T(8,128)(2,1)}, bf16[2,24,4096]{2,1,0:T(8,128)(2,1)}, u32[]{:S(2)}, u32[]{:S(2)}) collective-permute-start(bf16[2,24,4096]{2,1,0:T(8,128)(2,1)} %pad_maximum_fusion.2), channel_id=1, source_target_pairs={{0,1},{1,0},{2,3},{3,2},{4,5},{5,4},{6,7},{7,6},{8,9},{9,8},{10,11... | collective-permute-start | bytes 1179656 | tf_op jit(solution)/shard_map/ppermute | solution.py:21
  18.8 53.9 %collective-permute-start.6 = (bf16[344,4096]{1,0:T(8,128)(2,1)}, bf16[344,4096]{1,0:T(8,128)(2,1)}, u32[]{:S(2)}, u32[]{:S(2)}) collective-permute-start(bf16[344,4096]{1,0:T(8,128)(2,1)} %param.8), channel_id=1, source_target_pairs={{0,1},{1,0},{2,3},{3,2},{4,5},{5,4},{6,7},{7,6},{8,9},{9,8},{10,11... | collective-permute-start | bytes 8454152 | tf_op jit(solution)/shard_map/ppermute | solution.py:21
  21.3 54.0 %collective-permute-start.7 = (bf16[344,4096]{1,0:T(8,128)(2,1)}, bf16[344,4096]{1,0:T(8,128)(2,1)S(1)}, u32[]{:S(2)}, u32[]{:S(2)}) collective-permute-start(bf16[344,4096]{1,0:T(8,128)(2,1)} %param.10), channel_id=1, source_target_pairs={{0,1},{1,0},{2,3},{3,2},{4,5},{5,4},{6,7},{7,6},{8,9},{9,8},{10,11... | collective-permute-start | bytes 8454152 | tf_op jit(solution)/shard_map/ppermute | solution.py:21
  23.2 7.1 %collective-permute-start.8 = (bf16[344]{0:T(512)(128)(2,1)}, bf16[344]{0:T(512)(128)(2,1)S(1)}, u32[]{:S(2)}, u32[]{:S(2)}) collective-permute-start(bf16[344]{0:T(512)(128)(2,1)} %param.9), channel_id=1, source_target_pairs={{0,1},{1,0},{2,3},{3,2},{4,5},{5,4},{6,7},{7,6},{8,9},{9,8},{10,11... | collective-permute-start | bytes 2072 | tf_op jit(solution)/shard_map/ppermute | solution.py:21
  31.1 8.8 %collective-permute-start.1 = (bf16[2,24,4096]{2,1,0:T(8,128)(2,1)S(1)}, bf16[2,24,4096]{2,1,0:T(8,128)(2,1)S(1)}, u32[]{:S(2)}, u32[]{:S(2)}) collective-permute-start(bf16[2,24,4096]{2,1,0:T(8,128)(2,1)S(1)} %collective-permute-done), channel_id=1, source_target_pairs={{0,2},{1,23},{2,4},{3,1},{4,6},{5,3},{6,8},{7,5},{8,10},{9,7},{10,... | collective-permute-start | bytes 1179656 | tf_op jit(solution)/shard_map/ppermute | solution.py:21
  33.5 10.6 %collective-permute-start.10 = (bf16[2,24,4096]{2,1,0:T(8,128)(2,1)}, bf16[2,24,4096]{2,1,0:T(8,128)(2,1)S(1)}, u32[]{:S(2)}, u32[]{:S(2)}) collective-permute-start(bf16[2,24,4096]{2,1,0:T(8,128)(2,1)} %collective-permute-done.9), channel_id=1, source_target_pairs={{0,2},{1,23},{2,4},{3,1},{4,6},{5,3},{6,8},{7,5},{8,10},{9,7},{10,... | collective-permute-start | bytes 1179656 | tf_op jit(solution)/shard_map/ppermute | solution.py:21
  39.9 8.8 %collective-permute-start.2 = (bf16[2,24,4096]{2,1,0:T(8,128)(2,1)S(1)}, bf16[2,24,4096]{2,1,0:T(8,128)(2,1)S(1)}, u32[]{:S(2)}, u32[]{:S(2)}) collective-permute-start(bf16[2,24,4096]{2,1,0:T(8,128)(2,1)S(1)} %collective-permute-done.1), channel_id=1, source_target_pairs={{0,2},{1,23},{2,4},{3,1},{4,6},{5,3},{6,8},{7,5},{8,10},{9,7},{10,... | collective-permute-start | bytes 1179656 | tf_op jit(solution)/shard_map/ppermute | solution.py:21
  44.1 8.9 %collective-permute-start.11 = (bf16[2,24,4096]{2,1,0:T(8,128)(2,1)S(1)}, bf16[2,24,4096]{2,1,0:T(8,128)(2,1)S(1)}, u32[]{:S(2)}, u32[]{:S(2)}) collective-permute-start(bf16[2,24,4096]{2,1,0:T(8,128)(2,1)S(1)} %collective-permute-done.10), channel_id=1, source_target_pairs={{0,2},{1,23},{2,4},{3,1},{4,6},{5,3},{6,8},{7,5},{8,10},{9,7},{10,... | collective-permute-start | bytes 1179656 | tf_op jit(solution)/shard_map/ppermute | solution.py:21
  48.7 9.3 %collective-permute-start.3 = (bf16[2,24,4096]{2,1,0:T(8,128)(2,1)S(1)}, bf16[2,24,4096]{2,1,0:T(8,128)(2,1)S(1)}, u32[]{:S(2)}, u32[]{:S(2)}) collective-permute-start(bf16[2,24,4096]{2,1,0:T(8,128)(2,1)S(1)} %collective-permute-done.2), channel_id=1, source_target_pairs={{0,2},{1,23},{2,4},{3,1},{4,6},{5,3},{6,8},{7,5},{8,10},{9,7},{10,... | collective-permute-start | bytes 1179656 | tf_op jit(solution)/shard_map/ppermute | solution.py:21
  53.0 9.7 %collective-permute-start.12 = (bf16[2,24,4096]{2,1,0:T(8,128)(2,1)S(1)}, bf16[2,24,4096]{2,1,0:T(8,128)(2,1)}, u32[]{:S(2)}, u32[]{:S(2)}) collective-permute-start(bf16[2,24,4096]{2,1,0:T(8,128)(2,1)S(1)} %collective-permute-done.11), channel_id=1, source_target_pairs={{0,2},{1,23},{2,4},{3,1},{4,6},{5,3},{6,8},{7,5},{8,10},{9,7},{10,... | collective-permute-start | bytes 1179656 | tf_op jit(solution)/shard_map/ppermute | solution.py:21
  58.0 9.8 %collective-permute-start.4 = (bf16[2,24,4096]{2,1,0:T(8,128)(2,1)S(1)}, bf16[2,24,4096]{2,1,0:T(8,128)(2,1)S(1)}, u32[]{:S(2)}, u32[]{:S(2)}) collective-permute-start(bf16[2,24,4096]{2,1,0:T(8,128)(2,1)S(1)} %collective-permute-done.3), channel_id=1, source_target_pairs={{0,2},{1,23},{2,4},{3,1},{4,6},{5,3},{6,8},{7,5},{8,10},{9,7},{10,... | collective-permute-start | bytes 1179656 | tf_op jit(solution)/shard_map/ppermute | solution.py:21
  62.7 13.3 %collective-permute-start.13 = (bf16[2,24,4096]{2,1,0:T(8,128)(2,1)}, bf16[2,24,4096]{2,1,0:T(8,128)(2,1)}, u32[]{:S(2)}, u32[]{:S(2)}) collective-permute-start(bf16[2,24,4096]{2,1,0:T(8,128)(2,1)} %collective-permute-done.12), channel_id=1, source_target_pairs={{0,2},{1,23},{2,4},{3,1},{4,6},{5,3},{6,8},{7,5},{8,10},{9,7},{10,... | collective-permute-start | bytes 1179656 | tf_op jit(solution)/shard_map/ppermute | solution.py:21
  67.0 5.6 %copy-start.2 = (bf16[24,4096]{1,0:T(8,128)(2,1)S(1)}, bf16[24,4096]{1,0:T(8,128)(2,1)}, u32[]{:S(2)}) copy-start(bf16[24,4096]{1,0:T(8,128)(2,1)} %param.7) | copy-start | bytes 589828
  67.0 5.6 %copy-start.3 = (bf16[24,4096]{1,0:T(8,128)(2,1)S(1)}, bf16[24,4096]{1,0:T(8,128)(2,1)}, u32[]{:S(2)}) copy-start(bf16[24,4096]{1,0:T(8,128)(2,1)} %param.6) | copy-start | bytes 589828
  67.8 4.8 %collective-permute-start.5 = (bf16[2,24,4096]{2,1,0:T(8,128)(2,1)S(1)}, bf16[2,24,4096]{2,1,0:T(8,128)(2,1)S(1)}, u32[]{:S(2)}, u32[]{:S(2)}) collective-permute-start(bf16[2,24,4096]{2,1,0:T(8,128)(2,1)S(1)} %collective-permute-done.4), channel_id=1, source_target_pairs={{0,2},{2,4},{4,6},{6,8},{8,10},{10,12},{12,14},{14,16},{16,18},{18... | collective-permute-start | bytes 1179656 | tf_op jit(solution)/shard_map/ppermute | solution.py:21
  69.2 3.5 %copy-start = (bf16[344,4096]{1,0:T(8,128)(2,1)S(1)}, bf16[344,4096]{1,0:T(8,128)(2,1)}, u32[]{:S(2)}) copy-start(bf16[344,4096]{1,0:T(8,128)(2,1)} %param.8) | copy-start | bytes 8454148
  72.7 2.6 %copy-start.1 = (bf16[344,4096]{1,0:T(8,128)(2,1)S(1)}, bf16[344,4096]{1,0:T(8,128)(2,1)}, u32[]{:S(2)}) copy-start(bf16[344,4096]{1,0:T(8,128)(2,1)} %param.10) | copy-start | bytes 8454148
  76.0 9.6 %collective-permute-start.14 = (bf16[2,24,4096]{2,1,0:T(8,128)(2,1)}, bf16[2,24,4096]{2,1,0:T(8,128)(2,1)S(1)}, u32[]{:S(2)}, u32[]{:S(2)}) collective-permute-start(bf16[2,24,4096]{2,1,0:T(8,128)(2,1)} %collective-permute-done.13), channel_id=1, source_target_pairs={{0,2},{1,23},{2,4},{3,1},{4,6},{5,3},{6,8},{7,5},{8,10},{9,7},{10,... | collective-permute-start | bytes 1179656 | tf_op jit(solution)/shard_map/ppermute | solution.py:21
  95.1 0.9 collective-permute-start.15
  101.7 1.4 collective-permute-start.22
  102.4 2.7 %collective-permute-start.16 = (bf16[24,4096]{1,0:T(8,128)(2,1)S(1)}, bf16[24,4096]{1,0:T(8,128)(2,1)S(1)}, u32[]{:S(2)}, u32[]{:S(2)}) collective-permute-start(bf16[24,4096]{1,0:T(8,128)(2,1)S(1)} %get-tuple-element.47), channel_id=1, source_target_pairs={{2,0},{4,2},{6,4},{8,6},{10,8},{12,10},{14,12},{16,14},{18,16},{20... | collective-permute-start | bytes 589832 | tf_op jit(solution)/shard_map/ppermute | solution.py:21
  103.1 8.0 %collective-permute-start.23 = (bf16[24,4096]{1,0:T(8,128)(2,1)S(1)}, bf16[24,4096]{1,0:T(8,128)(2,1)S(1)}, u32[]{:S(2)}, u32[]{:S(2)}) collective-permute-start(bf16[24,4096]{1,0:T(8,128)(2,1)S(1)} %add_convert_fusion.6), channel_id=1, source_target_pairs={{2,0},{23,1},{4,2},{1,3},{6,4},{3,5},{8,6},{5,7},{10,8},{7,9},{12,... | collective-permute-start | bytes 589832 | tf_op jit(solution)/shard_map/ppermute | solution.py:21
  105.1 8.1 %collective-permute-start.17 = (bf16[24,4096]{1,0:T(8,128)(2,1)S(1)}, bf16[24,4096]{1,0:T(8,128)(2,1)S(1)}, u32[]{:S(2)}, u32[]{:S(2)}) collective-permute-start(bf16[24,4096]{1,0:T(8,128)(2,1)S(1)} %add_convert_fusion.11), channel_id=1, source_target_pairs={{2,0},{23,1},{4,2},{1,3},{6,4},{3,5},{8,6},{5,7},{10,8},{7,9},{12,... | collective-permute-start | bytes 589832 | tf_op jit(solution)/shard_map/ppermute | solution.py:21
  111.2 10.0 %collective-permute-start.24 = (bf16[24,4096]{1,0:T(8,128)(2,1)S(1)}, bf16[24,4096]{1,0:T(8,128)(2,1)S(1)}, u32[]{:S(2)}, u32[]{:S(2)}) collective-permute-start(bf16[24,4096]{1,0:T(8,128)(2,1)S(1)} %add_convert_fusion.5), channel_id=1, source_target_pairs={{2,0},{23,1},{4,2},{1,3},{6,4},{3,5},{8,6},{5,7},{10,8},{7,9},{12,... | collective-permute-start | bytes 589832 | tf_op jit(solution)/shard_map/ppermute | solution.py:21
  113.3 10.8 %collective-permute-start.18 = (bf16[24,4096]{1,0:T(8,128)(2,1)S(1)}, bf16[24,4096]{1,0:T(8,128)(2,1)S(1)}, u32[]{:S(2)}, u32[]{:S(2)}) collective-permute-start(bf16[24,4096]{1,0:T(8,128)(2,1)S(1)} %add_convert_fusion.10), channel_id=1, source_target_pairs={{2,0},{23,1},{4,2},{1,3},{6,4},{3,5},{8,6},{5,7},{10,8},{7,9},{12,... | collective-permute-start | bytes 589832 | tf_op jit(solution)/shard_map/ppermute | solution.py:21
  121.2 7.6 %collective-permute-start.25 = (bf16[24,4096]{1,0:T(8,128)(2,1)S(1)}, bf16[24,4096]{1,0:T(8,128)(2,1)S(1)}, u32[]{:S(2)}, u32[]{:S(2)}) collective-permute-start(bf16[24,4096]{1,0:T(8,128)(2,1)S(1)} %add_convert_fusion.4), channel_id=1, source_target_pairs={{2,0},{23,1},{4,2},{1,3},{6,4},{3,5},{8,6},{5,7},{10,8},{7,9},{12,... | collective-permute-start | bytes 589832 | tf_op jit(solution)/shard_map/ppermute | solution.py:21
  124.1 7.6 %collective-permute-start.19 = (bf16[24,4096]{1,0:T(8,128)(2,1)S(1)}, bf16[24,4096]{1,0:T(8,128)(2,1)S(1)}, u32[]{:S(2)}, u32[]{:S(2)}) collective-permute-start(bf16[24,4096]{1,0:T(8,128)(2,1)S(1)} %add_convert_fusion.9), channel_id=1, source_target_pairs={{2,0},{23,1},{4,2},{1,3},{6,4},{3,5},{8,6},{5,7},{10,8},{7,9},{12,... | collective-permute-start | bytes 589832 | tf_op jit(solution)/shard_map/ppermute | solution.py:21
  128.9 7.6 %collective-permute-start.26 = (bf16[24,4096]{1,0:T(8,128)(2,1)S(1)}, bf16[24,4096]{1,0:T(8,128)(2,1)S(1)}, u32[]{:S(2)}, u32[]{:S(2)}) collective-permute-start(bf16[24,4096]{1,0:T(8,128)(2,1)S(1)} %add_convert_fusion.3), channel_id=1, source_target_pairs={{2,0},{23,1},{4,2},{1,3},{6,4},{3,5},{8,6},{5,7},{10,8},{7,9},{12,... | collective-permute-start | bytes 589832 | tf_op jit(solution)/shard_map/ppermute | solution.py:21
  131.8 7.6 %collective-permute-start.20 = (bf16[24,4096]{1,0:T(8,128)(2,1)S(1)}, bf16[24,4096]{1,0:T(8,128)(2,1)S(1)}, u32[]{:S(2)}, u32[]{:S(2)}) collective-permute-start(bf16[24,4096]{1,0:T(8,128)(2,1)S(1)} %add_convert_fusion.8), channel_id=1, source_target_pairs={{2,0},{23,1},{4,2},{1,3},{6,4},{3,5},{8,6},{5,7},{10,8},{7,9},{12,... | collective-permute-start | bytes 589832 | tf_op jit(solution)/shard_map/ppermute | solution.py:21
  136.6 7.6 %collective-permute-start.27 = (bf16[24,4096]{1,0:T(8,128)(2,1)S(1)}, bf16[24,4096]{1,0:T(8,128)(2,1)S(1)}, u32[]{:S(2)}, u32[]{:S(2)}) collective-permute-start(bf16[24,4096]{1,0:T(8,128)(2,1)S(1)} %add_convert_fusion.2), channel_id=1, source_target_pairs={{2,0},{23,1},{4,2},{1,3},{6,4},{3,5},{8,6},{5,7},{10,8},{7,9},{12,... | collective-permute-start | bytes 589832 | tf_op jit(solution)/shard_map/ppermute | solution.py:21
  139.5 40.8 %collective-permute-start.21 = (bf16[24,4096]{1,0:T(8,128)(2,1)S(1)}, bf16[24,4096]{1,0:T(8,128)(2,1)S(1)}, u32[]{:S(2)}, u32[]{:S(2)}) collective-permute-start(bf16[24,4096]{1,0:T(8,128)(2,1)S(1)} %add_convert_fusion.7), channel_id=1, source_target_pairs={{2,0},{23,1},{4,2},{1,3},{6,4},{3,5},{8,6},{5,7},{10,8},{7,9},{12,... | collective-permute-start | bytes 589832 | tf_op jit(solution)/shard_map/ppermute | solution.py:21
  144.3 36.4 %collective-permute-start.28 = (bf16[24,4096]{1,0:T(8,128)(2,1)S(1)}, bf16[24,4096]{1,0:T(8,128)(2,1)S(1)}, u32[]{:S(2)}, u32[]{:S(2)}) collective-permute-start(bf16[24,4096]{1,0:T(8,128)(2,1)S(1)} %add_convert_fusion.1), channel_id=1, source_target_pairs={{0,1},{1,0},{2,3},{3,2},{4,5},{5,4},{6,7},{7,6},{8,9},{9,8},{10,11... | collective-permute-start | bytes 589832 | tf_op jit(solution)/shard_map/ppermute | solution.py:21

commit v2 on v1

--- a/solution.py
+++ b/solution.py
@@ -40,7 +40,8 @@
     other = hop(mine, sibling)
 
     def both(block):
-        return jnp.concatenate([block, hop(block, sibling)], axis=0)
+        theirs = hop(block, sibling)
+        return lax.optimization_barrier(jnp.concatenate([block, theirs], axis=0))
 
     up = both(up_weight_t)
     down = both(down_weight)
@@ -60,22 +61,19 @@
     chain_mine, chain_other = [mine], [other]
     for step in range(1, steps + 1):
         pairs = out if step < steps else out_far
-        if step == steps - 1:
-            up, down, bias, chain_other[-1] = lax.optimization_barrier(
-                (up, down, bias, chain_other[-1])
-            )
         chain_mine.append(hop(chain_mine[-1], pairs))
         chain_other.append(hop(chain_other[-1], pairs))
     chain_mine[steps] = jnp.where(core == 0, chain_mine[steps], mine)
     chain_other[steps] = jnp.where(core == 0, chain_other[steps], other)
 
-    near = terms(chain_mine[1:steps] + chain_other[1:steps])
+    arrivals = [piece for pair in zip(chain_mine[1:steps], chain_other[1:steps]) for piece in pair]
+    near = terms(arrivals)
     far_pieces, near = lax.optimization_barrier(
         ([chain_mine[steps], chain_other[steps]], near)
     )
     far = terms(far_pieces)
-    for_mine = near[: steps - 1] + far[:1]
-    for_other = near[steps - 1 :] + far[1:]
+    for_mine = near[0::2] + far[:1]
+    for_other = near[1::2] + far[1:]
 
     def add(moved, part):
         return (moved.astype(jnp.float32) + part.astype(jnp.float32)).astype(jnp.bfloat16)

time: 183 us -> 163 us (0.89)
  starting transfers between devices: 116 us -> 106 us
  local copies, waits for them, and re-layouts: 10.3 us -> 4.41 us
  matrix products: 13.1 us -> 9.76 us
    ppermute x29, starting transfers between devices: 116 us -> 106 us  [hop(): return lax.ppermute(block, 'tensor', pairs)]
    unnamed x17 -> x27, local copies, waits for them, and re-layouts: 9.18 us -> 4.1 us
    concatenate x2 -> x3, other arithmetic: 3.17 us -> 3.78 us  [both(): return lax.optimization_barrier(jnp.concatenate([block, theirs], axis=0))]
  transfers between devices with their start and end apart: 29 -> 29, of which waited for: 15 -> 18; matrix products, arithmetic and copies ran while one was open for 8% -> 3% of each run, Pallas kernels for 0% -> 0%
where the time goes in v2:
time: 163 us; the launch traced here: 162 us
  starting transfers between devices  106 us (65%)
  waiting for transfers between devices  31.6 us (19%)
  matrix products  9.76 us (6%)
  other arithmetic  8.81 us (5%)
  local copies, waits for them, and re-layouts  4.41 us (3%)
    ppermute x29, starting transfers between devices, hop(): return lax.ppermute(block, 'tensor', pairs)  106 us
    ppermute x29, waiting for transfers between devices, hop(): return lax.ppermute(block, 'tensor', pairs)  31.6 us
    unnamed x27, local copies, waits for them, and re-layouts  4.1 us
    concatenate x3, other arithmetic, both(): return lax.optimization_barrier(jnp.concatenate([block, theirs], axis=0))  3.78 us
    dot_general x2, matrix products, terms(): lax.dot_general(out_grads, down, contract, preferred_element_type=jnp.flo...  3.49 us
    dot_general x2, matrix products, terms(): lax.dot_general(inputs, up, contract, preferred_element_type=jnp.float32)  3.39 us
  transfers between devices with their start and end apart: 29, of which 18 were waited for; matrix products, arithmetic and copies ran while one was open for 3% of the time, Pallas kernels for 0%

profile of v2, /device:TPU:1, one launch (start us, length us, event | category | flops | bytes accessed | tf_op | source)
XLA Modules:
  0.0 162.2 jit_solution(6969450038306528728)
XLA Ops:
  0.0 1.8 %pad_maximum_fusion.2 = bf16[2,24,4096]{2,1,0:T(8,128)(2,1)} fusion(bf16[1,24,4096]{2,1,0:T(8,128)(2,1)} %bitcast.102, bf16[1,24,4096]{2,1,0:T(8,128)(2,1)} %bitcast.104), kind=kLoop, calls=%fused_computation.15 | loop fusion | flops 196608 | bytes 786432 | tf_op jit(solution)/shard_map/stack | solution.py:39
  1.8 12.4 %collective-permute-start.6 = (bf16[2,24,4096]{2,1,0:T(8,128)(2,1)}, bf16[2,24,4096]{2,1,0:T(8,128)(2,1)}, u32[]{:S(2)}, u32[]{:S(2)}) collective-permute-start(bf16[2,24,4096]{2,1,0:T(8,128)(2,1)} %pad_maximum_fusion.2), channel_id=1, source_target_pairs={{0,1},{1,0},{2,3},{3,2},{4,5},{5,4},{6,7},{7,6},{8,9},{9,8},{10,11... | collective-permute-start | bytes 1179656 | tf_op jit(solution)/shard_map/ppermute | solution.py:21
  14.2 5.3 %collective-permute-start = (bf16[2,24,4096]{2,1,0:T(8,128)(2,1)}, bf16[2,24,4096]{2,1,0:T(8,128)(2,1)S(1)}, u32[]{:S(2)}, u32[]{:S(2)}) collective-permute-start(bf16[2,24,4096]{2,1,0:T(8,128)(2,1)} %pad_maximum_fusion.2), channel_id=1, source_target_pairs={{0,2},{1,23},{2,4},{3,1},{4,6},{5,3},{6,8},{7,5},{8,10},{9,7},{10,... | collective-permute-start | bytes 1179656 | tf_op jit(solution)/shard_map/ppermute | solution.py:21
  19.5 1.9 %collective-permute-start.13 = (bf16[344,4096]{1,0:T(8,128)(2,1)}, bf16[344,4096]{1,0:T(8,128)(2,1)S(1)}, u32[]{:S(2)}, u32[]{:S(2)}) collective-permute-start(bf16[344,4096]{1,0:T(8,128)(2,1)} %param.8), channel_id=1, source_target_pairs={{0,1},{1,0},{2,3},{3,2},{4,5},{5,4},{6,7},{7,6},{8,9},{9,8},{10,11... | collective-permute-start | bytes 8454152 | tf_op jit(solution)/shard_map/ppermute | solution.py:21
  21.5 2.4 %collective-permute-start.14 = (bf16[344]{0:T(512)(128)(2,1)}, bf16[344]{0:T(512)(128)(2,1)S(1)}, u32[]{:S(2)}, u32[]{:S(2)}) collective-permute-start(bf16[344]{0:T(512)(128)(2,1)} %param.9), channel_id=1, source_target_pairs={{0,1},{1,0},{2,3},{3,2},{4,5},{5,4},{6,7},{7,6},{8,9},{9,8},{10,11... | collective-permute-start | bytes 2072 | tf_op jit(solution)/shard_map/ppermute | solution.py:21
  23.9 1.9 %collective-permute-start.15 = (bf16[344,4096]{1,0:T(8,128)(2,1)}, bf16[344,4096]{1,0:T(8,128)(2,1)}, u32[]{:S(2)}, u32[]{:S(2)}) collective-permute-start(bf16[344,4096]{1,0:T(8,128)(2,1)} %param.10), channel_id=1, source_target_pairs={{0,1},{1,0},{2,3},{3,2},{4,5},{5,4},{6,7},{7,6},{8,9},{9,8},{10,11... | collective-permute-start | bytes 8454152 | tf_op jit(solution)/shard_map/ppermute | solution.py:21
  25.8 1.0 collective-permute-done.14
  26.8 0.8 pad_maximum_fusion.3
  27.6 2.2 %collective-permute-start.7 = (bf16[2,24,4096]{2,1,0:T(8,128)(2,1)}, bf16[2,24,4096]{2,1,0:T(8,128)(2,1)S(1)}, u32[]{:S(2)}, u32[]{:S(2)}) collective-permute-start(bf16[2,24,4096]{2,1,0:T(8,128)(2,1)} %collective-permute-done.6), channel_id=1, source_target_pairs={{0,2},{1,23},{2,4},{3,1},{4,6},{5,3},{6,8},{7,5},{8,10},{9,7},{10,... | collective-permute-start | bytes 1179656 | tf_op jit(solution)/shard_map/ppermute | solution.py:21
  29.8 3.0 %collective-permute-start.1 = (bf16[2,24,4096]{2,1,0:T(8,128)(2,1)S(1)}, bf16[2,24,4096]{2,1,0:T(8,128)(2,1)S(1)}, u32[]{:S(2)}, u32[]{:S(2)}) collective-permute-start(bf16[2,24,4096]{2,1,0:T(8,128)(2,1)S(1)} %collective-permute-done), channel_id=1, source_target_pairs={{0,2},{1,23},{2,4},{3,1},{4,6},{5,3},{6,8},{7,5},{8,10},{9,7},{10,... | collective-permute-start | bytes 1179656 | tf_op jit(solution)/shard_map/ppermute | solution.py:21
  32.8 3.8 %collective-permute-done.7 = bf16[2,24,4096]{2,1,0:T(8,128)(2,1)S(1)} collective-permute-done((bf16[2,24,4096]{2,1,0:T(8,128)(2,1)}, bf16[2,24,4096]{2,1,0:T(8,128)(2,1)S(1)}, u32[]{:S(2)}, u32[]{:S(2)}) %collective-permute-start.7) | collective-permute-done | bytes 393248 | tf_op jit(solution)/shard_map/ppermute | solution.py:21
  36.6 3.1 %collective-permute-start.8 = (bf16[2,24,4096]{2,1,0:T(8,128)(2,1)S(1)}, bf16[2,24,4096]{2,1,0:T(8,128)(2,1)S(1)}, u32[]{:S(2)}, u32[]{:S(2)}) collective-permute-start(bf16[2,24,4096]{2,1,0:T(8,128)(2,1)S(1)} %collective-permute-done.7), channel_id=1, source_target_pairs={{0,2},{1,23},{2,4},{3,1},{4,6},{5,3},{6,8},{7,5},{8,10},{9,7},{10,... | collective-permute-start | bytes 1179656 | tf_op jit(solution)/shard_map/ppermute | solution.py:21
  39.7 1.1 collective-permute-done.1
  40.8 3.1 %collective-permute-start.2 = (bf16[2,24,4096]{2,1,0:T(8,128)(2,1)S(1)}, bf16[2,24,4096]{2,1,0:T(8,128)(2,1)S(1)}, u32[]{:S(2)}, u32[]{:S(2)}) collective-permute-start(bf16[2,24,4096]{2,1,0:T(8,128)(2,1)S(1)} %collective-permute-done.1), channel_id=1, source_target_pairs={{0,2},{1,23},{2,4},{3,1},{4,6},{5,3},{6,8},{7,5},{8,10},{9,7},{10,... | collective-permute-start | bytes 1179656 | tf_op jit(solution)/shard_map/ppermute | solution.py:21
  44.0 1.4 collective-permute-done.8
  45.4 4.0 %collective-permute-start.9 = (bf16[2,24,4096]{2,1,0:T(8,128)(2,1)S(1)}, bf16[2,24,4096]{2,1,0:T(8,128)(2,1)S(1)}, u32[]{:S(2)}, u32[]{:S(2)}) collective-permute-start(bf16[2,24,4096]{2,1,0:T(8,128)(2,1)S(1)} %collective-permute-done.8), channel_id=1, source_target_pairs={{0,2},{1,23},{2,4},{3,1},{4,6},{5,3},{6,8},{7,5},{8,10},{9,7},{10,... | collective-permute-start | bytes 1179656 | tf_op jit(solution)/shard_map/ppermute | solution.py:21
  49.4 0.2 collective-permute-done.2
  49.6 4.0 %collective-permute-start.3 = (bf16[2,24,4096]{2,1,0:T(8,128)(2,1)S(1)}, bf16[2,24,4096]{2,1,0:T(8,128)(2,1)S(1)}, u32[]{:S(2)}, u32[]{:S(2)}) collective-permute-start(bf16[2,24,4096]{2,1,0:T(8,128)(2,1)S(1)} %collective-permute-done.2), channel_id=1, source_target_pairs={{0,2},{1,23},{2,4},{3,1},{4,6},{5,3},{6,8},{7,5},{8,10},{9,7},{10,... | collective-permute-start | bytes 1179656 | tf_op jit(solution)/shard_map/ppermute | solution.py:21
  53.7 0.4 collective-permute-done.9
  54.1 5.0 %collective-permute-start.10 = (bf16[2,24,4096]{2,1,0:T(8,128)(2,1)S(1)}, bf16[2,24,4096]{2,1,0:T(8,128)(2,1)S(1)}, u32[]{:S(2)}, u32[]{:S(2)}) collective-permute-start(bf16[2,24,4096]{2,1,0:T(8,128)(2,1)S(1)} %collective-permute-done.9), channel_id=1, source_target_pairs={{0,2},{1,23},{2,4},{3,1},{4,6},{5,3},{6,8},{7,5},{8,10},{9,7},{10,... | collective-permute-start | bytes 1179656 | tf_op jit(solution)/shard_map/ppermute | solution.py:21
  59.2 4.2 %collective-permute-start.4 = (bf16[2,24,4096]{2,1,0:T(8,128)(2,1)S(1)}, bf16[2,24,4096]{2,1,0:T(8,128)(2,1)S(1)}, u32[]{:S(2)}, u32[]{:S(2)}) collective-permute-start(bf16[2,24,4096]{2,1,0:T(8,128)(2,1)S(1)} %collective-permute-done.3), channel_id=1, source_target_pairs={{0,2},{1,23},{2,4},{3,1},{4,6},{5,3},{6,8},{7,5},{8,10},{9,7},{10,... | collective-permute-start | bytes 1179656 | tf_op jit(solution)/shard_map/ppermute | solution.py:21
  63.4 0.4 collective-permute-done.10
  63.8 5.0 %collective-permute-start.11 = (bf16[2,24,4096]{2,1,0:T(8,128)(2,1)S(1)}, bf16[2,24,4096]{2,1,0:T(8,128)(2,1)S(1)}, u32[]{:S(2)}, u32[]{:S(2)}) collective-permute-start(bf16[2,24,4096]{2,1,0:T(8,128)(2,1)S(1)} %collective-permute-done.10), channel_id=1, source_target_pairs={{0,2},{1,23},{2,4},{3,1},{4,6},{5,3},{6,8},{7,5},{8,10},{9,7},{10,... | collective-permute-start | bytes 1179656 | tf_op jit(solution)/shard_map/ppermute | solution.py:21
  68.9 0.7 collective-permute-start.5
  69.7 3.9 %collective-permute-done.11 = bf16[2,24,4096]{2,1,0:T(8,128)(2,1)S(1)} collective-permute-done((bf16[2,24,4096]{2,1,0:T(8,128)(2,1)S(1)}, bf16[2,24,4096]{2,1,0:T(8,128)(2,1)S(1)}, u32[]{:S(2)}, u32[]{:S(2)}) %collective-permute-start.11) | collective-permute-done | bytes 393248 | tf_op jit(solution)/shard_map/ppermute | solution.py:21
  73.6 0.7 collective-permute-start.12
  74.4 1.3 copy-done.5
  75.7 0.6 copy-done.7
  76.3 1.8 %broadcast_select_fusion = bf16[2,24,4096]{2,1,0:T(8,128)(2,1)} fusion(bf16[2,24,4096]{2,1,0:T(8,128)(2,1)S(1)} %collective-permute-done.12, bf16[2,24,4096]{2,1,0:T(8,128)(2,1)} %collective-permute-done.6, pred[]{:T(512)S(6)} %eq.9), kind=kLoop, calls=%fused_computation.35 | loop fusion | flops 196608 | bytes 1179649 | tf_op jit(solution)/shard_map/jit(_where)/select_n | solution.py:67
  78.1 0.7 pad_maximum_fusion
  78.8 1.1 copy-done.1
  79.9 2.4 %pad_maximum_fusion.1 = bf16[688,4096]{1,0:T(8,128)(2,1)S(1)} fusion(bf16[344,4096]{1,0:T(8,128)(2,1)} %collective-permute-done.15, bf16[344,4096]{1,0:T(8,128)(2,1)S(1)} %copy-done.1), kind=kLoop, calls=%fused_computation.1 | loop fusion | flops 11272192 | bytes 11272192 | tf_op jit(solution)/shard_map/concatenate | solution.py:44
  82.3 1.7 %convolution_add_fusion = f32[240,688]{0,1:T(8,128)S(1)} fusion(bf16[240,4096]{1,0:T(8,128)(2,1)S(1)} %copy-done.6, bf16[688,4096]{1,0:T(8,128)(2,1)S(1)} %pad_maximum_fusion, f32[688]{0:T(1024)S(1)} %convert_element_type.139), kind=kOutput, calls=%fused_computation.5 | convolution fusion | flops 1352828160 | bytes 8265408 | tf_op jit(solution)/shard_map/dot_general | solution.py:53
  84.0 1.8 %fusion = bf16[240,688]{0,1:T(8,128)(2,1)S(1)} fusion(bf16[240,4096]{1,0:T(8,128)(2,1)S(1)} %copy-done.8, bf16[688,4096]{1,0:T(8,128)(2,1)S(1)} %pad_maximum_fusion.1, f32[240,688]{0,1:T(8,128)S(1)} %convolution_add_fusion), kind=kOutput, calls=%fused_computation.6 | convolution fusion | flops 1354314240 | bytes 8592896 | tf_op jit(solution)/shard_map/dot_general | solution.py:54
  85.8 1.8 %convolution_convert_fusion = bf16[240,4096]{1,0:T(8,128)(2,1)S(1)} fusion(bf16[240,688]{0,1:T(8,128)(2,1)S(1)} %fusion, bf16[688,4096]{1,0:T(8,128)(2,1)S(1)} %pad_maximum_fusion), kind=kOutput, calls=%fused_computation.2 | convolution fusion | flops 1353646080 | bytes 7932416 | tf_op jit(solution)/shard_map/dot_general | solution.py:57
  87.5 0.2 fusion.38
  87.7 0.8 copy-done.3
  88.6 1.7 %convolution_add_fusion.1 = f32[48,688]{1,0:T(8,128)S(1)} fusion(bf16[688,4096]{1,0:T(8,128)(2,1)S(1)} %pad_maximum_fusion, bf16[24,4096]{1,0:T(8,128)(2,1)S(1)} %get-tuple-element.43, bf16[24,4096]{1,0:T(8,128)(2,1)S(1)} %get-tuple-element.66, f32[688]{0:T(1024)S(1)} %convert_element_type.139), kind=kOutput, calls=%fused_computation.8 | convolution fusion | flops 271352064 | bytes 6164160 | tf_op jit(solution)/shard_map/dot_general | solution.py:53
  90.3 1.7 %fusion.1 = bf16[48,688]{1,0:T(8,128)(2,1)S(1)} fusion(bf16[688,4096]{1,0:T(8,128)(2,1)S(1)} %pad_maximum_fusion.1, bf16[24,4096]{1,0:T(8,128)(2,1)S(1)} %get-tuple-element.44, bf16[24,4096]{1,0:T(8,128)(2,1)S(1)} %get-tuple-element.65, f32[48,688]{1,0:T(8,128)S(1)} %convolution_add_fusion.1), kind=kOutput, calls=%fused_computation.9 | convolution fusion | flops 271649280 | bytes 6227456 | tf_op jit(solution)/shard_map/dot_general | solution.py:54
  92.1 1.1 convolution_convert_fusion.1
  93.2 0.7 collective-permute-start.22
  93.9 0.7 collective-permute-start.16
  94.7 1.9 %collective-permute-start.23 = (bf16[24,4096]{1,0:T(8,128)(2,1)S(1)}, bf16[24,4096]{1,0:T(8,128)(2,1)S(1)}, u32[]{:S(2)}, u32[]{:S(2)}) collective-permute-start(bf16[24,4096]{1,0:T(8,128)(2,1)S(1)} %add_convert_fusion.6), channel_id=1, source_target_pairs={{2,0},{23,1},{4,2},{1,3},{6,4},{3,5},{8,6},{5,7},{10,8},{7,9},{12,... | collective-permute-start | bytes 589832 | tf_op jit(solution)/shard_map/ppermute | solution.py:21
  96.7 1.9 %collective-permute-start.17 = (bf16[24,4096]{1,0:T(8,128)(2,1)S(1)}, bf16[24,4096]{1,0:T(8,128)(2,1)S(1)}, u32[]{:S(2)}, u32[]{:S(2)}) collective-permute-start(bf16[24,4096]{1,0:T(8,128)(2,1)S(1)} %add_convert_fusion.11), channel_id=1, source_target_pairs={{2,0},{23,1},{4,2},{1,3},{6,4},{3,5},{8,6},{5,7},{10,8},{7,9},{12,... | collective-permute-start | bytes 589832 | tf_op jit(solution)/shard_map/ppermute | solution.py:21
  98.6 4.2 %collective-permute-done.23 = bf16[24,4096]{1,0:T(8,128)(2,1)S(1)} collective-permute-done((bf16[24,4096]{1,0:T(8,128)(2,1)S(1)}, bf16[24,4096]{1,0:T(8,128)(2,1)S(1)}, u32[]{:S(2)}, u32[]{:S(2)}) %collective-permute-start.23) | collective-permute-done | bytes 196640 | tf_op jit(solution)/shard_map/ppermute | solution.py:21
  102.8 1.9 %collective-permute-start.24 = (bf16[24,4096]{1,0:T(8,128)(2,1)S(1)}, bf16[24,4096]{1,0:T(8,128)(2,1)S(1)}, u32[]{:S(2)}, u32[]{:S(2)}) collective-permute-start(bf16[24,4096]{1,0:T(8,128)(2,1)S(1)} %add_convert_fusion.5), channel_id=1, source_target_pairs={{2,0},{23,1},{4,2},{1,3},{6,4},{3,5},{8,6},{5,7},{10,8},{7,9},{12,... | collective-permute-start | bytes 589832 | tf_op jit(solution)/shard_map/ppermute | solution.py:21
  104.7 0.1 collective-permute-done.17
  104.9 1.9 %collective-permute-start.18 = (bf16[24,4096]{1,0:T(8,128)(2,1)S(1)}, bf16[24,4096]{1,0:T(8,128)(2,1)S(1)}, u32[]{:S(2)}, u32[]{:S(2)}) collective-permute-start(bf16[24,4096]{1,0:T(8,128)(2,1)S(1)} %add_convert_fusion.10), channel_id=1, source_target_pairs={{2,0},{23,1},{4,2},{1,3},{6,4},{3,5},{8,6},{5,7},{10,8},{7,9},{12,... | collective-permute-start | bytes 589832 | tf_op jit(solution)/shard_map/ppermute | solution.py:21
  106.8 3.6 %collective-permute-done.24 = bf16[24,4096]{1,0:T(8,128)(2,1)S(1)} collective-permute-done((bf16[24,4096]{1,0:T(8,128)(2,1)S(1)}, bf16[24,4096]{1,0:T(8,128)(2,1)S(1)}, u32[]{:S(2)}, u32[]{:S(2)}) %collective-permute-start.24) | collective-permute-done | bytes 196640 | tf_op jit(solution)/shard_map/ppermute | solution.py:21
  110.5 1.9 %collective-permute-start.25 = (bf16[24,4096]{1,0:T(8,128)(2,1)S(1)}, bf16[24,4096]{1,0:T(8,128)(2,1)S(1)}, u32[]{:S(2)}, u32[]{:S(2)}) collective-permute-start(bf16[24,4096]{1,0:T(8,128)(2,1)S(1)} %add_convert_fusion.4), channel_id=1, source_target_pairs={{2,0},{23,1},{4,2},{1,3},{6,4},{3,5},{8,6},{5,7},{10,8},{7,9},{12,... | collective-permute-start | bytes 589832 | tf_op jit(solution)/shard_map/ppermute | solution.py:21
  112.4 0.1 collective-permute-done.18
  112.6 1.9 %collective-permute-start.19 = (bf16[24,4096]{1,0:T(8,128)(2,1)S(1)}, bf16[24,4096]{1,0:T(8,128)(2,1)S(1)}, u32[]{:S(2)}, u32[]{:S(2)}) collective-permute-start(bf16[24,4096]{1,0:T(8,128)(2,1)S(1)} %add_convert_fusion.9), channel_id=1, source_target_pairs={{2,0},{23,1},{4,2},{1,3},{6,4},{3,5},{8,6},{5,7},{10,8},{7,9},{12,... | collective-permute-start | bytes 589832 | tf_op jit(solution)/shard_map/ppermute | solution.py:21
  114.5 3.6 %collective-permute-done.25 = bf16[24,4096]{1,0:T(8,128)(2,1)S(1)} collective-permute-done((bf16[24,4096]{1,0:T(8,128)(2,1)S(1)}, bf16[24,4096]{1,0:T(8,128)(2,1)S(1)}, u32[]{:S(2)}, u32[]{:S(2)}) %collective-permute-start.25) | collective-permute-done | bytes 196640 | tf_op jit(solution)/shard_map/ppermute | solution.py:21
  118.2 1.9 %collective-permute-start.26 = (bf16[24,4096]{1,0:T(8,128)(2,1)S(1)}, bf16[24,4096]{1,0:T(8,128)(2,1)S(1)}, u32[]{:S(2)}, u32[]{:S(2)}) collective-permute-start(bf16[24,4096]{1,0:T(8,128)(2,1)S(1)} %add_convert_fusion.3), channel_id=1, source_target_pairs={{2,0},{23,1},{4,2},{1,3},{6,4},{3,5},{8,6},{5,7},{10,8},{7,9},{12,... | collective-permute-start | bytes 589832 | tf_op jit(solution)/shard_map/ppermute | solution.py:21
  120.1 0.1 collective-permute-done.19
  120.3 1.9 %collective-permute-start.20 = (bf16[24,4096]{1,0:T(8,128)(2,1)S(1)}, bf16[24,4096]{1,0:T(8,128)(2,1)S(1)}, u32[]{:S(2)}, u32[]{:S(2)}) collective-permute-start(bf16[24,4096]{1,0:T(8,128)(2,1)S(1)} %add_convert_fusion.8), channel_id=1, source_target_pairs={{2,0},{23,1},{4,2},{1,3},{6,4},{3,5},{8,6},{5,7},{10,8},{7,9},{12,... | collective-permute-start | bytes 589832 | tf_op jit(solution)/shard_map/ppermute | solution.py:21
  122.2 3.6 %collective-permute-done.26 = bf16[24,4096]{1,0:T(8,128)(2,1)S(1)} collective-permute-done((bf16[24,4096]{1,0:T(8,128)(2,1)S(1)}, bf16[24,4096]{1,0:T(8,128)(2,1)S(1)}, u32[]{:S(2)}, u32[]{:S(2)}) %collective-permute-start.26) | collective-permute-done | bytes 196640 | tf_op jit(solution)/shard_map/ppermute | solution.py:21
  125.8 1.9 %collective-permute-start.27 = (bf16[24,4096]{1,0:T(8,128)(2,1)S(1)}, bf16[24,4096]{1,0:T(8,128)(2,1)S(1)}, u32[]{:S(2)}, u32[]{:S(2)}) collective-permute-start(bf16[24,4096]{1,0:T(8,128)(2,1)S(1)} %add_convert_fusion.2), channel_id=1, source_target_pairs={{2,0},{23,1},{4,2},{1,3},{6,4},{3,5},{8,6},{5,7},{10,8},{7,9},{12,... | collective-permute-start | bytes 589832 | tf_op jit(solution)/shard_map/ppermute | solution.py:21
  127.8 0.1 collective-permute-done.20
  127.9 1.9 %collective-permute-start.21 = (bf16[24,4096]{1,0:T(8,128)(2,1)S(1)}, bf16[24,4096]{1,0:T(8,128)(2,1)S(1)}, u32[]{:S(2)}, u32[]{:S(2)}) collective-permute-start(bf16[24,4096]{1,0:T(8,128)(2,1)S(1)} %add_convert_fusion.7), channel_id=1, source_target_pairs={{2,0},{23,1},{4,2},{1,3},{6,4},{3,5},{8,6},{5,7},{10,8},{7,9},{12,... | collective-permute-start | bytes 589832 | tf_op jit(solution)/shard_map/ppermute | solution.py:21
  129.9 3.6 %collective-permute-done.27 = bf16[24,4096]{1,0:T(8,128)(2,1)S(1)} collective-permute-done((bf16[24,4096]{1,0:T(8,128)(2,1)S(1)}, bf16[24,4096]{1,0:T(8,128)(2,1)S(1)}, u32[]{:S(2)}, u32[]{:S(2)}) %collective-permute-start.27) | collective-permute-done | bytes 196640 | tf_op jit(solution)/shard_map/ppermute | solution.py:21
  133.5 26.8 %collective-permute-start.28 = (bf16[24,4096]{1,0:T(8,128)(2,1)S(1)}, bf16[24,4096]{1,0:T(8,128)(2,1)S(1)}, u32[]{:S(2)}, u32[]{:S(2)}) collective-permute-start(bf16[24,4096]{1,0:T(8,128)(2,1)S(1)} %add_convert_fusion.1), channel_id=1, source_target_pairs={{0,1},{1,0},{2,3},{3,2},{4,5},{5,4},{6,7},{7,6},{8,9},{9,8},{10,11... | collective-permute-start | bytes 589832 | tf_op jit(solution)/shard_map/ppermute | solution.py:21
  161.0 0.4 collective-permute-done.28
  161.4 0.8 select_convert_fusion
  (51 shorter events, 1.1 us)
Async XLA Ops:
  1.8 25.8 %collective-permute-start.6 = (bf16[2,24,4096]{2,1,0:T(8,128)(2,1)}, bf16[2,24,4096]{2,1,0:T(8,128)(2,1)}, u32[]{:S(2)}, u32[]{:S(2)}) collective-permute-start(bf16[2,24,4096]{2,1,0:T(8,128)(2,1)} %pad_maximum_fusion.2), channel_id=1, source_target_pairs={{0,1},{1,0},{2,3},{3,2},{4,5},{5,4},{6,7},{7,6},{8,9},{9,8},{10,11... | collective-permute-start | bytes 1179656 | tf_op jit(solution)/shard_map/ppermute | solution.py:21
  14.2 15.6 %collective-permute-start = (bf16[2,24,4096]{2,1,0:T(8,128)(2,1)}, bf16[2,24,4096]{2,1,0:T(8,128)(2,1)S(1)}, u32[]{:S(2)}, u32[]{:S(2)}) collective-permute-start(bf16[2,24,4096]{2,1,0:T(8,128)(2,1)} %pad_maximum_fusion.2), channel_id=1, source_target_pairs={{0,2},{1,23},{2,4},{3,1},{4,6},{5,3},{6,8},{7,5},{8,10},{9,7},{10,... | collective-permute-start | bytes 1179656 | tf_op jit(solution)/shard_map/ppermute | solution.py:21
  19.5 58.6 %collective-permute-start.13 = (bf16[344,4096]{1,0:T(8,128)(2,1)}, bf16[344,4096]{1,0:T(8,128)(2,1)S(1)}, u32[]{:S(2)}, u32[]{:S(2)}) collective-permute-start(bf16[344,4096]{1,0:T(8,128)(2,1)} %param.8), channel_id=1, source_target_pairs={{0,1},{1,0},{2,3},{3,2},{4,5},{5,4},{6,7},{7,6},{8,9},{9,8},{10,11... | collective-permute-start | bytes 8454152 | tf_op jit(solution)/shard_map/ppermute | solution.py:21
  21.5 5.4 %collective-permute-start.14 = (bf16[344]{0:T(512)(128)(2,1)}, bf16[344]{0:T(512)(128)(2,1)S(1)}, u32[]{:S(2)}, u32[]{:S(2)}) collective-permute-start(bf16[344]{0:T(512)(128)(2,1)} %param.9), channel_id=1, source_target_pairs={{0,1},{1,0},{2,3},{3,2},{4,5},{5,4},{6,7},{7,6},{8,9},{9,8},{10,11... | collective-permute-start | bytes 2072 | tf_op jit(solution)/shard_map/ppermute | solution.py:21
  23.9 54.9 %collective-permute-start.15 = (bf16[344,4096]{1,0:T(8,128)(2,1)}, bf16[344,4096]{1,0:T(8,128)(2,1)}, u32[]{:S(2)}, u32[]{:S(2)}) collective-permute-start(bf16[344,4096]{1,0:T(8,128)(2,1)} %param.10), channel_id=1, source_target_pairs={{0,1},{1,0},{2,3},{3,2},{4,5},{5,4},{6,7},{7,6},{8,9},{9,8},{10,11... | collective-permute-start | bytes 8454152 | tf_op jit(solution)/shard_map/ppermute | solution.py:21
  27.6 9.0 %collective-permute-start.7 = (bf16[2,24,4096]{2,1,0:T(8,128)(2,1)}, bf16[2,24,4096]{2,1,0:T(8,128)(2,1)S(1)}, u32[]{:S(2)}, u32[]{:S(2)}) collective-permute-start(bf16[2,24,4096]{2,1,0:T(8,128)(2,1)} %collective-permute-done.6), channel_id=1, source_target_pairs={{0,2},{1,23},{2,4},{3,1},{4,6},{5,3},{6,8},{7,5},{8,10},{9,7},{10,... | collective-permute-start | bytes 1179656 | tf_op jit(solution)/shard_map/ppermute | solution.py:21
  29.8 11.0 %collective-permute-start.1 = (bf16[2,24,4096]{2,1,0:T(8,128)(2,1)S(1)}, bf16[2,24,4096]{2,1,0:T(8,128)(2,1)S(1)}, u32[]{:S(2)}, u32[]{:S(2)}) collective-permute-start(bf16[2,24,4096]{2,1,0:T(8,128)(2,1)S(1)} %collective-permute-done), channel_id=1, source_target_pairs={{0,2},{1,23},{2,4},{3,1},{4,6},{5,3},{6,8},{7,5},{8,10},{9,7},{10,... | collective-permute-start | bytes 1179656 | tf_op jit(solution)/shard_map/ppermute | solution.py:21
  36.6 8.8 %collective-permute-start.8 = (bf16[2,24,4096]{2,1,0:T(8,128)(2,1)S(1)}, bf16[2,24,4096]{2,1,0:T(8,128)(2,1)S(1)}, u32[]{:S(2)}, u32[]{:S(2)}) collective-permute-start(bf16[2,24,4096]{2,1,0:T(8,128)(2,1)S(1)} %collective-permute-done.7), channel_id=1, source_target_pairs={{0,2},{1,23},{2,4},{3,1},{4,6},{5,3},{6,8},{7,5},{8,10},{9,7},{10,... | collective-permute-start | bytes 1179656 | tf_op jit(solution)/shard_map/ppermute | solution.py:21
  40.8 8.8 %collective-permute-start.2 = (bf16[2,24,4096]{2,1,0:T(8,128)(2,1)S(1)}, bf16[2,24,4096]{2,1,0:T(8,128)(2,1)S(1)}, u32[]{:S(2)}, u32[]{:S(2)}) collective-permute-start(bf16[2,24,4096]{2,1,0:T(8,128)(2,1)S(1)} %collective-permute-done.1), channel_id=1, source_target_pairs={{0,2},{1,23},{2,4},{3,1},{4,6},{5,3},{6,8},{7,5},{8,10},{9,7},{10,... | collective-permute-start | bytes 1179656 | tf_op jit(solution)/shard_map/ppermute | solution.py:21
  45.4 8.7 %collective-permute-start.9 = (bf16[2,24,4096]{2,1,0:T(8,128)(2,1)S(1)}, bf16[2,24,4096]{2,1,0:T(8,128)(2,1)S(1)}, u32[]{:S(2)}, u32[]{:S(2)}) collective-permute-start(bf16[2,24,4096]{2,1,0:T(8,128)(2,1)S(1)} %collective-permute-done.8), channel_id=1, source_target_pairs={{0,2},{1,23},{2,4},{3,1},{4,6},{5,3},{6,8},{7,5},{8,10},{9,7},{10,... | collective-permute-start | bytes 1179656 | tf_op jit(solution)/shard_map/ppermute | solution.py:21
  49.6 9.5 %collective-permute-start.3 = (bf16[2,24,4096]{2,1,0:T(8,128)(2,1)S(1)}, bf16[2,24,4096]{2,1,0:T(8,128)(2,1)S(1)}, u32[]{:S(2)}, u32[]{:S(2)}) collective-permute-start(bf16[2,24,4096]{2,1,0:T(8,128)(2,1)S(1)} %collective-permute-done.2), channel_id=1, source_target_pairs={{0,2},{1,23},{2,4},{3,1},{4,6},{5,3},{6,8},{7,5},{8,10},{9,7},{10,... | collective-permute-start | bytes 1179656 | tf_op jit(solution)/shard_map/ppermute | solution.py:21
  53.7 20.6 %copy-start.2 = (bf16[24,4096]{1,0:T(8,128)(2,1)S(1)}, bf16[24,4096]{1,0:T(8,128)(2,1)}, u32[]{:S(2)}) copy-start(bf16[24,4096]{1,0:T(8,128)(2,1)} %param.7) | copy-start | bytes 589828
  53.7 20.6 %copy-start.4 = (bf16[24,4096]{1,0:T(8,128)(2,1)S(1)}, bf16[24,4096]{1,0:T(8,128)(2,1)}, u32[]{:S(2)}) copy-start(bf16[24,4096]{1,0:T(8,128)(2,1)} %param.6) | copy-start | bytes 589828
  54.1 9.7 %collective-permute-start.10 = (bf16[2,24,4096]{2,1,0:T(8,128)(2,1)S(1)}, bf16[2,24,4096]{2,1,0:T(8,128)(2,1)S(1)}, u32[]{:S(2)}, u32[]{:S(2)}) collective-permute-start(bf16[2,24,4096]{2,1,0:T(8,128)(2,1)S(1)} %collective-permute-done.9), channel_id=1, source_target_pairs={{0,2},{1,23},{2,4},{3,1},{4,6},{5,3},{6,8},{7,5},{8,10},{9,7},{10,... | collective-permute-start | bytes 1179656 | tf_op jit(solution)/shard_map/ppermute | solution.py:21
  59.2 9.7 %collective-permute-start.4 = (bf16[2,24,4096]{2,1,0:T(8,128)(2,1)S(1)}, bf16[2,24,4096]{2,1,0:T(8,128)(2,1)S(1)}, u32[]{:S(2)}, u32[]{:S(2)}) collective-permute-start(bf16[2,24,4096]{2,1,0:T(8,128)(2,1)S(1)} %collective-permute-done.3), channel_id=1, source_target_pairs={{0,2},{1,23},{2,4},{3,1},{4,6},{5,3},{6,8},{7,5},{8,10},{9,7},{10,... | collective-permute-start | bytes 1179656 | tf_op jit(solution)/shard_map/ppermute | solution.py:21
  63.8 9.7 %collective-permute-start.11 = (bf16[2,24,4096]{2,1,0:T(8,128)(2,1)S(1)}, bf16[2,24,4096]{2,1,0:T(8,128)(2,1)S(1)}, u32[]{:S(2)}, u32[]{:S(2)}) collective-permute-start(bf16[2,24,4096]{2,1,0:T(8,128)(2,1)S(1)} %collective-permute-done.10), channel_id=1, source_target_pairs={{0,2},{1,23},{2,4},{3,1},{4,6},{5,3},{6,8},{7,5},{8,10},{9,7},{10,... | collective-permute-start | bytes 1179656 | tf_op jit(solution)/shard_map/ppermute | solution.py:21
  68.9 5.4 %collective-permute-start.5 = (bf16[2,24,4096]{2,1,0:T(8,128)(2,1)S(1)}, bf16[2,24,4096]{2,1,0:T(8,128)(2,1)S(1)}, u32[]{:S(2)}, u32[]{:S(2)}) collective-permute-start(bf16[2,24,4096]{2,1,0:T(8,128)(2,1)S(1)} %collective-permute-done.4), channel_id=1, source_target_pairs={{0,2},{2,4},{4,6},{6,8},{8,10},{10,12},{12,14},{14,16},{16,18},{18... | collective-permute-start | bytes 1179656 | tf_op jit(solution)/shard_map/ppermute | solution.py:21
  69.6 8.5 %copy-start = (bf16[344,4096]{1,0:T(8,128)(2,1)S(1)}, bf16[344,4096]{1,0:T(8,128)(2,1)}, u32[]{:S(2)}) copy-start(bf16[344,4096]{1,0:T(8,128)(2,1)} %param.8) | copy-start | bytes 8454148
  73.6 0.8 collective-permute-start.12
  74.4 1.3 copy-start.5
  74.4 1.9 %copy-start.7 = (bf16[240,4096]{1,0:T(8,128)(2,1)}, bf16[240,4096]{1,0:T(8,128)(2,1)S(1)}, u32[]{:S(2)}) copy-start(bf16[240,4096]{1,0:T(8,128)(2,1)S(1)} %get-tuple-element.46) | copy-start | bytes 5898244
  78.1 1.8 %copy-start.1 = (bf16[344,4096]{1,0:T(8,128)(2,1)S(1)}, bf16[344,4096]{1,0:T(8,128)(2,1)}, u32[]{:S(2)}) copy-start(bf16[344,4096]{1,0:T(8,128)(2,1)} %param.10) | copy-start | bytes 8454148
  78.8 3.5 %copy-start.6 = (bf16[240,4096]{1,0:T(8,128)(2,1)S(1)}, bf16[240,4096]{1,0:T(8,128)(2,1)}, u32[]{:S(2)}) copy-start(bf16[240,4096]{1,0:T(8,128)(2,1)} %copy-done.5) | copy-start | bytes 5898244
  82.3 1.7 %copy-start.8 = (bf16[240,4096]{1,0:T(8,128)(2,1)S(1)}, bf16[240,4096]{1,0:T(8,128)(2,1)}, u32[]{:S(2)}) copy-start(bf16[240,4096]{1,0:T(8,128)(2,1)} %copy-done.7) | copy-start | bytes 5898244
  87.5 1.0 copy-start.3
  93.2 1.4 collective-permute-start.22
  93.9 2.7 %collective-permute-start.16 = (bf16[24,4096]{1,0:T(8,128)(2,1)S(1)}, bf16[24,4096]{1,0:T(8,128)(2,1)S(1)}, u32[]{:S(2)}, u32[]{:S(2)}) collective-permute-start(bf16[24,4096]{1,0:T(8,128)(2,1)S(1)} %get-tuple-element.39), channel_id=1, source_target_pairs={{2,0},{4,2},{6,4},{8,6},{10,8},{12,10},{14,12},{16,14},{18,16},{20... | collective-permute-start | bytes 589832 | tf_op jit(solution)/shard_map/ppermute | solution.py:21
  94.7 8.1 %collective-permute-start.23 = (bf16[24,4096]{1,0:T(8,128)(2,1)S(1)}, bf16[24,4096]{1,0:T(8,128)(2,1)S(1)}, u32[]{:S(2)}, u32[]{:S(2)}) collective-permute-start(bf16[24,4096]{1,0:T(8,128)(2,1)S(1)} %add_convert_fusion.6), channel_id=1, source_target_pairs={{2,0},{23,1},{4,2},{1,3},{6,4},{3,5},{8,6},{5,7},{10,8},{7,9},{12,... | collective-permute-start | bytes 589832 | tf_op jit(solution)/shard_map/ppermute | solution.py:21
  96.7 8.2 %collective-permute-start.17 = (bf16[24,4096]{1,0:T(8,128)(2,1)S(1)}, bf16[24,4096]{1,0:T(8,128)(2,1)S(1)}, u32[]{:S(2)}, u32[]{:S(2)}) collective-permute-start(bf16[24,4096]{1,0:T(8,128)(2,1)S(1)} %add_convert_fusion.11), channel_id=1, source_target_pairs={{2,0},{23,1},{4,2},{1,3},{6,4},{3,5},{8,6},{5,7},{10,8},{7,9},{12,... | collective-permute-start | bytes 589832 | tf_op jit(solution)/shard_map/ppermute | solution.py:21
  102.8 7.6 %collective-permute-start.24 = (bf16[24,4096]{1,0:T(8,128)(2,1)S(1)}, bf16[24,4096]{1,0:T(8,128)(2,1)S(1)}, u32[]{:S(2)}, u32[]{:S(2)}) collective-permute-start(bf16[24,4096]{1,0:T(8,128)(2,1)S(1)} %add_convert_fusion.5), channel_id=1, source_target_pairs={{2,0},{23,1},{4,2},{1,3},{6,4},{3,5},{8,6},{5,7},{10,8},{7,9},{12,... | collective-permute-start | bytes 589832 | tf_op jit(solution)/shard_map/ppermute | solution.py:21
  104.9 7.6 %collective-permute-start.18 = (bf16[24,4096]{1,0:T(8,128)(2,1)S(1)}, bf16[24,4096]{1,0:T(8,128)(2,1)S(1)}, u32[]{:S(2)}, u32[]{:S(2)}) collective-permute-start(bf16[24,4096]{1,0:T(8,128)(2,1)S(1)} %add_convert_fusion.10), channel_id=1, source_target_pairs={{2,0},{23,1},{4,2},{1,3},{6,4},{3,5},{8,6},{5,7},{10,8},{7,9},{12,... | collective-permute-start | bytes 589832 | tf_op jit(solution)/shard_map/ppermute | solution.py:21
  110.5 7.6 %collective-permute-start.25 = (bf16[24,4096]{1,0:T(8,128)(2,1)S(1)}, bf16[24,4096]{1,0:T(8,128)(2,1)S(1)}, u32[]{:S(2)}, u32[]{:S(2)}) collective-permute-start(bf16[24,4096]{1,0:T(8,128)(2,1)S(1)} %add_convert_fusion.4), channel_id=1, source_target_pairs={{2,0},{23,1},{4,2},{1,3},{6,4},{3,5},{8,6},{5,7},{10,8},{7,9},{12,... | collective-permute-start | bytes 589832 | tf_op jit(solution)/shard_map/ppermute | solution.py:21
  112.6 7.6 %collective-permute-start.19 = (bf16[24,4096]{1,0:T(8,128)(2,1)S(1)}, bf16[24,4096]{1,0:T(8,128)(2,1)S(1)}, u32[]{:S(2)}, u32[]{:S(2)}) collective-permute-start(bf16[24,4096]{1,0:T(8,128)(2,1)S(1)} %add_convert_fusion.9), channel_id=1, source_target_pairs={{2,0},{23,1},{4,2},{1,3},{6,4},{3,5},{8,6},{5,7},{10,8},{7,9},{12,... | collective-permute-start | bytes 589832 | tf_op jit(solution)/shard_map/ppermute | solution.py:21
  118.2 7.6 %collective-permute-start.26 = (bf16[24,4096]{1,0:T(8,128)(2,1)S(1)}, bf16[24,4096]{1,0:T(8,128)(2,1)S(1)}, u32[]{:S(2)}, u32[]{:S(2)}) collective-permute-start(bf16[24,4096]{1,0:T(8,128)(2,1)S(1)} %add_convert_fusion.3), channel_id=1, source_target_pairs={{2,0},{23,1},{4,2},{1,3},{6,4},{3,5},{8,6},{5,7},{10,8},{7,9},{12,... | collective-permute-start | bytes 589832 | tf_op jit(solution)/shard_map/ppermute | solution.py:21
  120.3 7.6 %collective-permute-start.20 = (bf16[24,4096]{1,0:T(8,128)(2,1)S(1)}, bf16[24,4096]{1,0:T(8,128)(2,1)S(1)}, u32[]{:S(2)}, u32[]{:S(2)}) collective-permute-start(bf16[24,4096]{1,0:T(8,128)(2,1)S(1)} %add_convert_fusion.8), channel_id=1, source_target_pairs={{2,0},{23,1},{4,2},{1,3},{6,4},{3,5},{8,6},{5,7},{10,8},{7,9},{12,... | collective-permute-start | bytes 589832 | tf_op jit(solution)/shard_map/ppermute | solution.py:21
  125.8 7.6 %collective-permute-start.27 = (bf16[24,4096]{1,0:T(8,128)(2,1)S(1)}, bf16[24,4096]{1,0:T(8,128)(2,1)S(1)}, u32[]{:S(2)}, u32[]{:S(2)}) collective-permute-start(bf16[24,4096]{1,0:T(8,128)(2,1)S(1)} %add_convert_fusion.2), channel_id=1, source_target_pairs={{2,0},{23,1},{4,2},{1,3},{6,4},{3,5},{8,6},{5,7},{10,8},{7,9},{12,... | collective-permute-start | bytes 589832 | tf_op jit(solution)/shard_map/ppermute | solution.py:21
  127.9 33.0 %collective-permute-start.21 = (bf16[24,4096]{1,0:T(8,128)(2,1)S(1)}, bf16[24,4096]{1,0:T(8,128)(2,1)S(1)}, u32[]{:S(2)}, u32[]{:S(2)}) collective-permute-start(bf16[24,4096]{1,0:T(8,128)(2,1)S(1)} %add_convert_fusion.7), channel_id=1, source_target_pairs={{2,0},{23,1},{4,2},{1,3},{6,4},{3,5},{8,6},{5,7},{10,8},{7,9},{12,... | collective-permute-start | bytes 589832 | tf_op jit(solution)/shard_map/ppermute | solution.py:21
  133.5 27.8 %collective-permute-start.28 = (bf16[24,4096]{1,0:T(8,128)(2,1)S(1)}, bf16[24,4096]{1,0:T(8,128)(2,1)S(1)}, u32[]{:S(2)}, u32[]{:S(2)}) collective-permute-start(bf16[24,4096]{1,0:T(8,128)(2,1)S(1)} %add_convert_fusion.1), channel_id=1, source_target_pairs={{0,1},{1,0},{2,3},{3,2},{4,5},{5,4},{6,7},{7,6},{8,9},{9,8},{10,11... | collective-permute-start | bytes 589832 | tf_op jit(solution)/shard_map/ppermute | solution.py:21

commit v3 on v2

--- a/solution.py
+++ b/solution.py
@@ -35,9 +35,13 @@
     home = [(target, source) for source, target in out]
     out_far = [(source, target) for source, target in out if source % CORES == 0]
     home_far = [(target, source) for source, target in out_far]
+    out_cross = [(source ^ 1, target) for source, target in out]
+    home_cross = [(target, source) for source, target in out_cross]
+    to_second = [(i, i + 1) for i in range(0, members, CORES)]
+    to_first = [(target, source) for source, target in to_second]
 
     mine = jnp.stack((kept_input, kept_grad), axis=0)
-    other = hop(mine, sibling)
+    other = hop(mine, to_second)
 
     def both(block):
         theirs = hop(block, sibling)
@@ -58,11 +62,12 @@
         partials = partials.astype(jnp.bfloat16)
         return [partials[i * slots : (i + 1) * slots] for i in range(len(pieces))]
 
-    chain_mine, chain_other = [mine], [other]
+    chain_mine, chain_other = [mine], [mine]
     for step in range(1, steps + 1):
         pairs = out if step < steps else out_far
         chain_mine.append(hop(chain_mine[-1], pairs))
-        chain_other.append(hop(chain_other[-1], pairs))
+        crossing = out_cross if step == 1 else pairs
+        chain_other.append(hop(chain_other[-1], crossing))
     chain_mine[steps] = jnp.where(core == 0, chain_mine[steps], mine)
     chain_other[steps] = jnp.where(core == 0, chain_other[steps], other)
 
@@ -81,15 +86,15 @@
     sum_other = hop(for_other[-1], home_far)
     sum_mine = hop(for_mine[-1], home_far)
     for step in range(2, steps + 1):
-        sum_other = hop(add(sum_other, for_other[steps - step]), home)
+        crossing = home_cross if step == steps else home
+        sum_other = hop(add(sum_other, for_other[steps - step]), crossing)
         sum_mine = hop(add(sum_mine, for_mine[steps - step]), home)
-    kept_here = core == 1
-    sum_other = sum_other.astype(jnp.float32) + jnp.where(kept_here, for_other[-1], 0.0)
-    from_sibling = hop(sum_other.astype(jnp.bfloat16), sibling)
+    kept = jnp.where(core == 1, for_mine[-1], 0.0).astype(jnp.float32)
+    joined = hop(for_other[-1], to_first)
     branch = (
         sum_mine.astype(jnp.float32)
-        + jnp.where(kept_here, for_mine[-1], 0.0).astype(jnp.float32)
-        + from_sibling.astype(jnp.float32)
+        + sum_other.astype(jnp.float32)
+        + (kept + joined.astype(jnp.float32))
     ).astype(jnp.bfloat16)
     usable = jnp.arange(slots, dtype=jnp.int32) < kept_count[0]
     summed = kept_grad.astype(jnp.float32) + branch.astype(jnp.float32)

time: 163 us -> 167 us (1.025)
  the two profiles are of different devices: /device:TPU:1 before, /device:TPU:46 now
where the time goes in v3:
time: 167 us; the launch traced here: 166 us
  starting transfers between devices  89.2 us (53%)
  waiting for transfers between devices  54.3 us (33%)
  matrix products  9.75 us (6%)
  other arithmetic  7.76 us (5%)
  local copies, waits for them, and re-layouts  3.52 us (2%)
    ppermute x29, starting transfers between devices, hop(): return lax.ppermute(block, 'tensor', pairs)  89.2 us
    ppermute x29, waiting for transfers between devices, hop(): return lax.ppermute(block, 'tensor', pairs)  54.3 us
    concatenate x3, other arithmetic, both(): return lax.optimization_barrier(jnp.concatenate([block, theirs], axis=0))  3.78 us
    dot_general x2, matrix products, terms(): lax.dot_general(out_grads, down, contract, preferred_element_type=jnp.flo...  3.49 us
    dot_general x2, matrix products, terms(): lax.dot_general(inputs, up, contract, preferred_element_type=jnp.float32)  3.39 us
  transfers between devices with their start and end apart: 29, of which 13 were waited for; matrix products, arithmetic and copies ran while one was open for 2% of the time, Pallas kernels for 0%

profile of v3, /device:TPU:46, one launch (start us, length us, event | category | flops | bytes accessed | tf_op | source)
XLA Modules:
  0.0 165.9 jit_solution(3861080176257658805)
XLA Ops:
  0.0 1.8 %pad_maximum_fusion.2 = bf16[2,24,4096]{2,1,0:T(8,128)(2,1)} fusion(bf16[1,24,4096]{2,1,0:T(8,128)(2,1)} %bitcast.102, bf16[1,24,4096]{2,1,0:T(8,128)(2,1)} %bitcast.104), kind=kLoop, calls=%fused_computation.15 | loop fusion | flops 196608 | bytes 786432 | tf_op jit(solution)/shard_map/stack | solution.py:43
  1.8 4.3 %collective-permute-start = (bf16[2,24,4096]{2,1,0:T(8,128)(2,1)}, bf16[2,24,4096]{2,1,0:T(8,128)(2,1)}, u32[]{:S(2)}, u32[]{:S(2)}) collective-permute-start(bf16[2,24,4096]{2,1,0:T(8,128)(2,1)} %pad_maximum_fusion.2), channel_id=1, source_target_pairs={{0,2},{1,23},{2,4},{3,1},{4,6},{5,3},{6,8},{7,5},{8,10},{9,7},{10,... | collective-permute-start | bytes 1179656 | tf_op jit(solution)/shard_map/ppermute | solution.py:21
  6.1 11.9 %collective-permute-start.6 = (bf16[2,24,4096]{2,1,0:T(8,128)(2,1)}, bf16[2,24,4096]{2,1,0:T(8,128)(2,1)S(1)}, u32[]{:S(2)}, u32[]{:S(2)}) collective-permute-start(bf16[2,24,4096]{2,1,0:T(8,128)(2,1)} %pad_maximum_fusion.2), channel_id=1, source_target_pairs={{1,2},{0,23},{3,4},{2,1},{5,6},{4,3},{7,8},{6,5},{9,10},{8,7},{11,... | collective-permute-start | bytes 1179656 | tf_op jit(solution)/shard_map/ppermute | solution.py:21
  18.0 2.5 %collective-permute-start.12 = (bf16[2,24,4096]{2,1,0:T(8,128)(2,1)}, bf16[2,24,4096]{2,1,0:T(8,128)(2,1)}, u32[]{:S(2)}, u32[]{:S(2)}) collective-permute-start(bf16[2,24,4096]{2,1,0:T(8,128)(2,1)} %pad_maximum_fusion.2), channel_id=1, source_target_pairs={{0,1},{2,3},{4,5},{6,7},{8,9},{10,11},{12,13},{14,15},{16,17},{18,... | collective-permute-start | bytes 1179656 | tf_op jit(solution)/shard_map/ppermute | solution.py:21
  20.5 1.9 %collective-permute-start.13 = (bf16[344,4096]{1,0:T(8,128)(2,1)}, bf16[344,4096]{1,0:T(8,128)(2,1)S(1)}, u32[]{:S(2)}, u32[]{:S(2)}) collective-permute-start(bf16[344,4096]{1,0:T(8,128)(2,1)} %param.8), channel_id=1, source_target_pairs={{0,1},{1,0},{2,3},{3,2},{4,5},{5,4},{6,7},{7,6},{8,9},{9,8},{10,11... | collective-permute-start | bytes 8454152 | tf_op jit(solution)/shard_map/ppermute | solution.py:21
  22.5 2.4 %collective-permute-start.14 = (bf16[344]{0:T(512)(128)(2,1)}, bf16[344]{0:T(512)(128)(2,1)S(1)}, u32[]{:S(2)}, u32[]{:S(2)}) collective-permute-start(bf16[344]{0:T(512)(128)(2,1)} %param.9), channel_id=1, source_target_pairs={{0,1},{1,0},{2,3},{3,2},{4,5},{5,4},{6,7},{7,6},{8,9},{9,8},{10,11... | collective-permute-start | bytes 2072 | tf_op jit(solution)/shard_map/ppermute | solution.py:21
  24.9 2.9 %collective-permute-done.14 = bf16[344]{0:T(512)(128)(2,1)S(1)} collective-permute-done((bf16[344]{0:T(512)(128)(2,1)}, bf16[344]{0:T(512)(128)(2,1)S(1)}, u32[]{:S(2)}, u32[]{:S(2)}) %collective-permute-start.14) | collective-permute-done | bytes 720 | tf_op jit(solution)/shard_map/ppermute | solution.py:21
  27.8 2.0 %collective-permute-start.15 = (bf16[344,4096]{1,0:T(8,128)(2,1)}, bf16[344,4096]{1,0:T(8,128)(2,1)}, u32[]{:S(2)}, u32[]{:S(2)}) collective-permute-start(bf16[344,4096]{1,0:T(8,128)(2,1)} %param.10), channel_id=1, source_target_pairs={{0,1},{1,0},{2,3},{3,2},{4,5},{5,4},{6,7},{7,6},{8,9},{9,8},{10,11... | collective-permute-start | bytes 8454152 | tf_op jit(solution)/shard_map/ppermute | solution.py:21
  29.9 0.8 pad_maximum_fusion.3
  30.6 1.0 fusion.31
  31.7 2.9 %collective-permute-start.1 = (bf16[2,24,4096]{2,1,0:T(8,128)(2,1)}, bf16[2,24,4096]{2,1,0:T(8,128)(2,1)S(1)}, u32[]{:S(2)}, u32[]{:S(2)}) collective-permute-start(bf16[2,24,4096]{2,1,0:T(8,128)(2,1)} %collective-permute-done), channel_id=1, source_target_pairs={{0,2},{1,23},{2,4},{3,1},{4,6},{5,3},{6,8},{7,5},{8,10},{9,7},{10,... | collective-permute-start | bytes 1179656 | tf_op jit(solution)/shard_map/ppermute | solution.py:21
  34.6 0.0 collective-permute-done.6
  34.6 1.9 %collective-permute-start.7 = (bf16[2,24,4096]{2,1,0:T(8,128)(2,1)S(1)}, bf16[2,24,4096]{2,1,0:T(8,128)(2,1)S(1)}, u32[]{:S(2)}, u32[]{:S(2)}) collective-permute-start(bf16[2,24,4096]{2,1,0:T(8,128)(2,1)S(1)} %collective-permute-done.6), channel_id=1, source_target_pairs={{0,2},{1,23},{2,4},{3,1},{4,6},{5,3},{6,8},{7,5},{8,10},{9,7},{10,... | collective-permute-start | bytes 1179656 | tf_op jit(solution)/shard_map/ppermute | solution.py:21
  36.6 6.2 %collective-permute-done.1 = bf16[2,24,4096]{2,1,0:T(8,128)(2,1)S(1)} collective-permute-done((bf16[2,24,4096]{2,1,0:T(8,128)(2,1)}, bf16[2,24,4096]{2,1,0:T(8,128)(2,1)S(1)}, u32[]{:S(2)}, u32[]{:S(2)}) %collective-permute-start.1) | collective-permute-done | bytes 393248 | tf_op jit(solution)/shard_map/ppermute | solution.py:21
  42.8 1.9 %collective-permute-start.2 = (bf16[2,24,4096]{2,1,0:T(8,128)(2,1)S(1)}, bf16[2,24,4096]{2,1,0:T(8,128)(2,1)S(1)}, u32[]{:S(2)}, u32[]{:S(2)}) collective-permute-start(bf16[2,24,4096]{2,1,0:T(8,128)(2,1)S(1)} %collective-permute-done.1), channel_id=1, source_target_pairs={{0,2},{1,23},{2,4},{3,1},{4,6},{5,3},{6,8},{7,5},{8,10},{9,7},{10,... | collective-permute-start | bytes 1179656 | tf_op jit(solution)/shard_map/ppermute | solution.py:21
  44.7 2.3 %collective-permute-done.7 = bf16[2,24,4096]{2,1,0:T(8,128)(2,1)S(1)} collective-permute-done((bf16[2,24,4096]{2,1,0:T(8,128)(2,1)S(1)}, bf16[2,24,4096]{2,1,0:T(8,128)(2,1)S(1)}, u32[]{:S(2)}, u32[]{:S(2)}) %collective-permute-start.7) | collective-permute-done | bytes 393248 | tf_op jit(solution)/shard_map/ppermute | solution.py:21
  47.0 1.9 %collective-permute-start.8 = (bf16[2,24,4096]{2,1,0:T(8,128)(2,1)S(1)}, bf16[2,24,4096]{2,1,0:T(8,128)(2,1)S(1)}, u32[]{:S(2)}, u32[]{:S(2)}) collective-permute-start(bf16[2,24,4096]{2,1,0:T(8,128)(2,1)S(1)} %collective-permute-done.7), channel_id=1, source_target_pairs={{0,2},{1,23},{2,4},{3,1},{4,6},{5,3},{6,8},{7,5},{8,10},{9,7},{10,... | collective-permute-start | bytes 1179656 | tf_op jit(solution)/shard_map/ppermute | solution.py:21
  49.0 4.7 %collective-permute-done.2 = bf16[2,24,4096]{2,1,0:T(8,128)(2,1)S(1)} collective-permute-done((bf16[2,24,4096]{2,1,0:T(8,128)(2,1)S(1)}, bf16[2,24,4096]{2,1,0:T(8,128)(2,1)S(1)}, u32[]{:S(2)}, u32[]{:S(2)}) %collective-permute-start.2) | collective-permute-done | bytes 393248 | tf_op jit(solution)/shard_map/ppermute | solution.py:21
  53.7 1.9 %collective-permute-start.3 = (bf16[2,24,4096]{2,1,0:T(8,128)(2,1)S(1)}, bf16[2,24,4096]{2,1,0:T(8,128)(2,1)S(1)}, u32[]{:S(2)}, u32[]{:S(2)}) collective-permute-start(bf16[2,24,4096]{2,1,0:T(8,128)(2,1)S(1)} %collective-permute-done.2), channel_id=1, source_target_pairs={{0,2},{1,23},{2,4},{3,1},{4,6},{5,3},{6,8},{7,5},{8,10},{9,7},{10,... | collective-permute-start | bytes 1179656 | tf_op jit(solution)/shard_map/ppermute | solution.py:21
  55.6 2.3 %collective-permute-done.8 = bf16[2,24,4096]{2,1,0:T(8,128)(2,1)S(1)} collective-permute-done((bf16[2,24,4096]{2,1,0:T(8,128)(2,1)S(1)}, bf16[2,24,4096]{2,1,0:T(8,128)(2,1)S(1)}, u32[]{:S(2)}, u32[]{:S(2)}) %collective-permute-start.8) | collective-permute-done | bytes 393248 | tf_op jit(solution)/shard_map/ppermute | solution.py:21
  57.9 1.9 %collective-permute-start.9 = (bf16[2,24,4096]{2,1,0:T(8,128)(2,1)S(1)}, bf16[2,24,4096]{2,1,0:T(8,128)(2,1)S(1)}, u32[]{:S(2)}, u32[]{:S(2)}) collective-permute-start(bf16[2,24,4096]{2,1,0:T(8,128)(2,1)S(1)} %collective-permute-done.8), channel_id=1, source_target_pairs={{0,2},{1,23},{2,4},{3,1},{4,6},{5,3},{6,8},{7,5},{8,10},{9,7},{10,... | collective-permute-start | bytes 1179656 | tf_op jit(solution)/shard_map/ppermute | solution.py:21
  59.8 0.0 copy-start.2
  59.8 0.0 copy-start.4
  59.9 4.6 %collective-permute-done.3 = bf16[2,24,4096]{2,1,0:T(8,128)(2,1)S(1)} collective-permute-done((bf16[2,24,4096]{2,1,0:T(8,128)(2,1)S(1)}, bf16[2,24,4096]{2,1,0:T(8,128)(2,1)S(1)}, u32[]{:S(2)}, u32[]{:S(2)}) %collective-permute-start.3) | collective-permute-done | bytes 393248 | tf_op jit(solution)/shard_map/ppermute | solution.py:21
  64.5 1.9 %collective-permute-start.4 = (bf16[2,24,4096]{2,1,0:T(8,128)(2,1)S(1)}, bf16[2,24,4096]{2,1,0:T(8,128)(2,1)S(1)}, u32[]{:S(2)}, u32[]{:S(2)}) collective-permute-start(bf16[2,24,4096]{2,1,0:T(8,128)(2,1)S(1)} %collective-permute-done.3), channel_id=1, source_target_pairs={{0,2},{1,23},{2,4},{3,1},{4,6},{5,3},{6,8},{7,5},{8,10},{9,7},{10,... | collective-permute-start | bytes 1179656 | tf_op jit(solution)/shard_map/ppermute | solution.py:21
  66.4 2.3 %collective-permute-done.9 = bf16[2,24,4096]{2,1,0:T(8,128)(2,1)S(1)} collective-permute-done((bf16[2,24,4096]{2,1,0:T(8,128)(2,1)S(1)}, bf16[2,24,4096]{2,1,0:T(8,128)(2,1)S(1)}, u32[]{:S(2)}, u32[]{:S(2)}) %collective-permute-start.9) | collective-permute-done | bytes 393248 | tf_op jit(solution)/shard_map/ppermute | solution.py:21
  68.7 1.9 %collective-permute-start.10 = (bf16[2,24,4096]{2,1,0:T(8,128)(2,1)S(1)}, bf16[2,24,4096]{2,1,0:T(8,128)(2,1)S(1)}, u32[]{:S(2)}, u32[]{:S(2)}) collective-permute-start(bf16[2,24,4096]{2,1,0:T(8,128)(2,1)S(1)} %collective-permute-done.9), channel_id=1, source_target_pairs={{0,2},{1,23},{2,4},{3,1},{4,6},{5,3},{6,8},{7,5},{8,10},{9,7},{10,... | collective-permute-start | bytes 1179656 | tf_op jit(solution)/shard_map/ppermute | solution.py:21
  70.7 8.9 %collective-permute-done.10 = bf16[2,24,4096]{2,1,0:T(8,128)(2,1)S(1)} collective-permute-done((bf16[2,24,4096]{2,1,0:T(8,128)(2,1)S(1)}, bf16[2,24,4096]{2,1,0:T(8,128)(2,1)S(1)}, u32[]{:S(2)}, u32[]{:S(2)}) %collective-permute-start.10) | collective-permute-done | bytes 393248 | tf_op jit(solution)/shard_map/ppermute | solution.py:21
  79.6 1.9 %collective-permute-start.11 = (bf16[2,24,4096]{2,1,0:T(8,128)(2,1)S(1)}, bf16[2,24,4096]{2,1,0:T(8,128)(2,1)S(1)}, u32[]{:S(2)}, u32[]{:S(2)}) collective-permute-start(bf16[2,24,4096]{2,1,0:T(8,128)(2,1)S(1)} %collective-permute-done.10), channel_id=1, source_target_pairs={{0,2},{2,4},{4,6},{6,8},{8,10},{10,12},{12,14},{14,16},{16,18},{18... | collective-permute-start | bytes 1179656 | tf_op jit(solution)/shard_map/ppermute | solution.py:21
  81.5 1.9 %collective-permute-start.5 = (bf16[2,24,4096]{2,1,0:T(8,128)(2,1)S(1)}, bf16[2,24,4096]{2,1,0:T(8,128)(2,1)S(1)}, u32[]{:S(2)}, u32[]{:S(2)}) collective-permute-start(bf16[2,24,4096]{2,1,0:T(8,128)(2,1)S(1)} %collective-permute-done.4), channel_id=1, source_target_pairs={{0,2},{2,4},{4,6},{6,8},{8,10},{10,12},{12,14},{14,16},{16,18},{18... | collective-permute-start | bytes 1179656 | tf_op jit(solution)/shard_map/ppermute | solution.py:21
  83.5 0.0 copy-start
  83.6 11.1 %collective-permute-done.5 = bf16[2,24,4096]{2,1,0:T(8,128)(2,1)S(1)} collective-permute-done((bf16[2,24,4096]{2,1,0:T(8,128)(2,1)S(1)}, bf16[2,24,4096]{2,1,0:T(8,128)(2,1)S(1)}, u32[]{:S(2)}, u32[]{:S(2)}) %collective-permute-start.5) | collective-permute-done | bytes 393248 | tf_op jit(solution)/shard_map/ppermute | solution.py:21
  94.7 0.1 broadcast_select_fusion.1
  94.8 0.8 broadcast_select_fusion
  95.6 0.7 pad_maximum_fusion
  96.3 1.1 copy-done.1
  97.4 2.4 %pad_maximum_fusion.1 = bf16[688,4096]{1,0:T(8,128)(2,1)S(1)} fusion(bf16[344,4096]{1,0:T(8,128)(2,1)} %collective-permute-done.15, bf16[344,4096]{1,0:T(8,128)(2,1)S(1)} %copy-done.1), kind=kLoop, calls=%fused_computation.1 | loop fusion | flops 11272192 | bytes 11272192 | tf_op jit(solution)/shard_map/concatenate | solution.py:48
  99.8 1.7 convolution_add_fusion
  101.5 1.8 %fusion = bf16[240,688]{0,1:T(8,128)(2,1)S(1)} fusion(bf16[240,4096]{1,0:T(8,128)(2,1)S(1)} %copy-done.8, bf16[688,4096]{1,0:T(8,128)(2,1)S(1)} %pad_maximum_fusion.1, f32[240,688]{0,1:T(8,128)S(1)} %convolution_add_fusion), kind=kOutput, calls=%fused_computation.6 | convolution fusion | flops 1354314240 | bytes 8592896 | tf_op jit(solution)/shard_map/dot_general | solution.py:58
  103.2 1.8 %convolution_convert_fusion = bf16[240,4096]{1,0:T(8,128)(2,1)S(1)} fusion(bf16[240,688]{0,1:T(8,128)(2,1)S(1)} %fusion, bf16[688,4096]{1,0:T(8,128)(2,1)S(1)} %pad_maximum_fusion), kind=kOutput, calls=%fused_computation.2 | convolution fusion | flops 1353646080 | bytes 7932416 | tf_op jit(solution)/shard_map/dot_general | solution.py:61
  105.0 0.2 fusion.38
  105.2 0.8 copy-done.3
  106.0 0.1 slice_bitcast_fusion.22
  106.1 1.7 %convolution_add_fusion.1 = f32[48,688]{1,0:T(8,128)S(1)} fusion(bf16[688,4096]{1,0:T(8,128)(2,1)S(1)} %pad_maximum_fusion, bf16[24,4096]{1,0:T(8,128)(2,1)S(1)} %get-tuple-element.43, bf16[24,4096]{1,0:T(8,128)(2,1)S(1)} %get-tuple-element.66, f32[688]{0:T(1024)S(1)} %convert_element_type.132), kind=kOutput, calls=%fused_computation.8 | convolution fusion | flops 271352064 | bytes 6164160 | tf_op jit(solution)/shard_map/dot_general | solution.py:57
  107.8 1.7 %fusion.1 = bf16[48,688]{1,0:T(8,128)(2,1)S(1)} fusion(bf16[688,4096]{1,0:T(8,128)(2,1)S(1)} %pad_maximum_fusion.1, bf16[24,4096]{1,0:T(8,128)(2,1)S(1)} %get-tuple-element.44, bf16[24,4096]{1,0:T(8,128)(2,1)S(1)} %get-tuple-element.65, f32[48,688]{1,0:T(8,128)S(1)} %convolution_add_fusion.1), kind=kOutput, calls=%fused_computation.9 | convolution fusion | flops 271649280 | bytes 6227456 | tf_op jit(solution)/shard_map/dot_general | solution.py:58
  109.5 1.1 convolution_convert_fusion.1
  110.7 1.9 %collective-permute-start.16 = (bf16[24,4096]{1,0:T(8,128)(2,1)S(1)}, bf16[24,4096]{1,0:T(8,128)(2,1)S(1)}, u32[]{:S(2)}, u32[]{:S(2)}) collective-permute-start(bf16[24,4096]{1,0:T(8,128)(2,1)S(1)} %get-tuple-element.39), channel_id=1, source_target_pairs={{2,0},{4,2},{6,4},{8,6},{10,8},{12,10},{14,12},{16,14},{18,16},{20... | collective-permute-start | bytes 589832 | tf_op jit(solution)/shard_map/ppermute | solution.py:21
  112.6 1.9 %collective-permute-start.22 = (bf16[24,4096]{1,0:T(8,128)(2,1)S(1)}, bf16[24,4096]{1,0:T(8,128)(2,1)S(1)}, u32[]{:S(2)}, u32[]{:S(2)}) collective-permute-start(bf16[24,4096]{1,0:T(8,128)(2,1)S(1)} %get-tuple-element.40), channel_id=1, source_target_pairs={{2,0},{4,2},{6,4},{8,6},{10,8},{12,10},{14,12},{16,14},{18,16},{20... | collective-permute-start | bytes 589832 | tf_op jit(solution)/shard_map/ppermute | solution.py:21
  114.5 1.3 collective-permute-start.28
  115.8 2.4 %collective-permute-done.16 = bf16[24,4096]{1,0:T(8,128)(2,1)S(1)} collective-permute-done((bf16[24,4096]{1,0:T(8,128)(2,1)S(1)}, bf16[24,4096]{1,0:T(8,128)(2,1)S(1)}, u32[]{:S(2)}, u32[]{:S(2)}) %collective-permute-start.16) | collective-permute-done | bytes 196640 | tf_op jit(solution)/shard_map/ppermute | solution.py:21
  118.3 3.1 %collective-permute-start.17 = (bf16[24,4096]{1,0:T(8,128)(2,1)S(1)}, bf16[24,4096]{1,0:T(8,128)(2,1)S(1)}, u32[]{:S(2)}, u32[]{:S(2)}) collective-permute-start(bf16[24,4096]{1,0:T(8,128)(2,1)S(1)} %add_convert_fusion.10), channel_id=1, source_target_pairs={{2,0},{23,1},{4,2},{1,3},{6,4},{3,5},{8,6},{5,7},{10,8},{7,9},{12,... | collective-permute-start | bytes 589832 | tf_op jit(solution)/shard_map/ppermute | solution.py:21
  121.5 3.4 %collective-permute-start.23 = (bf16[24,4096]{1,0:T(8,128)(2,1)S(1)}, bf16[24,4096]{1,0:T(8,128)(2,1)S(1)}, u32[]{:S(2)}, u32[]{:S(2)}) collective-permute-start(bf16[24,4096]{1,0:T(8,128)(2,1)S(1)} %add_convert_fusion.5), channel_id=1, source_target_pairs={{2,0},{23,1},{4,2},{1,3},{6,4},{3,5},{8,6},{5,7},{10,8},{7,9},{12,... | collective-permute-start | bytes 589832 | tf_op jit(solution)/shard_map/ppermute | solution.py:21
  124.9 0.9 collective-permute-done.17
  125.9 4.3 %collective-permute-start.18 = (bf16[24,4096]{1,0:T(8,128)(2,1)S(1)}, bf16[24,4096]{1,0:T(8,128)(2,1)S(1)}, u32[]{:S(2)}, u32[]{:S(2)}) collective-permute-start(bf16[24,4096]{1,0:T(8,128)(2,1)S(1)} %add_convert_fusion.9), channel_id=1, source_target_pairs={{2,0},{23,1},{4,2},{1,3},{6,4},{3,5},{8,6},{5,7},{10,8},{7,9},{12,... | collective-permute-start | bytes 589832 | tf_op jit(solution)/shard_map/ppermute | solution.py:21
  130.3 3.4 %collective-permute-start.24 = (bf16[24,4096]{1,0:T(8,128)(2,1)S(1)}, bf16[24,4096]{1,0:T(8,128)(2,1)S(1)}, u32[]{:S(2)}, u32[]{:S(2)}) collective-permute-start(bf16[24,4096]{1,0:T(8,128)(2,1)S(1)} %add_convert_fusion.4), channel_id=1, source_target_pairs={{2,0},{23,1},{4,2},{1,3},{6,4},{3,5},{8,6},{5,7},{10,8},{7,9},{12,... | collective-permute-start | bytes 589832 | tf_op jit(solution)/shard_map/ppermute | solution.py:21
  133.8 5.3 %collective-permute-start.19 = (bf16[24,4096]{1,0:T(8,128)(2,1)S(1)}, bf16[24,4096]{1,0:T(8,128)(2,1)S(1)}, u32[]{:S(2)}, u32[]{:S(2)}) collective-permute-start(bf16[24,4096]{1,0:T(8,128)(2,1)S(1)} %add_convert_fusion.8), channel_id=1, source_target_pairs={{2,0},{23,1},{4,2},{1,3},{6,4},{3,5},{8,6},{5,7},{10,8},{7,9},{12,... | collective-permute-start | bytes 589832 | tf_op jit(solution)/shard_map/ppermute | solution.py:21
  139.2 3.4 %collective-permute-start.25 = (bf16[24,4096]{1,0:T(8,128)(2,1)S(1)}, bf16[24,4096]{1,0:T(8,128)(2,1)S(1)}, u32[]{:S(2)}, u32[]{:S(2)}) collective-permute-start(bf16[24,4096]{1,0:T(8,128)(2,1)S(1)} %add_convert_fusion.3), channel_id=1, source_target_pairs={{2,0},{23,1},{4,2},{1,3},{6,4},{3,5},{8,6},{5,7},{10,8},{7,9},{12,... | collective-permute-start | bytes 589832 | tf_op jit(solution)/shard_map/ppermute | solution.py:21
  142.7 5.3 %collective-permute-start.20 = (bf16[24,4096]{1,0:T(8,128)(2,1)S(1)}, bf16[24,4096]{1,0:T(8,128)(2,1)S(1)}, u32[]{:S(2)}, u32[]{:S(2)}) collective-permute-start(bf16[24,4096]{1,0:T(8,128)(2,1)S(1)} %add_convert_fusion.7), channel_id=1, source_target_pairs={{2,0},{23,1},{4,2},{1,3},{6,4},{3,5},{8,6},{5,7},{10,8},{7,9},{12,... | collective-permute-start | bytes 589832 | tf_op jit(solution)/shard_map/ppermute | solution.py:21
  148.0 3.4 %collective-permute-start.26 = (bf16[24,4096]{1,0:T(8,128)(2,1)S(1)}, bf16[24,4096]{1,0:T(8,128)(2,1)S(1)}, u32[]{:S(2)}, u32[]{:S(2)}) collective-permute-start(bf16[24,4096]{1,0:T(8,128)(2,1)S(1)} %add_convert_fusion.2), channel_id=1, source_target_pairs={{2,0},{23,1},{4,2},{1,3},{6,4},{3,5},{8,6},{5,7},{10,8},{7,9},{12,... | collective-permute-start | bytes 589832 | tf_op jit(solution)/shard_map/ppermute | solution.py:21
  151.5 5.3 %collective-permute-start.21 = (bf16[24,4096]{1,0:T(8,128)(2,1)S(1)}, bf16[24,4096]{1,0:T(8,128)(2,1)S(1)}, u32[]{:S(2)}, u32[]{:S(2)}) collective-permute-start(bf16[24,4096]{1,0:T(8,128)(2,1)S(1)} %add_convert_fusion.6), channel_id=1, source_target_pairs={{2,0},{23,1},{4,2},{1,3},{6,4},{3,5},{8,6},{5,7},{10,8},{7,9},{12,... | collective-permute-start | bytes 589832 | tf_op jit(solution)/shard_map/ppermute | solution.py:21
  156.8 1.9 %collective-permute-start.27 = (bf16[24,4096]{1,0:T(8,128)(2,1)S(1)}, bf16[24,4096]{1,0:T(8,128)(2,1)S(1)}, u32[]{:S(2)}, u32[]{:S(2)}) collective-permute-start(bf16[24,4096]{1,0:T(8,128)(2,1)S(1)} %add_convert_fusion.1), channel_id=1, source_target_pairs={{2,1},{23,0},{4,3},{1,2},{6,5},{3,4},{8,7},{5,6},{10,9},{7,8},{12,... | collective-permute-start | bytes 589832 | tf_op jit(solution)/shard_map/ppermute | solution.py:21
  159.4 0.5 collective-permute-done.21
  159.9 5.1 %collective-permute-done.27 = bf16[24,4096]{1,0:T(8,128)(2,1)S(1)} collective-permute-done((bf16[24,4096]{1,0:T(8,128)(2,1)S(1)}, bf16[24,4096]{1,0:T(8,128)(2,1)S(1)}, u32[]{:S(2)}, u32[]{:S(2)}) %collective-permute-start.27) | collective-permute-done | bytes 196640 | tf_op jit(solution)/shard_map/ppermute | solution.py:21
  165.0 0.8 select_convert_fusion
  (50 shorter events, 0.9 us)
Async XLA Ops:
  1.8 28.8 %collective-permute-start = (bf16[2,24,4096]{2,1,0:T(8,128)(2,1)}, bf16[2,24,4096]{2,1,0:T(8,128)(2,1)}, u32[]{:S(2)}, u32[]{:S(2)}) collective-permute-start(bf16[2,24,4096]{2,1,0:T(8,128)(2,1)} %pad_maximum_fusion.2), channel_id=1, source_target_pairs={{0,2},{1,23},{2,4},{3,1},{4,6},{5,3},{6,8},{7,5},{8,10},{9,7},{10,... | collective-permute-start | bytes 1179656 | tf_op jit(solution)/shard_map/ppermute | solution.py:21
  6.1 28.5 %collective-permute-start.6 = (bf16[2,24,4096]{2,1,0:T(8,128)(2,1)}, bf16[2,24,4096]{2,1,0:T(8,128)(2,1)S(1)}, u32[]{:S(2)}, u32[]{:S(2)}) collective-permute-start(bf16[2,24,4096]{2,1,0:T(8,128)(2,1)} %pad_maximum_fusion.2), channel_id=1, source_target_pairs={{1,2},{0,23},{3,4},{2,1},{5,6},{4,3},{7,8},{6,5},{9,10},{8,7},{11,... | collective-permute-start | bytes 1179656 | tf_op jit(solution)/shard_map/ppermute | solution.py:21
  18.0 76.7 %collective-permute-start.12 = (bf16[2,24,4096]{2,1,0:T(8,128)(2,1)}, bf16[2,24,4096]{2,1,0:T(8,128)(2,1)}, u32[]{:S(2)}, u32[]{:S(2)}) collective-permute-start(bf16[2,24,4096]{2,1,0:T(8,128)(2,1)} %pad_maximum_fusion.2), channel_id=1, source_target_pairs={{0,1},{2,3},{4,5},{6,7},{8,9},{10,11},{12,13},{14,15},{16,17},{18,... | collective-permute-start | bytes 1179656 | tf_op jit(solution)/shard_map/ppermute | solution.py:21
  20.5 75.0 %collective-permute-start.13 = (bf16[344,4096]{1,0:T(8,128)(2,1)}, bf16[344,4096]{1,0:T(8,128)(2,1)S(1)}, u32[]{:S(2)}, u32[]{:S(2)}) collective-permute-start(bf16[344,4096]{1,0:T(8,128)(2,1)} %param.8), channel_id=1, source_target_pairs={{0,1},{1,0},{2,3},{3,2},{4,5},{5,4},{6,7},{7,6},{8,9},{9,8},{10,11... | collective-permute-start | bytes 8454152 | tf_op jit(solution)/shard_map/ppermute | solution.py:21
  22.5 5.4 %collective-permute-start.14 = (bf16[344]{0:T(512)(128)(2,1)}, bf16[344]{0:T(512)(128)(2,1)S(1)}, u32[]{:S(2)}, u32[]{:S(2)}) collective-permute-start(bf16[344]{0:T(512)(128)(2,1)} %param.9), channel_id=1, source_target_pairs={{0,1},{1,0},{2,3},{3,2},{4,5},{5,4},{6,7},{7,6},{8,9},{9,8},{10,11... | collective-permute-start | bytes 2072 | tf_op jit(solution)/shard_map/ppermute | solution.py:21
  27.8 68.4 %collective-permute-start.15 = (bf16[344,4096]{1,0:T(8,128)(2,1)}, bf16[344,4096]{1,0:T(8,128)(2,1)}, u32[]{:S(2)}, u32[]{:S(2)}) collective-permute-start(bf16[344,4096]{1,0:T(8,128)(2,1)} %param.10), channel_id=1, source_target_pairs={{0,1},{1,0},{2,3},{3,2},{4,5},{5,4},{6,7},{7,6},{8,9},{9,8},{10,11... | collective-permute-start | bytes 8454152 | tf_op jit(solution)/shard_map/ppermute | solution.py:21
  31.7 11.1 %collective-permute-start.1 = (bf16[2,24,4096]{2,1,0:T(8,128)(2,1)}, bf16[2,24,4096]{2,1,0:T(8,128)(2,1)S(1)}, u32[]{:S(2)}, u32[]{:S(2)}) collective-permute-start(bf16[2,24,4096]{2,1,0:T(8,128)(2,1)} %collective-permute-done), channel_id=1, source_target_pairs={{0,2},{1,23},{2,4},{3,1},{4,6},{5,3},{6,8},{7,5},{8,10},{9,7},{10,... | collective-permute-start | bytes 1179656 | tf_op jit(solution)/shard_map/ppermute | solution.py:21
  34.6 12.4 %collective-permute-start.7 = (bf16[2,24,4096]{2,1,0:T(8,128)(2,1)S(1)}, bf16[2,24,4096]{2,1,0:T(8,128)(2,1)S(1)}, u32[]{:S(2)}, u32[]{:S(2)}) collective-permute-start(bf16[2,24,4096]{2,1,0:T(8,128)(2,1)S(1)} %collective-permute-done.6), channel_id=1, source_target_pairs={{0,2},{1,23},{2,4},{3,1},{4,6},{5,3},{6,8},{7,5},{8,10},{9,7},{10,... | collective-permute-start | bytes 1179656 | tf_op jit(solution)/shard_map/ppermute | solution.py:21
  42.8 10.9 %collective-permute-start.2 = (bf16[2,24,4096]{2,1,0:T(8,128)(2,1)S(1)}, bf16[2,24,4096]{2,1,0:T(8,128)(2,1)S(1)}, u32[]{:S(2)}, u32[]{:S(2)}) collective-permute-start(bf16[2,24,4096]{2,1,0:T(8,128)(2,1)S(1)} %collective-permute-done.1), channel_id=1, source_target_pairs={{0,2},{1,23},{2,4},{3,1},{4,6},{5,3},{6,8},{7,5},{8,10},{9,7},{10,... | collective-permute-start | bytes 1179656 | tf_op jit(solution)/shard_map/ppermute | solution.py:21
  47.0 10.9 %collective-permute-start.8 = (bf16[2,24,4096]{2,1,0:T(8,128)(2,1)S(1)}, bf16[2,24,4096]{2,1,0:T(8,128)(2,1)S(1)}, u32[]{:S(2)}, u32[]{:S(2)}) collective-permute-start(bf16[2,24,4096]{2,1,0:T(8,128)(2,1)S(1)} %collective-permute-done.7), channel_id=1, source_target_pairs={{0,2},{1,23},{2,4},{3,1},{4,6},{5,3},{6,8},{7,5},{8,10},{9,7},{10,... | collective-permute-start | bytes 1179656 | tf_op jit(solution)/shard_map/ppermute | solution.py:21
  53.7 10.9 %collective-permute-start.3 = (bf16[2,24,4096]{2,1,0:T(8,128)(2,1)S(1)}, bf16[2,24,4096]{2,1,0:T(8,128)(2,1)S(1)}, u32[]{:S(2)}, u32[]{:S(2)}) collective-permute-start(bf16[2,24,4096]{2,1,0:T(8,128)(2,1)S(1)} %collective-permute-done.2), channel_id=1, source_target_pairs={{0,2},{1,23},{2,4},{3,1},{4,6},{5,3},{6,8},{7,5},{8,10},{9,7},{10,... | collective-permute-start | bytes 1179656 | tf_op jit(solution)/shard_map/ppermute | solution.py:21
  57.9 10.9 %collective-permute-start.9 = (bf16[2,24,4096]{2,1,0:T(8,128)(2,1)S(1)}, bf16[2,24,4096]{2,1,0:T(8,128)(2,1)S(1)}, u32[]{:S(2)}, u32[]{:S(2)}) collective-permute-start(bf16[2,24,4096]{2,1,0:T(8,128)(2,1)S(1)} %collective-permute-done.8), channel_id=1, source_target_pairs={{0,2},{1,23},{2,4},{3,1},{4,6},{5,3},{6,8},{7,5},{8,10},{9,7},{10,... | collective-permute-start | bytes 1179656 | tf_op jit(solution)/shard_map/ppermute | solution.py:21
  59.8 34.9 %copy-start.2 = (bf16[24,4096]{1,0:T(8,128)(2,1)S(1)}, bf16[24,4096]{1,0:T(8,128)(2,1)}, u32[]{:S(2)}) copy-start(bf16[24,4096]{1,0:T(8,128)(2,1)} %param.7) | copy-start | bytes 589828
  59.8 34.9 %copy-start.4 = (bf16[24,4096]{1,0:T(8,128)(2,1)S(1)}, bf16[24,4096]{1,0:T(8,128)(2,1)}, u32[]{:S(2)}) copy-start(bf16[24,4096]{1,0:T(8,128)(2,1)} %param.6) | copy-start | bytes 589828
  64.5 17.0 %collective-permute-start.4 = (bf16[2,24,4096]{2,1,0:T(8,128)(2,1)S(1)}, bf16[2,24,4096]{2,1,0:T(8,128)(2,1)S(1)}, u32[]{:S(2)}, u32[]{:S(2)}) collective-permute-start(bf16[2,24,4096]{2,1,0:T(8,128)(2,1)S(1)} %collective-permute-done.3), channel_id=1, source_target_pairs={{0,2},{1,23},{2,4},{3,1},{4,6},{5,3},{6,8},{7,5},{8,10},{9,7},{10,... | collective-permute-start | bytes 1179656 | tf_op jit(solution)/shard_map/ppermute | solution.py:21
  68.7 10.9 %collective-permute-start.10 = (bf16[2,24,4096]{2,1,0:T(8,128)(2,1)S(1)}, bf16[2,24,4096]{2,1,0:T(8,128)(2,1)S(1)}, u32[]{:S(2)}, u32[]{:S(2)}) collective-permute-start(bf16[2,24,4096]{2,1,0:T(8,128)(2,1)S(1)} %collective-permute-done.9), channel_id=1, source_target_pairs={{0,2},{1,23},{2,4},{3,1},{4,6},{5,3},{6,8},{7,5},{8,10},{9,7},{10,... | collective-permute-start | bytes 1179656 | tf_op jit(solution)/shard_map/ppermute | solution.py:21
  79.6 15.2 %collective-permute-start.11 = (bf16[2,24,4096]{2,1,0:T(8,128)(2,1)S(1)}, bf16[2,24,4096]{2,1,0:T(8,128)(2,1)S(1)}, u32[]{:S(2)}, u32[]{:S(2)}) collective-permute-start(bf16[2,24,4096]{2,1,0:T(8,128)(2,1)S(1)} %collective-permute-done.10), channel_id=1, source_target_pairs={{0,2},{2,4},{4,6},{6,8},{8,10},{10,12},{12,14},{14,16},{16,18},{18... | collective-permute-start | bytes 1179656 | tf_op jit(solution)/shard_map/ppermute | solution.py:21
  81.5 13.2 %collective-permute-start.5 = (bf16[2,24,4096]{2,1,0:T(8,128)(2,1)S(1)}, bf16[2,24,4096]{2,1,0:T(8,128)(2,1)S(1)}, u32[]{:S(2)}, u32[]{:S(2)}) collective-permute-start(bf16[2,24,4096]{2,1,0:T(8,128)(2,1)S(1)} %collective-permute-done.4), channel_id=1, source_target_pairs={{0,2},{2,4},{4,6},{6,8},{8,10},{10,12},{12,14},{14,16},{16,18},{18... | collective-permute-start | bytes 1179656 | tf_op jit(solution)/shard_map/ppermute | solution.py:21
  83.5 12.1 %copy-start = (bf16[344,4096]{1,0:T(8,128)(2,1)S(1)}, bf16[344,4096]{1,0:T(8,128)(2,1)}, u32[]{:S(2)}) copy-start(bf16[344,4096]{1,0:T(8,128)(2,1)} %param.8) | copy-start | bytes 8454148
  83.6 11.2 %copy-start.5 = (bf16[240,4096]{1,0:T(8,128)(2,1)}, bf16[240,4096]{1,0:T(8,128)(2,1)S(1)}, u32[]{:S(2)}) copy-start(bf16[240,4096]{1,0:T(8,128)(2,1)S(1)} %get-tuple-element.45) | copy-start | bytes 5898244
  83.6 12.0 %copy-start.7 = (bf16[240,4096]{1,0:T(8,128)(2,1)}, bf16[240,4096]{1,0:T(8,128)(2,1)S(1)}, u32[]{:S(2)}) copy-start(bf16[240,4096]{1,0:T(8,128)(2,1)S(1)} %get-tuple-element.46) | copy-start | bytes 5898244
  95.6 1.8 %copy-start.1 = (bf16[344,4096]{1,0:T(8,128)(2,1)S(1)}, bf16[344,4096]{1,0:T(8,128)(2,1)}, u32[]{:S(2)}) copy-start(bf16[344,4096]{1,0:T(8,128)(2,1)} %param.10) | copy-start | bytes 8454148
  96.3 3.5 %copy-start.6 = (bf16[240,4096]{1,0:T(8,128)(2,1)S(1)}, bf16[240,4096]{1,0:T(8,128)(2,1)}, u32[]{:S(2)}) copy-start(bf16[240,4096]{1,0:T(8,128)(2,1)} %copy-done.5) | copy-start | bytes 5898244
  99.8 1.7 %copy-start.8 = (bf16[240,4096]{1,0:T(8,128)(2,1)S(1)}, bf16[240,4096]{1,0:T(8,128)(2,1)}, u32[]{:S(2)}) copy-start(bf16[240,4096]{1,0:T(8,128)(2,1)} %copy-done.7) | copy-start | bytes 5898244
  105.0 1.0 copy-start.3
  110.7 7.6 %collective-permute-start.16 = (bf16[24,4096]{1,0:T(8,128)(2,1)S(1)}, bf16[24,4096]{1,0:T(8,128)(2,1)S(1)}, u32[]{:S(2)}, u32[]{:S(2)}) collective-permute-start(bf16[24,4096]{1,0:T(8,128)(2,1)S(1)} %get-tuple-element.39), channel_id=1, source_target_pairs={{2,0},{4,2},{6,4},{8,6},{10,8},{12,10},{14,12},{16,14},{18,16},{20... | collective-permute-start | bytes 589832 | tf_op jit(solution)/shard_map/ppermute | solution.py:21
  112.6 8.8 %collective-permute-start.22 = (bf16[24,4096]{1,0:T(8,128)(2,1)S(1)}, bf16[24,4096]{1,0:T(8,128)(2,1)S(1)}, u32[]{:S(2)}, u32[]{:S(2)}) collective-permute-start(bf16[24,4096]{1,0:T(8,128)(2,1)S(1)} %get-tuple-element.40), channel_id=1, source_target_pairs={{2,0},{4,2},{6,4},{8,6},{10,8},{12,10},{14,12},{16,14},{18,16},{20... | collective-permute-start | bytes 589832 | tf_op jit(solution)/shard_map/ppermute | solution.py:21
  114.5 44.9 %collective-permute-start.28 = (bf16[24,4096]{1,0:T(8,128)(2,1)S(1)}, bf16[24,4096]{1,0:T(8,128)(2,1)S(1)}, u32[]{:S(2)}, u32[]{:S(2)}) collective-permute-start(bf16[24,4096]{1,0:T(8,128)(2,1)S(1)} %get-tuple-element.40), channel_id=1, source_target_pairs={{1,0},{3,2},{5,4},{7,6},{9,8},{11,10},{13,12},{15,14},{17,16},{19,... | collective-permute-start | bytes 589832 | tf_op jit(solution)/shard_map/ppermute | solution.py:21
  118.3 7.6 %collective-permute-start.17 = (bf16[24,4096]{1,0:T(8,128)(2,1)S(1)}, bf16[24,4096]{1,0:T(8,128)(2,1)S(1)}, u32[]{:S(2)}, u32[]{:S(2)}) collective-permute-start(bf16[24,4096]{1,0:T(8,128)(2,1)S(1)} %add_convert_fusion.10), channel_id=1, source_target_pairs={{2,0},{23,1},{4,2},{1,3},{6,4},{3,5},{8,6},{5,7},{10,8},{7,9},{12,... | collective-permute-start | bytes 589832 | tf_op jit(solution)/shard_map/ppermute | solution.py:21
  121.5 8.8 %collective-permute-start.23 = (bf16[24,4096]{1,0:T(8,128)(2,1)S(1)}, bf16[24,4096]{1,0:T(8,128)(2,1)S(1)}, u32[]{:S(2)}, u32[]{:S(2)}) collective-permute-start(bf16[24,4096]{1,0:T(8,128)(2,1)S(1)} %add_convert_fusion.5), channel_id=1, source_target_pairs={{2,0},{23,1},{4,2},{1,3},{6,4},{3,5},{8,6},{5,7},{10,8},{7,9},{12,... | collective-permute-start | bytes 589832 | tf_op jit(solution)/shard_map/ppermute | solution.py:21
  125.9 7.9 %collective-permute-start.18 = (bf16[24,4096]{1,0:T(8,128)(2,1)S(1)}, bf16[24,4096]{1,0:T(8,128)(2,1)S(1)}, u32[]{:S(2)}, u32[]{:S(2)}) collective-permute-start(bf16[24,4096]{1,0:T(8,128)(2,1)S(1)} %add_convert_fusion.9), channel_id=1, source_target_pairs={{2,0},{23,1},{4,2},{1,3},{6,4},{3,5},{8,6},{5,7},{10,8},{7,9},{12,... | collective-permute-start | bytes 589832 | tf_op jit(solution)/shard_map/ppermute | solution.py:21
  130.3 8.8 %collective-permute-start.24 = (bf16[24,4096]{1,0:T(8,128)(2,1)S(1)}, bf16[24,4096]{1,0:T(8,128)(2,1)S(1)}, u32[]{:S(2)}, u32[]{:S(2)}) collective-permute-start(bf16[24,4096]{1,0:T(8,128)(2,1)S(1)} %add_convert_fusion.4), channel_id=1, source_target_pairs={{2,0},{23,1},{4,2},{1,3},{6,4},{3,5},{8,6},{5,7},{10,8},{7,9},{12,... | collective-permute-start | bytes 589832 | tf_op jit(solution)/shard_map/ppermute | solution.py:21
  133.8 8.8 %collective-permute-start.19 = (bf16[24,4096]{1,0:T(8,128)(2,1)S(1)}, bf16[24,4096]{1,0:T(8,128)(2,1)S(1)}, u32[]{:S(2)}, u32[]{:S(2)}) collective-permute-start(bf16[24,4096]{1,0:T(8,128)(2,1)S(1)} %add_convert_fusion.8), channel_id=1, source_target_pairs={{2,0},{23,1},{4,2},{1,3},{6,4},{3,5},{8,6},{5,7},{10,8},{7,9},{12,... | collective-permute-start | bytes 589832 | tf_op jit(solution)/shard_map/ppermute | solution.py:21
  139.2 8.8 %collective-permute-start.25 = (bf16[24,4096]{1,0:T(8,128)(2,1)S(1)}, bf16[24,4096]{1,0:T(8,128)(2,1)S(1)}, u32[]{:S(2)}, u32[]{:S(2)}) collective-permute-start(bf16[24,4096]{1,0:T(8,128)(2,1)S(1)} %add_convert_fusion.3), channel_id=1, source_target_pairs={{2,0},{23,1},{4,2},{1,3},{6,4},{3,5},{8,6},{5,7},{10,8},{7,9},{12,... | collective-permute-start | bytes 589832 | tf_op jit(solution)/shard_map/ppermute | solution.py:21
  142.7 8.8 %collective-permute-start.20 = (bf16[24,4096]{1,0:T(8,128)(2,1)S(1)}, bf16[24,4096]{1,0:T(8,128)(2,1)S(1)}, u32[]{:S(2)}, u32[]{:S(2)}) collective-permute-start(bf16[24,4096]{1,0:T(8,128)(2,1)S(1)} %add_convert_fusion.7), channel_id=1, source_target_pairs={{2,0},{23,1},{4,2},{1,3},{6,4},{3,5},{8,6},{5,7},{10,8},{7,9},{12,... | collective-permute-start | bytes 589832 | tf_op jit(solution)/shard_map/ppermute | solution.py:21
  148.0 8.8 %collective-permute-start.26 = (bf16[24,4096]{1,0:T(8,128)(2,1)S(1)}, bf16[24,4096]{1,0:T(8,128)(2,1)S(1)}, u32[]{:S(2)}, u32[]{:S(2)}) collective-permute-start(bf16[24,4096]{1,0:T(8,128)(2,1)S(1)} %add_convert_fusion.2), channel_id=1, source_target_pairs={{2,0},{23,1},{4,2},{1,3},{6,4},{3,5},{8,6},{5,7},{10,8},{7,9},{12,... | collective-permute-start | bytes 589832 | tf_op jit(solution)/shard_map/ppermute | solution.py:21
  151.5 8.4 %collective-permute-start.21 = (bf16[24,4096]{1,0:T(8,128)(2,1)S(1)}, bf16[24,4096]{1,0:T(8,128)(2,1)S(1)}, u32[]{:S(2)}, u32[]{:S(2)}) collective-permute-start(bf16[24,4096]{1,0:T(8,128)(2,1)S(1)} %add_convert_fusion.6), channel_id=1, source_target_pairs={{2,0},{23,1},{4,2},{1,3},{6,4},{3,5},{8,6},{5,7},{10,8},{7,9},{12,... | collective-permute-start | bytes 589832 | tf_op jit(solution)/shard_map/ppermute | solution.py:21
  156.8 8.2 %collective-permute-start.27 = (bf16[24,4096]{1,0:T(8,128)(2,1)S(1)}, bf16[24,4096]{1,0:T(8,128)(2,1)S(1)}, u32[]{:S(2)}, u32[]{:S(2)}) collective-permute-start(bf16[24,4096]{1,0:T(8,128)(2,1)S(1)} %add_convert_fusion.1), channel_id=1, source_target_pairs={{2,1},{23,0},{4,3},{1,2},{6,5},{3,4},{8,7},{5,6},{10,9},{7,8},{12,... | collective-permute-start | bytes 589832 | tf_op jit(solution)/shard_map/ppermute | solution.py:21

commit v4 on v2

--- a/solution.py
+++ b/solution.py
@@ -5,6 +5,7 @@
 
 
 CORES = 2
+CHAINS = 3
 
 INV_SQRT_TWO = 0.7071067811865476
 INV_SQRT_TWO_PI = 0.3989422804014327
@@ -35,6 +36,9 @@
     home = [(target, source) for source, target in out]
     out_far = [(source, target) for source, target in out if source % CORES == 0]
     home_far = [(target, source) for source, target in out_far]
+    home_cross = [(source, target ^ 1) for source, target in home]
+    to_first = [(i + 1, i) for i in range(0, members, CORES)]
+    part = 2 * slots // CHAINS
 
     mine = jnp.stack((kept_input, kept_grad), axis=0)
     other = hop(mine, sibling)
@@ -56,40 +60,43 @@
         pre_grad = lax.optimization_barrier(pre_grad)
         partials = jnp.dot(pre_grad, up, preferred_element_type=jnp.float32)
         partials = partials.astype(jnp.bfloat16)
-        return [partials[i * slots : (i + 1) * slots] for i in range(len(pieces))]
+        return [partials[i * part : (i + 1) * part] for i in range(len(pieces))]
 
-    chain_mine, chain_other = [mine], [other]
+    middle = jnp.concatenate([mine[:, part:], other[:, : 2 * part - slots]], axis=1)
+    start = [mine[:, :part], middle, other[:, 2 * part - slots :]]
+    chains = [[piece] for piece in start]
     for step in range(1, steps + 1):
         pairs = out if step < steps else out_far
-        chain_mine.append(hop(chain_mine[-1], pairs))
-        chain_other.append(hop(chain_other[-1], pairs))
-    chain_mine[steps] = jnp.where(core == 0, chain_mine[steps], mine)
-    chain_other[steps] = jnp.where(core == 0, chain_other[steps], other)
+        for chain in chains:
+            chain.append(hop(chain[-1], pairs))
+    last = [jnp.where(core == 0, chain[steps], piece) for chain, piece in zip(chains, start)]
 
-    arrivals = [piece for pair in zip(chain_mine[1:steps], chain_other[1:steps]) for piece in pair]
+    arrivals = [chain[step] for step in range(1, steps) for chain in chains]
     near = terms(arrivals)
-    far_pieces, near = lax.optimization_barrier(
-        ([chain_mine[steps], chain_other[steps]], near)
+    last, near = lax.optimization_barrier((last, near))
+    far = terms(last)
+
+    def add(moved, term):
+        return (moved.astype(jnp.float32) + term.astype(jnp.float32)).astype(jnp.bfloat16)
+
+    sums = [hop(term, home_far) for term in far]
+    for step in range(2, steps + 1):
+        group = near[CHAINS * (steps - step) : CHAINS * (steps - step + 1)]
+        totals = [add(moved, term) for moved, term in zip(sums, group)]
+        if step < steps:
+            sums = [hop(total, home) for total in totals]
+    seam = slots - part
+    mine_sum = jnp.concatenate([hop(totals[0], home), hop(totals[1][:seam], home)], axis=0)
+    other_sum = jnp.concatenate(
+        [hop(totals[1][seam:], home_cross), hop(totals[2], home_cross)], axis=0
     )
-    far = terms(far_pieces)
-    for_mine = near[0::2] + far[:1]
-    for_other = near[1::2] + far[1:]
-
-    def add(moved, part):
-        return (moved.astype(jnp.float32) + part.astype(jnp.float32)).astype(jnp.bfloat16)
-
-    sum_other = hop(for_other[-1], home_far)
-    sum_mine = hop(for_mine[-1], home_far)
-    for step in range(2, steps + 1):
-        sum_other = hop(add(sum_other, for_other[steps - step]), home)
-        sum_mine = hop(add(sum_mine, for_mine[steps - step]), home)
-    kept_here = core == 1
-    sum_other = sum_other.astype(jnp.float32) + jnp.where(kept_here, for_other[-1], 0.0)
-    from_sibling = hop(sum_other.astype(jnp.bfloat16), sibling)
+    worked = jnp.concatenate(far, axis=0)
+    kept = jnp.where(core == 1, worked[:slots], 0.0).astype(jnp.float32)
+    joined = hop(worked[slots:], to_first)
     branch = (
-        sum_mine.astype(jnp.float32)
-        + jnp.where(kept_here, for_mine[-1], 0.0).astype(jnp.float32)
-        + from_sibling.astype(jnp.float32)
+        mine_sum.astype(jnp.float32)
+        + other_sum.astype(jnp.float32)
+        + (kept + joined.astype(jnp.float32))
     ).astype(jnp.bfloat16)
     usable = jnp.arange(slots, dtype=jnp.int32) < kept_count[0]
     summed = kept_grad.astype(jnp.float32) + branch.astype(jnp.float32)

time: 163 us -> 173 us (1.061)
  the two profiles are of different devices: /device:TPU:1 before, /device:TPU:46 now
where the time goes in v4:
time: 173 us; the launch traced here: 172 us
  starting transfers between devices  124 us (72%)
  waiting for transfers between devices  21.6 us (12%)
  other arithmetic  11.2 us (6%)
  matrix products  9.91 us (6%)
  local copies, waits for them, and re-layouts  3.61 us (2%)
    ppermute x42, starting transfers between devices, hop(): return lax.ppermute(block, 'tensor', pairs)  124 us
    ppermute x42, waiting for transfers between devices, hop(): return lax.ppermute(block, 'tensor', pairs)  21.6 us
    another operation x3, other arithmetic, traced(): mine = jnp.stack((kept_input, kept_grad), axis=0)  4.39 us
    dot_general x2, matrix products, terms(): lax.dot_general(inputs, up, contract, preferred_element_type=jnp.float32)  3.53 us
    dot_general x2, matrix products, terms(): lax.dot_general(out_grads, down, contract, preferred_element_type=jnp.flo...  3.51 us
  transfers between devices with their start and end apart: 42, of which 15 were waited for; matrix products, arithmetic and copies ran while one was open for 4% of the time, Pallas kernels for 0%

profile of v4, /device:TPU:46, one launch (start us, length us, event | category | flops | bytes accessed | tf_op | source)
XLA Modules:
  0.0 171.9 jit_solution(17624792935337184428)
XLA Ops:
  0.0 1.8 %pad_maximum_fusion.2 = bf16[2,24,4096]{2,1,0:T(8,128)(2,1)} fusion(bf16[1,24,4096]{2,1,0:T(8,128)(2,1)} %bitcast.146, bf16[1,24,4096]{2,1,0:T(8,128)(2,1)} %bitcast.150), kind=kLoop, calls=%fused_computation.17 | loop fusion | flops 196608 | bytes 786432 | tf_op jit(solution)/shard_map/stack | solution.py:43
  1.8 1.9 %collective-permute-start.6 = (bf16[2,24,4096]{2,1,0:T(8,128)(2,1)}, bf16[2,24,4096]{2,1,0:T(8,128)(2,1)S(1)}, u32[]{:S(2)}, u32[]{:S(2)}) collective-permute-start(bf16[2,24,4096]{2,1,0:T(8,128)(2,1)} %pad_maximum_fusion.2), channel_id=1, source_target_pairs={{0,1},{1,0},{2,3},{3,2},{4,5},{5,4},{6,7},{7,6},{8,9},{9,8},{10,11... | collective-permute-start | bytes 1179656 | tf_op jit(solution)/shard_map/ppermute | solution.py:22
  3.7 1.7 fusion.16
  5.4 4.3 %collective-permute-start = (bf16[2,16,4096]{2,1,0:T(8,128)(2,1)}, bf16[2,16,4096]{2,1,0:T(8,128)(2,1)}, u32[]{:S(2)}, u32[]{:S(2)}) collective-permute-start(bf16[2,16,4096]{2,1,0:T(8,128)(2,1)} %fusion.16), channel_id=1, source_target_pairs={{0,2},{1,23},{2,4},{3,1},{4,6},{5,3},{6,8},{7,5},{8,10},{9,7},{10,... | collective-permute-start | bytes 786440 | tf_op jit(solution)/shard_map/ppermute | solution.py:22
  9.7 12.4 %collective-permute-start.19 = (bf16[344,4096]{1,0:T(8,128)(2,1)}, bf16[344,4096]{1,0:T(8,128)(2,1)S(1)}, u32[]{:S(2)}, u32[]{:S(2)}) collective-permute-start(bf16[344,4096]{1,0:T(8,128)(2,1)} %param.8), channel_id=1, source_target_pairs={{0,1},{1,0},{2,3},{3,2},{4,5},{5,4},{6,7},{7,6},{8,9},{9,8},{10,11... | collective-permute-start | bytes 8454152 | tf_op jit(solution)/shard_map/ppermute | solution.py:22
  22.1 1.9 %collective-permute-start.20 = (bf16[344]{0:T(512)(128)(2,1)}, bf16[344]{0:T(512)(128)(2,1)S(1)}, u32[]{:S(2)}, u32[]{:S(2)}) collective-permute-start(bf16[344]{0:T(512)(128)(2,1)} %param.9), channel_id=1, source_target_pairs={{0,1},{1,0},{2,3},{3,2},{4,5},{5,4},{6,7},{7,6},{8,9},{9,8},{10,11... | collective-permute-start | bytes 2072 | tf_op jit(solution)/shard_map/ppermute | solution.py:22
  24.1 2.4 %collective-permute-start.21 = (bf16[344,4096]{1,0:T(8,128)(2,1)}, bf16[344,4096]{1,0:T(8,128)(2,1)}, u32[]{:S(2)}, u32[]{:S(2)}) collective-permute-start(bf16[344,4096]{1,0:T(8,128)(2,1)} %param.10), channel_id=1, source_target_pairs={{0,1},{1,0},{2,3},{3,2},{4,5},{5,4},{6,7},{7,6},{8,9},{9,8},{10,11... | collective-permute-start | bytes 8454152 | tf_op jit(solution)/shard_map/ppermute | solution.py:22
  27.5 1.9 %collective-permute-start.1 = (bf16[2,16,4096]{2,1,0:T(8,128)(2,1)}, bf16[2,16,4096]{2,1,0:T(8,128)(2,1)S(1)}, u32[]{:S(2)}, u32[]{:S(2)}) collective-permute-start(bf16[2,16,4096]{2,1,0:T(8,128)(2,1)} %collective-permute-done), channel_id=1, source_target_pairs={{0,2},{1,23},{2,4},{3,1},{4,6},{5,3},{6,8},{7,5},{8,10},{9,7},{10,... | collective-permute-start | bytes 786440 | tf_op jit(solution)/shard_map/ppermute | solution.py:22
  29.5 1.9 %collective-permute-start.7 = (bf16[2,16,4096]{2,1,0:T(8,128)(2,1)S(1)}, bf16[2,16,4096]{2,1,0:T(8,128)(2,1)S(1)}, u32[]{:S(2)}, u32[]{:S(2)}) collective-permute-start(bf16[2,16,4096]{2,1,0:T(8,128)(2,1)S(1)} %pad_maximum_fusion.3), channel_id=1, source_target_pairs={{0,2},{1,23},{2,4},{3,1},{4,6},{5,3},{6,8},{7,5},{8,10},{9,7},{10,... | collective-permute-start | bytes 786440 | tf_op jit(solution)/shard_map/ppermute | solution.py:22
  31.4 1.9 %collective-permute-start.13 = (bf16[2,16,4096]{2,1,0:T(8,128)(2,1)S(1)}, bf16[2,16,4096]{2,1,0:T(8,128)(2,1)S(1)}, u32[]{:S(2)}, u32[]{:S(2)}) collective-permute-start(bf16[2,16,4096]{2,1,0:T(8,128)(2,1)S(1)} %slice.254), channel_id=1, source_target_pairs={{0,2},{1,23},{2,4},{3,1},{4,6},{5,3},{6,8},{7,5},{8,10},{9,7},{10,... | collective-permute-start | bytes 786440 | tf_op jit(solution)/shard_map/ppermute | solution.py:22
  33.4 1.0 fusion.51
  34.4 2.8 %collective-permute-done.1 = bf16[2,16,4096]{2,1,0:T(8,128)(2,1)S(1)} collective-permute-done((bf16[2,16,4096]{2,1,0:T(8,128)(2,1)}, bf16[2,16,4096]{2,1,0:T(8,128)(2,1)S(1)}, u32[]{:S(2)}, u32[]{:S(2)}) %collective-permute-start.1) | collective-permute-done | bytes 262176 | tf_op jit(solution)/shard_map/ppermute | solution.py:22
  37.2 1.9 %collective-permute-start.2 = (bf16[2,16,4096]{2,1,0:T(8,128)(2,1)S(1)}, bf16[2,16,4096]{2,1,0:T(8,128)(2,1)S(1)}, u32[]{:S(2)}, u32[]{:S(2)}) collective-permute-start(bf16[2,16,4096]{2,1,0:T(8,128)(2,1)S(1)} %collective-permute-done.1), channel_id=1, source_target_pairs={{0,2},{1,23},{2,4},{3,1},{4,6},{5,3},{6,8},{7,5},{8,10},{9,7},{10,... | collective-permute-start | bytes 786440 | tf_op jit(solution)/shard_map/ppermute | solution.py:22
  39.1 0.9 collective-permute-done.7
  40.0 1.9 %collective-permute-start.8 = (bf16[2,16,4096]{2,1,0:T(8,128)(2,1)S(1)}, bf16[2,16,4096]{2,1,0:T(8,128)(2,1)S(1)}, u32[]{:S(2)}, u32[]{:S(2)}) collective-permute-start(bf16[2,16,4096]{2,1,0:T(8,128)(2,1)S(1)} %collective-permute-done.7), channel_id=1, source_target_pairs={{0,2},{1,23},{2,4},{3,1},{4,6},{5,3},{6,8},{7,5},{8,10},{9,7},{10,... | collective-permute-start | bytes 786440 | tf_op jit(solution)/shard_map/ppermute | solution.py:22
  41.9 0.9 collective-permute-done.13
  42.8 2.0 %collective-permute-start.14 = (bf16[2,16,4096]{2,1,0:T(8,128)(2,1)S(1)}, bf16[2,16,4096]{2,1,0:T(8,128)(2,1)S(1)}, u32[]{:S(2)}, u32[]{:S(2)}) collective-permute-start(bf16[2,16,4096]{2,1,0:T(8,128)(2,1)S(1)} %collective-permute-done.13), channel_id=1, source_target_pairs={{0,2},{1,23},{2,4},{3,1},{4,6},{5,3},{6,8},{7,5},{8,10},{9,7},{10,... | collective-permute-start | bytes 786440 | tf_op jit(solution)/shard_map/ppermute | solution.py:22
  44.9 1.7 %collective-permute-done.2 = bf16[2,16,4096]{2,1,0:T(8,128)(2,1)S(1)} collective-permute-done((bf16[2,16,4096]{2,1,0:T(8,128)(2,1)S(1)}, bf16[2,16,4096]{2,1,0:T(8,128)(2,1)S(1)}, u32[]{:S(2)}, u32[]{:S(2)}) %collective-permute-start.2) | collective-permute-done | bytes 262176 | tf_op jit(solution)/shard_map/ppermute | solution.py:22
  46.7 1.9 %collective-permute-start.3 = (bf16[2,16,4096]{2,1,0:T(8,128)(2,1)S(1)}, bf16[2,16,4096]{2,1,0:T(8,128)(2,1)S(1)}, u32[]{:S(2)}, u32[]{:S(2)}) collective-permute-start(bf16[2,16,4096]{2,1,0:T(8,128)(2,1)S(1)} %collective-permute-done.2), channel_id=1, source_target_pairs={{0,2},{1,23},{2,4},{3,1},{4,6},{5,3},{6,8},{7,5},{8,10},{9,7},{10,... | collective-permute-start | bytes 786440 | tf_op jit(solution)/shard_map/ppermute | solution.py:22
  48.6 0.9 collective-permute-done.8
  49.5 2.7 %collective-permute-start.9 = (bf16[2,16,4096]{2,1,0:T(8,128)(2,1)S(1)}, bf16[2,16,4096]{2,1,0:T(8,128)(2,1)S(1)}, u32[]{:S(2)}, u32[]{:S(2)}) collective-permute-start(bf16[2,16,4096]{2,1,0:T(8,128)(2,1)S(1)} %collective-permute-done.8), channel_id=1, source_target_pairs={{0,2},{1,23},{2,4},{3,1},{4,6},{5,3},{6,8},{7,5},{8,10},{9,7},{10,... | collective-permute-start | bytes 786440 | tf_op jit(solution)/shard_map/ppermute | solution.py:22
  52.3 2.8 %collective-permute-start.15 = (bf16[2,16,4096]{2,1,0:T(8,128)(2,1)S(1)}, bf16[2,16,4096]{2,1,0:T(8,128)(2,1)S(1)}, u32[]{:S(2)}, u32[]{:S(2)}) collective-permute-start(bf16[2,16,4096]{2,1,0:T(8,128)(2,1)S(1)} %collective-permute-done.14), channel_id=1, source_target_pairs={{0,2},{1,23},{2,4},{3,1},{4,6},{5,3},{6,8},{7,5},{8,10},{9,7},{10,... | collective-permute-start | bytes 786440 | tf_op jit(solution)/shard_map/ppermute | solution.py:22
  55.2 0.9 collective-permute-done.3
  56.1 2.6 %collective-permute-start.4 = (bf16[2,16,4096]{2,1,0:T(8,128)(2,1)S(1)}, bf16[2,16,4096]{2,1,0:T(8,128)(2,1)S(1)}, u32[]{:S(2)}, u32[]{:S(2)}) collective-permute-start(bf16[2,16,4096]{2,1,0:T(8,128)(2,1)S(1)} %collective-permute-done.3), channel_id=1, source_target_pairs={{0,2},{1,23},{2,4},{3,1},{4,6},{5,3},{6,8},{7,5},{8,10},{9,7},{10,... | collective-permute-start | bytes 786440 | tf_op jit(solution)/shard_map/ppermute | solution.py:22
  58.9 2.8 %collective-permute-start.10 = (bf16[2,16,4096]{2,1,0:T(8,128)(2,1)S(1)}, bf16[2,16,4096]{2,1,0:T(8,128)(2,1)S(1)}, u32[]{:S(2)}, u32[]{:S(2)}) collective-permute-start(bf16[2,16,4096]{2,1,0:T(8,128)(2,1)S(1)} %collective-permute-done.9), channel_id=1, source_target_pairs={{0,2},{1,23},{2,4},{3,1},{4,6},{5,3},{6,8},{7,5},{8,10},{9,7},{10,... | collective-permute-start | bytes 786440 | tf_op jit(solution)/shard_map/ppermute | solution.py:22
  61.8 4.2 %collective-permute-start.16 = (bf16[2,16,4096]{2,1,0:T(8,128)(2,1)S(1)}, bf16[2,16,4096]{2,1,0:T(8,128)(2,1)S(1)}, u32[]{:S(2)}, u32[]{:S(2)}) collective-permute-start(bf16[2,16,4096]{2,1,0:T(8,128)(2,1)S(1)} %collective-permute-done.15), channel_id=1, source_target_pairs={{0,2},{1,23},{2,4},{3,1},{4,6},{5,3},{6,8},{7,5},{8,10},{9,7},{10,... | collective-permute-start | bytes 786440 | tf_op jit(solution)/shard_map/ppermute | solution.py:22
  66.1 2.0 %collective-permute-start.5 = (bf16[2,16,4096]{2,1,0:T(8,128)(2,1)S(1)}, bf16[2,16,4096]{2,1,0:T(8,128)(2,1)S(1)}, u32[]{:S(2)}, u32[]{:S(2)}) collective-permute-start(bf16[2,16,4096]{2,1,0:T(8,128)(2,1)S(1)} %collective-permute-done.4), channel_id=1, source_target_pairs={{0,2},{2,4},{4,6},{6,8},{8,10},{10,12},{12,14},{14,16},{16,18},{18... | collective-permute-start | bytes 786440 | tf_op jit(solution)/shard_map/ppermute | solution.py:22
  68.4 2.7 %collective-permute-start.11 = (bf16[2,16,4096]{2,1,0:T(8,128)(2,1)S(1)}, bf16[2,16,4096]{2,1,0:T(8,128)(2,1)S(1)}, u32[]{:S(2)}, u32[]{:S(2)}) collective-permute-start(bf16[2,16,4096]{2,1,0:T(8,128)(2,1)S(1)} %collective-permute-done.10), channel_id=1, source_target_pairs={{0,2},{1,23},{2,4},{3,1},{4,6},{5,3},{6,8},{7,5},{8,10},{9,7},{10,... | collective-permute-start | bytes 786440 | tf_op jit(solution)/shard_map/ppermute | solution.py:22
  71.2 4.2 %collective-permute-start.17 = (bf16[2,16,4096]{2,1,0:T(8,128)(2,1)S(1)}, bf16[2,16,4096]{2,1,0:T(8,128)(2,1)S(1)}, u32[]{:S(2)}, u32[]{:S(2)}) collective-permute-start(bf16[2,16,4096]{2,1,0:T(8,128)(2,1)S(1)} %collective-permute-done.16), channel_id=1, source_target_pairs={{0,2},{1,23},{2,4},{3,1},{4,6},{5,3},{6,8},{7,5},{8,10},{9,7},{10,... | collective-permute-start | bytes 786440 | tf_op jit(solution)/shard_map/ppermute | solution.py:22
  76.3 2.0 %collective-permute-done.11 = bf16[2,16,4096]{2,1,0:T(8,128)(2,1)S(1)} collective-permute-done((bf16[2,16,4096]{2,1,0:T(8,128)(2,1)S(1)}, bf16[2,16,4096]{2,1,0:T(8,128)(2,1)S(1)}, u32[]{:S(2)}, u32[]{:S(2)}) %collective-permute-start.11) | collective-permute-done | bytes 262176 | tf_op jit(solution)/shard_map/ppermute | solution.py:22
  78.3 1.9 %collective-permute-start.12 = (bf16[2,16,4096]{2,1,0:T(8,128)(2,1)S(1)}, bf16[2,16,4096]{2,1,0:T(8,128)(2,1)S(1)}, u32[]{:S(2)}, u32[]{:S(2)}) collective-permute-start(bf16[2,16,4096]{2,1,0:T(8,128)(2,1)S(1)} %collective-permute-done.11), channel_id=1, source_target_pairs={{0,2},{2,4},{4,6},{6,8},{8,10},{10,12},{12,14},{14,16},{16,18},{18... | collective-permute-start | bytes 786440 | tf_op jit(solution)/shard_map/ppermute | solution.py:22
  80.3 0.9 collective-permute-done.17
  81.2 2.5 %collective-permute-start.18 = (bf16[2,16,4096]{2,1,0:T(8,128)(2,1)S(1)}, bf16[2,16,4096]{2,1,0:T(8,128)(2,1)S(1)}, u32[]{:S(2)}, u32[]{:S(2)}) collective-permute-start(bf16[2,16,4096]{2,1,0:T(8,128)(2,1)S(1)} %collective-permute-done.17), channel_id=1, source_target_pairs={{0,2},{2,4},{4,6},{6,8},{8,10},{10,12},{12,14},{14,16},{16,18},{18... | collective-permute-start | bytes 786440 | tf_op jit(solution)/shard_map/ppermute | solution.py:22
  83.8 4.0 %collective-permute-done.12 = bf16[2,16,4096]{2,1,0:T(8,128)(2,1)S(1)} collective-permute-done((bf16[2,16,4096]{2,1,0:T(8,128)(2,1)S(1)}, bf16[2,16,4096]{2,1,0:T(8,128)(2,1)S(1)}, u32[]{:S(2)}, u32[]{:S(2)}) %collective-permute-start.12) | collective-permute-done | bytes 262176 | tf_op jit(solution)/shard_map/ppermute | solution.py:22
  88.6 2.0 %collective-permute-done.18 = bf16[2,16,4096]{2,1,0:T(8,128)(2,1)S(1)} collective-permute-done((bf16[2,16,4096]{2,1,0:T(8,128)(2,1)S(1)}, bf16[2,16,4096]{2,1,0:T(8,128)(2,1)S(1)}, u32[]{:S(2)}, u32[]{:S(2)}) %collective-permute-start.18) | collective-permute-done | bytes 262176 | tf_op jit(solution)/shard_map/ppermute | solution.py:22
  92.1 1.1 copy-done.3
  93.2 2.4 %pad_maximum_fusion.1 = bf16[688,4096]{1,0:T(8,128)(2,1)S(1)} fusion(bf16[344,4096]{1,0:T(8,128)(2,1)} %collective-permute-done.21, bf16[344,4096]{1,0:T(8,128)(2,1)S(1)} %copy-done.3), kind=kLoop, calls=%fused_computation.1 | loop fusion | flops 11272192 | bytes 11272192 | tf_op jit(solution)/shard_map/concatenate | solution.py:48
  95.6 1.8 %convolution_add_fusion = f32[240,688]{0,1:T(8,128)S(1)} fusion(bf16[240,4096]{1,0:T(8,128)(2,1)S(1)} %copy-done.8, bf16[688,4096]{1,0:T(8,128)(2,1)S(1)} %pad_maximum_fusion, f32[688]{0:T(1024)S(1)} %convert_element_type.177), kind=kOutput, calls=%fused_computation.5 | convolution fusion | flops 1352828160 | bytes 8265408 | tf_op jit(solution)/shard_map/dot_general | solution.py:57
  97.4 1.8 %fusion = bf16[240,688]{0,1:T(8,128)(2,1)S(1)} fusion(bf16[240,4096]{1,0:T(8,128)(2,1)S(1)} %copy-done.10, bf16[688,4096]{1,0:T(8,128)(2,1)S(1)} %pad_maximum_fusion.1, f32[240,688]{0,1:T(8,128)S(1)} %convolution_add_fusion), kind=kOutput, calls=%fused_computation.6 | convolution fusion | flops 1354314240 | bytes 8592896 | tf_op jit(solution)/shard_map/dot_general | solution.py:58
  99.2 1.8 %convolution_convert_fusion = bf16[240,4096]{1,0:T(8,128)(2,1)S(1)} fusion(bf16[240,688]{0,1:T(8,128)(2,1)S(1)} %fusion, bf16[688,4096]{1,0:T(8,128)(2,1)S(1)} %pad_maximum_fusion), kind=kOutput, calls=%fused_computation.2 | convolution fusion | flops 1353646080 | bytes 7932416 | tf_op jit(solution)/shard_map/dot_general | solution.py:61
  102.1 1.7 %convolution_add_fusion.1 = f32[48,688]{1,0:T(8,128)S(1)} fusion(bf16[688,4096]{1,0:T(8,128)(2,1)S(1)} %pad_maximum_fusion, bf16[16,4096]{1,0:T(8,128)(2,1)S(1)} %get-tuple-element.63, bf16[16,4096]{1,0:T(8,128)(2,1)S(1)} %get-tuple-element.98, bf16[16,4096]{1,0:T(8,128)(2,1)S(1)} %get-tuple-element.59, f32[688]{0:T(1024)S(1)} %convert_element_type.177), kind=kOutput, calls=%fused_computation.8 | convolution fusion | flops 271745280 | bytes 6164160 | tf_op jit(solution)/shard_map/dot_general | solution.py:57
  103.9 1.7 %fusion.1 = bf16[48,688]{1,0:T(8,128)(2,1)S(1)} fusion(bf16[688,4096]{1,0:T(8,128)(2,1)S(1)} %pad_maximum_fusion.1, bf16[16,4096]{1,0:T(8,128)(2,1)S(1)} %get-tuple-element.64, bf16[16,4096]{1,0:T(8,128)(2,1)S(1)} %get-tuple-element.97, bf16[16,4096]{1,0:T(8,128)(2,1)S(1)} %get-tuple-element.60, f32[48,688]{1,0:T(8,128)S(1)} %convolution_add_fusion.1), kind=kOutput, calls=%fused_computation.9 | convolution fusion | flops 272042496 | bytes 6227456 | tf_op jit(solution)/shard_map/dot_general | solution.py:58
  105.6 1.1 convolution_convert_fusion.1
  106.8 3.0 %collective-permute-start.35 = (bf16[16,4096]{1,0:T(8,128)(2,1)S(1)}, bf16[16,4096]{1,0:T(8,128)(2,1)S(1)}, u32[]{:S(2)}, u32[]{:S(2)}) collective-permute-start(bf16[16,4096]{1,0:T(8,128)(2,1)S(1)} %get-tuple-element.56), channel_id=1, source_target_pairs={{2,0},{4,2},{6,4},{8,6},{10,8},{12,10},{14,12},{16,14},{18,16},{20... | collective-permute-start | bytes 393224 | tf_op jit(solution)/shard_map/ppermute | solution.py:22
  110.5 1.9 %collective-permute-start.22 = (bf16[16,4096]{1,0:T(8,128)(2,1)S(1)}, bf16[16,4096]{1,0:T(8,128)(2,1)S(1)}, u32[]{:S(2)}, u32[]{:S(2)}) collective-permute-start(bf16[16,4096]{1,0:T(8,128)(2,1)S(1)} %get-tuple-element.58), channel_id=1, source_target_pairs={{2,0},{4,2},{6,4},{8,6},{10,8},{12,10},{14,12},{16,14},{18,16},{20... | collective-permute-start | bytes 393224 | tf_op jit(solution)/shard_map/ppermute | solution.py:22
  112.4 2.6 %collective-permute-start.28 = (bf16[16,4096]{1,0:T(8,128)(2,1)S(1)}, bf16[16,4096]{1,0:T(8,128)(2,1)S(1)}, u32[]{:S(2)}, u32[]{:S(2)}) collective-permute-start(bf16[16,4096]{1,0:T(8,128)(2,1)S(1)} %get-tuple-element.57), channel_id=1, source_target_pairs={{2,0},{4,2},{6,4},{8,6},{10,8},{12,10},{14,12},{16,14},{18,16},{20... | collective-permute-start | bytes 393224 | tf_op jit(solution)/shard_map/ppermute | solution.py:22
  115.1 1.3 collective-permute-start.41
  116.4 5.1 %collective-permute-start.36 = (bf16[16,4096]{1,0:T(8,128)(2,1)S(1)}, bf16[16,4096]{1,0:T(8,128)(2,1)S(1)}, u32[]{:S(2)}, u32[]{:S(2)}) collective-permute-start(bf16[16,4096]{1,0:T(8,128)(2,1)S(1)} %add_convert_fusion.5), channel_id=1, source_target_pairs={{2,0},{23,1},{4,2},{1,3},{6,4},{3,5},{8,6},{5,7},{10,8},{7,9},{12,... | collective-permute-start | bytes 393224 | tf_op jit(solution)/shard_map/ppermute | solution.py:22
  121.6 3.1 %collective-permute-start.23 = (bf16[16,4096]{1,0:T(8,128)(2,1)S(1)}, bf16[16,4096]{1,0:T(8,128)(2,1)S(1)}, u32[]{:S(2)}, u32[]{:S(2)}) collective-permute-start(bf16[16,4096]{1,0:T(8,128)(2,1)S(1)} %add_convert_fusion.15), channel_id=1, source_target_pairs={{2,0},{23,1},{4,2},{1,3},{6,4},{3,5},{8,6},{5,7},{10,8},{7,9},{12,... | collective-permute-start | bytes 393224 | tf_op jit(solution)/shard_map/ppermute | solution.py:22
  124.7 1.9 %collective-permute-start.29 = (bf16[16,4096]{1,0:T(8,128)(2,1)S(1)}, bf16[16,4096]{1,0:T(8,128)(2,1)S(1)}, u32[]{:S(2)}, u32[]{:S(2)}) collective-permute-start(bf16[16,4096]{1,0:T(8,128)(2,1)S(1)} %add_convert_fusion.10), channel_id=1, source_target_pairs={{2,0},{23,1},{4,2},{1,3},{6,4},{3,5},{8,6},{5,7},{10,8},{7,9},{12,... | collective-permute-start | bytes 393224 | tf_op jit(solution)/shard_map/ppermute | solution.py:22
  126.7 3.0 %collective-permute-start.37 = (bf16[16,4096]{1,0:T(8,128)(2,1)S(1)}, bf16[16,4096]{1,0:T(8,128)(2,1)S(1)}, u32[]{:S(2)}, u32[]{:S(2)}) collective-permute-start(bf16[16,4096]{1,0:T(8,128)(2,1)S(1)} %add_convert_fusion.4), channel_id=1, source_target_pairs={{2,0},{23,1},{4,2},{1,3},{6,4},{3,5},{8,6},{5,7},{10,8},{7,9},{12,... | collective-permute-start | bytes 393224 | tf_op jit(solution)/shard_map/ppermute | solution.py:22
  129.7 4.7 %collective-permute-start.24 = (bf16[16,4096]{1,0:T(8,128)(2,1)S(1)}, bf16[16,4096]{1,0:T(8,128)(2,1)S(1)}, u32[]{:S(2)}, u32[]{:S(2)}) collective-permute-start(bf16[16,4096]{1,0:T(8,128)(2,1)S(1)} %add_convert_fusion.14), channel_id=1, source_target_pairs={{2,0},{23,1},{4,2},{1,3},{6,4},{3,5},{8,6},{5,7},{10,8},{7,9},{12,... | collective-permute-start | bytes 393224 | tf_op jit(solution)/shard_map/ppermute | solution.py:22
  134.5 2.1 %collective-permute-start.30 = (bf16[16,4096]{1,0:T(8,128)(2,1)S(1)}, bf16[16,4096]{1,0:T(8,128)(2,1)S(1)}, u32[]{:S(2)}, u32[]{:S(2)}) collective-permute-start(bf16[16,4096]{1,0:T(8,128)(2,1)S(1)} %add_convert_fusion.9), channel_id=1, source_target_pairs={{2,0},{23,1},{4,2},{1,3},{6,4},{3,5},{8,6},{5,7},{10,8},{7,9},{12,... | collective-permute-start | bytes 393224 | tf_op jit(solution)/shard_map/ppermute | solution.py:22
  136.6 1.9 %collective-permute-start.38 = (bf16[16,4096]{1,0:T(8,128)(2,1)S(1)}, bf16[16,4096]{1,0:T(8,128)(2,1)S(1)}, u32[]{:S(2)}, u32[]{:S(2)}) collective-permute-start(bf16[16,4096]{1,0:T(8,128)(2,1)S(1)} %add_convert_fusion.3), channel_id=1, source_target_pairs={{2,0},{23,1},{4,2},{1,3},{6,4},{3,5},{8,6},{5,7},{10,8},{7,9},{12,... | collective-permute-start | bytes 393224 | tf_op jit(solution)/shard_map/ppermute | solution.py:22
  138.6 3.9 %collective-permute-start.25 = (bf16[16,4096]{1,0:T(8,128)(2,1)S(1)}, bf16[16,4096]{1,0:T(8,128)(2,1)S(1)}, u32[]{:S(2)}, u32[]{:S(2)}) collective-permute-start(bf16[16,4096]{1,0:T(8,128)(2,1)S(1)} %add_convert_fusion.13), channel_id=1, source_target_pairs={{2,0},{23,1},{4,2},{1,3},{6,4},{3,5},{8,6},{5,7},{10,8},{7,9},{12,... | collective-permute-start | bytes 393224 | tf_op jit(solution)/shard_map/ppermute | solution.py:22
  142.6 3.6 %collective-permute-start.31 = (bf16[16,4096]{1,0:T(8,128)(2,1)S(1)}, bf16[16,4096]{1,0:T(8,128)(2,1)S(1)}, u32[]{:S(2)}, u32[]{:S(2)}) collective-permute-start(bf16[16,4096]{1,0:T(8,128)(2,1)S(1)} %add_convert_fusion.8), channel_id=1, source_target_pairs={{2,0},{23,1},{4,2},{1,3},{6,4},{3,5},{8,6},{5,7},{10,8},{7,9},{12,... | collective-permute-start | bytes 393224 | tf_op jit(solution)/shard_map/ppermute | solution.py:22
  146.2 3.0 %collective-permute-start.39 = (bf16[16,4096]{1,0:T(8,128)(2,1)S(1)}, bf16[16,4096]{1,0:T(8,128)(2,1)S(1)}, u32[]{:S(2)}, u32[]{:S(2)}) collective-permute-start(bf16[16,4096]{1,0:T(8,128)(2,1)S(1)} %add_convert_fusion.2), channel_id=1, source_target_pairs={{2,0},{23,1},{4,2},{1,3},{6,4},{3,5},{8,6},{5,7},{10,8},{7,9},{12,... | collective-permute-start | bytes 393224 | tf_op jit(solution)/shard_map/ppermute | solution.py:22
  149.3 1.9 %collective-permute-start.26 = (bf16[16,4096]{1,0:T(8,128)(2,1)S(1)}, bf16[16,4096]{1,0:T(8,128)(2,1)S(1)}, u32[]{:S(2)}, u32[]{:S(2)}) collective-permute-start(bf16[16,4096]{1,0:T(8,128)(2,1)S(1)} %add_convert_fusion.12), channel_id=1, source_target_pairs={{2,0},{23,1},{4,2},{1,3},{6,4},{3,5},{8,6},{5,7},{10,8},{7,9},{12,... | collective-permute-start | bytes 393224 | tf_op jit(solution)/shard_map/ppermute | solution.py:22
  151.3 3.0 %collective-permute-start.32 = (bf16[16,4096]{1,0:T(8,128)(2,1)S(1)}, bf16[16,4096]{1,0:T(8,128)(2,1)S(1)}, u32[]{:S(2)}, u32[]{:S(2)}) collective-permute-start(bf16[16,4096]{1,0:T(8,128)(2,1)S(1)} %add_convert_fusion.7), channel_id=1, source_target_pairs={{2,0},{23,1},{4,2},{1,3},{6,4},{3,5},{8,6},{5,7},{10,8},{7,9},{12,... | collective-permute-start | bytes 393224 | tf_op jit(solution)/shard_map/ppermute | solution.py:22
  154.3 2.2 %collective-permute-start.40 = (bf16[16,4096]{1,0:T(8,128)(2,1)S(1)}, bf16[16,4096]{1,0:T(8,128)(2,1)S(1)}, u32[]{:S(2)}, u32[]{:S(2)}) collective-permute-start(bf16[16,4096]{1,0:T(8,128)(2,1)S(1)} %add_convert_fusion.1), channel_id=1, source_target_pairs={{2,1},{23,0},{4,3},{1,2},{6,5},{3,4},{8,7},{5,6},{10,9},{7,8},{12,... | collective-permute-start | bytes 393224 | tf_op jit(solution)/shard_map/ppermute | solution.py:22
  156.6 4.5 %collective-permute-start.27 = (bf16[16,4096]{1,0:T(8,128)(2,1)S(1)}, bf16[16,4096]{1,0:T(8,128)(2,1)S(1)}, u32[]{:S(2)}, u32[]{:S(2)}) collective-permute-start(bf16[16,4096]{1,0:T(8,128)(2,1)S(1)} %add_convert_fusion.11), channel_id=1, source_target_pairs={{2,0},{23,1},{4,2},{1,3},{6,4},{3,5},{8,6},{5,7},{10,8},{7,9},{12,... | collective-permute-start | bytes 393224 | tf_op jit(solution)/shard_map/ppermute | solution.py:22
  161.2 3.1 %collective-permute-start.33 = (bf16[8,4096]{1,0:T(8,128)(2,1)S(1)}, bf16[8,4096]{1,0:T(8,128)(2,1)S(1)}, u32[]{:S(2)}, u32[]{:S(2)}) collective-permute-start(bf16[8,4096]{1,0:T(8,128)(2,1)S(1)} %get-tuple-element.96), channel_id=1, source_target_pairs={{2,0},{23,1},{4,2},{1,3},{6,4},{3,5},{8,6},{5,7},{10,8},{7,9},{12,... | collective-permute-start | bytes 196616 | tf_op jit(solution)/shard_map/ppermute | solution.py:22
  164.3 3.2 %collective-permute-start.34 = (bf16[8,4096]{1,0:T(8,128)(2,1)S(1)}, bf16[8,4096]{1,0:T(8,128)(2,1)S(1)}, u32[]{:S(2)}, u32[]{:S(2)}) collective-permute-start(bf16[8,4096]{1,0:T(8,128)(2,1)S(1)} %get-tuple-element.95), channel_id=1, source_target_pairs={{2,1},{23,0},{4,3},{1,2},{6,5},{3,4},{8,7},{5,6},{10,9},{7,8},{12,... | collective-permute-start | bytes 196616 | tf_op jit(solution)/shard_map/ppermute | solution.py:22
  167.6 3.5 %collective-permute-done.34 = bf16[8,4096]{1,0:T(8,128)(2,1)S(1)} collective-permute-done((bf16[8,4096]{1,0:T(8,128)(2,1)S(1)}, bf16[8,4096]{1,0:T(8,128)(2,1)S(1)}, u32[]{:S(2)}, u32[]{:S(2)}) %collective-permute-start.34) | collective-permute-done | bytes 65568 | tf_op jit(solution)/shard_map/ppermute | solution.py:22
  (101 shorter events, 7.8 us)
Async XLA Ops:
  0.0 27.4 %copy-start.11 = (bf16[344]{0:T(512)(128)(2,1)S(1)}, bf16[344]{0:T(512)(128)(2,1)}, u32[]{:S(2)}) copy-start(bf16[344]{0:T(512)(128)(2,1)} %param.9) | copy-start | bytes 2068
  1.8 27.6 %collective-permute-start.6 = (bf16[2,24,4096]{2,1,0:T(8,128)(2,1)}, bf16[2,24,4096]{2,1,0:T(8,128)(2,1)S(1)}, u32[]{:S(2)}, u32[]{:S(2)}) collective-permute-start(bf16[2,24,4096]{2,1,0:T(8,128)(2,1)} %pad_maximum_fusion.2), channel_id=1, source_target_pairs={{0,1},{1,0},{2,3},{3,2},{4,5},{5,4},{6,7},{7,6},{8,9},{9,8},{10,11... | collective-permute-start | bytes 1179656 | tf_op jit(solution)/shard_map/ppermute | solution.py:22
  5.4 22.1 %collective-permute-start = (bf16[2,16,4096]{2,1,0:T(8,128)(2,1)}, bf16[2,16,4096]{2,1,0:T(8,128)(2,1)}, u32[]{:S(2)}, u32[]{:S(2)}) collective-permute-start(bf16[2,16,4096]{2,1,0:T(8,128)(2,1)} %fusion.16), channel_id=1, source_target_pairs={{0,2},{1,23},{2,4},{3,1},{4,6},{5,3},{6,8},{7,5},{8,10},{9,7},{10,... | collective-permute-start | bytes 786440 | tf_op jit(solution)/shard_map/ppermute | solution.py:22
  9.7 81.7 %collective-permute-start.19 = (bf16[344,4096]{1,0:T(8,128)(2,1)}, bf16[344,4096]{1,0:T(8,128)(2,1)S(1)}, u32[]{:S(2)}, u32[]{:S(2)}) collective-permute-start(bf16[344,4096]{1,0:T(8,128)(2,1)} %param.8), channel_id=1, source_target_pairs={{0,1},{1,0},{2,3},{3,2},{4,5},{5,4},{6,7},{7,6},{8,9},{9,8},{10,11... | collective-permute-start | bytes 8454152 | tf_op jit(solution)/shard_map/ppermute | solution.py:22
  22.1 5.3 %collective-permute-start.20 = (bf16[344]{0:T(512)(128)(2,1)}, bf16[344]{0:T(512)(128)(2,1)S(1)}, u32[]{:S(2)}, u32[]{:S(2)}) collective-permute-start(bf16[344]{0:T(512)(128)(2,1)} %param.9), channel_id=1, source_target_pairs={{0,1},{1,0},{2,3},{3,2},{4,5},{5,4},{6,7},{7,6},{8,9},{9,8},{10,11... | collective-permute-start | bytes 2072 | tf_op jit(solution)/shard_map/ppermute | solution.py:22
  24.1 68.0 %collective-permute-start.21 = (bf16[344,4096]{1,0:T(8,128)(2,1)}, bf16[344,4096]{1,0:T(8,128)(2,1)}, u32[]{:S(2)}, u32[]{:S(2)}) collective-permute-start(bf16[344,4096]{1,0:T(8,128)(2,1)} %param.10), channel_id=1, source_target_pairs={{0,1},{1,0},{2,3},{3,2},{4,5},{5,4},{6,7},{7,6},{8,9},{9,8},{10,11... | collective-permute-start | bytes 8454152 | tf_op jit(solution)/shard_map/ppermute | solution.py:22
  27.5 9.7 %collective-permute-start.1 = (bf16[2,16,4096]{2,1,0:T(8,128)(2,1)}, bf16[2,16,4096]{2,1,0:T(8,128)(2,1)S(1)}, u32[]{:S(2)}, u32[]{:S(2)}) collective-permute-start(bf16[2,16,4096]{2,1,0:T(8,128)(2,1)} %collective-permute-done), channel_id=1, source_target_pairs={{0,2},{1,23},{2,4},{3,1},{4,6},{5,3},{6,8},{7,5},{8,10},{9,7},{10,... | collective-permute-start | bytes 786440 | tf_op jit(solution)/shard_map/ppermute | solution.py:22
  29.5 10.5 %collective-permute-start.7 = (bf16[2,16,4096]{2,1,0:T(8,128)(2,1)S(1)}, bf16[2,16,4096]{2,1,0:T(8,128)(2,1)S(1)}, u32[]{:S(2)}, u32[]{:S(2)}) collective-permute-start(bf16[2,16,4096]{2,1,0:T(8,128)(2,1)S(1)} %pad_maximum_fusion.3), channel_id=1, source_target_pairs={{0,2},{1,23},{2,4},{3,1},{4,6},{5,3},{6,8},{7,5},{8,10},{9,7},{10,... | collective-permute-start | bytes 786440 | tf_op jit(solution)/shard_map/ppermute | solution.py:22
  31.4 11.4 %collective-permute-start.13 = (bf16[2,16,4096]{2,1,0:T(8,128)(2,1)S(1)}, bf16[2,16,4096]{2,1,0:T(8,128)(2,1)S(1)}, u32[]{:S(2)}, u32[]{:S(2)}) collective-permute-start(bf16[2,16,4096]{2,1,0:T(8,128)(2,1)S(1)} %slice.254), channel_id=1, source_target_pairs={{0,2},{1,23},{2,4},{3,1},{4,6},{5,3},{6,8},{7,5},{8,10},{9,7},{10,... | collective-permute-start | bytes 786440 | tf_op jit(solution)/shard_map/ppermute | solution.py:22
  37.2 9.5 %collective-permute-start.2 = (bf16[2,16,4096]{2,1,0:T(8,128)(2,1)S(1)}, bf16[2,16,4096]{2,1,0:T(8,128)(2,1)S(1)}, u32[]{:S(2)}, u32[]{:S(2)}) collective-permute-start(bf16[2,16,4096]{2,1,0:T(8,128)(2,1)S(1)} %collective-permute-done.1), channel_id=1, source_target_pairs={{0,2},{1,23},{2,4},{3,1},{4,6},{5,3},{6,8},{7,5},{8,10},{9,7},{10,... | collective-permute-start | bytes 786440 | tf_op jit(solution)/shard_map/ppermute | solution.py:22
  40.0 9.5 %collective-permute-start.8 = (bf16[2,16,4096]{2,1,0:T(8,128)(2,1)S(1)}, bf16[2,16,4096]{2,1,0:T(8,128)(2,1)S(1)}, u32[]{:S(2)}, u32[]{:S(2)}) collective-permute-start(bf16[2,16,4096]{2,1,0:T(8,128)(2,1)S(1)} %collective-permute-done.7), channel_id=1, source_target_pairs={{0,2},{1,23},{2,4},{3,1},{4,6},{5,3},{6,8},{7,5},{8,10},{9,7},{10,... | collective-permute-start | bytes 786440 | tf_op jit(solution)/shard_map/ppermute | solution.py:22
  42.8 9.5 %collective-permute-start.14 = (bf16[2,16,4096]{2,1,0:T(8,128)(2,1)S(1)}, bf16[2,16,4096]{2,1,0:T(8,128)(2,1)S(1)}, u32[]{:S(2)}, u32[]{:S(2)}) collective-permute-start(bf16[2,16,4096]{2,1,0:T(8,128)(2,1)S(1)} %collective-permute-done.13), channel_id=1, source_target_pairs={{0,2},{1,23},{2,4},{3,1},{4,6},{5,3},{6,8},{7,5},{8,10},{9,7},{10,... | collective-permute-start | bytes 786440 | tf_op jit(solution)/shard_map/ppermute | solution.py:22
  46.7 9.5 %collective-permute-start.3 = (bf16[2,16,4096]{2,1,0:T(8,128)(2,1)S(1)}, bf16[2,16,4096]{2,1,0:T(8,128)(2,1)S(1)}, u32[]{:S(2)}, u32[]{:S(2)}) collective-permute-start(bf16[2,16,4096]{2,1,0:T(8,128)(2,1)S(1)} %collective-permute-done.2), channel_id=1, source_target_pairs={{0,2},{1,23},{2,4},{3,1},{4,6},{5,3},{6,8},{7,5},{8,10},{9,7},{10,... | collective-permute-start | bytes 786440 | tf_op jit(solution)/shard_map/ppermute | solution.py:22
  49.5 9.5 %collective-permute-start.9 = (bf16[2,16,4096]{2,1,0:T(8,128)(2,1)S(1)}, bf16[2,16,4096]{2,1,0:T(8,128)(2,1)S(1)}, u32[]{:S(2)}, u32[]{:S(2)}) collective-permute-start(bf16[2,16,4096]{2,1,0:T(8,128)(2,1)S(1)} %collective-permute-done.8), channel_id=1, source_target_pairs={{0,2},{1,23},{2,4},{3,1},{4,6},{5,3},{6,8},{7,5},{8,10},{9,7},{10,... | collective-permute-start | bytes 786440 | tf_op jit(solution)/shard_map/ppermute | solution.py:22
  52.3 9.5 %collective-permute-start.15 = (bf16[2,16,4096]{2,1,0:T(8,128)(2,1)S(1)}, bf16[2,16,4096]{2,1,0:T(8,128)(2,1)S(1)}, u32[]{:S(2)}, u32[]{:S(2)}) collective-permute-start(bf16[2,16,4096]{2,1,0:T(8,128)(2,1)S(1)} %collective-permute-done.14), channel_id=1, source_target_pairs={{0,2},{1,23},{2,4},{3,1},{4,6},{5,3},{6,8},{7,5},{8,10},{9,7},{10,... | collective-permute-start | bytes 786440 | tf_op jit(solution)/shard_map/ppermute | solution.py:22
  55.2 20.4 %copy-start = (bf16[24,4096]{1,0:T(8,128)(2,1)S(1)}, bf16[24,4096]{1,0:T(8,128)(2,1)}, u32[]{:S(2)}) copy-start(bf16[24,4096]{1,0:T(8,128)(2,1)} %param.7) | copy-start | bytes 589828
  55.2 20.4 %copy-start.1 = (bf16[24,4096]{1,0:T(8,128)(2,1)S(1)}, bf16[24,4096]{1,0:T(8,128)(2,1)}, u32[]{:S(2)}) copy-start(bf16[24,4096]{1,0:T(8,128)(2,1)} %param.6) | copy-start | bytes 589828
  56.1 9.9 %collective-permute-start.4 = (bf16[2,16,4096]{2,1,0:T(8,128)(2,1)S(1)}, bf16[2,16,4096]{2,1,0:T(8,128)(2,1)S(1)}, u32[]{:S(2)}, u32[]{:S(2)}) collective-permute-start(bf16[2,16,4096]{2,1,0:T(8,128)(2,1)S(1)} %collective-permute-done.3), channel_id=1, source_target_pairs={{0,2},{1,23},{2,4},{3,1},{4,6},{5,3},{6,8},{7,5},{8,10},{9,7},{10,... | collective-permute-start | bytes 786440 | tf_op jit(solution)/shard_map/ppermute | solution.py:22
  58.9 9.5 %collective-permute-start.10 = (bf16[2,16,4096]{2,1,0:T(8,128)(2,1)S(1)}, bf16[2,16,4096]{2,1,0:T(8,128)(2,1)S(1)}, u32[]{:S(2)}, u32[]{:S(2)}) collective-permute-start(bf16[2,16,4096]{2,1,0:T(8,128)(2,1)S(1)} %collective-permute-done.9), channel_id=1, source_target_pairs={{0,2},{1,23},{2,4},{3,1},{4,6},{5,3},{6,8},{7,5},{8,10},{9,7},{10,... | collective-permute-start | bytes 786440 | tf_op jit(solution)/shard_map/ppermute | solution.py:22
  61.8 9.5 %collective-permute-start.16 = (bf16[2,16,4096]{2,1,0:T(8,128)(2,1)S(1)}, bf16[2,16,4096]{2,1,0:T(8,128)(2,1)S(1)}, u32[]{:S(2)}, u32[]{:S(2)}) collective-permute-start(bf16[2,16,4096]{2,1,0:T(8,128)(2,1)S(1)} %collective-permute-done.15), channel_id=1, source_target_pairs={{0,2},{1,23},{2,4},{3,1},{4,6},{5,3},{6,8},{7,5},{8,10},{9,7},{10,... | collective-permute-start | bytes 786440 | tf_op jit(solution)/shard_map/ppermute | solution.py:22
  66.1 9.5 %collective-permute-start.5 = (bf16[2,16,4096]{2,1,0:T(8,128)(2,1)S(1)}, bf16[2,16,4096]{2,1,0:T(8,128)(2,1)S(1)}, u32[]{:S(2)}, u32[]{:S(2)}) collective-permute-start(bf16[2,16,4096]{2,1,0:T(8,128)(2,1)S(1)} %collective-permute-done.4), channel_id=1, source_target_pairs={{0,2},{2,4},{4,6},{6,8},{8,10},{10,12},{12,14},{14,16},{16,18},{18... | collective-permute-start | bytes 786440 | tf_op jit(solution)/shard_map/ppermute | solution.py:22
  68.4 9.9 %collective-permute-start.11 = (bf16[2,16,4096]{2,1,0:T(8,128)(2,1)S(1)}, bf16[2,16,4096]{2,1,0:T(8,128)(2,1)S(1)}, u32[]{:S(2)}, u32[]{:S(2)}) collective-permute-start(bf16[2,16,4096]{2,1,0:T(8,128)(2,1)S(1)} %collective-permute-done.10), channel_id=1, source_target_pairs={{0,2},{1,23},{2,4},{3,1},{4,6},{5,3},{6,8},{7,5},{8,10},{9,7},{10,... | collective-permute-start | bytes 786440 | tf_op jit(solution)/shard_map/ppermute | solution.py:22
  71.2 9.9 %collective-permute-start.17 = (bf16[2,16,4096]{2,1,0:T(8,128)(2,1)S(1)}, bf16[2,16,4096]{2,1,0:T(8,128)(2,1)S(1)}, u32[]{:S(2)}, u32[]{:S(2)}) collective-permute-start(bf16[2,16,4096]{2,1,0:T(8,128)(2,1)S(1)} %collective-permute-done.16), channel_id=1, source_target_pairs={{0,2},{1,23},{2,4},{3,1},{4,6},{5,3},{6,8},{7,5},{8,10},{9,7},{10,... | collective-permute-start | bytes 786440 | tf_op jit(solution)/shard_map/ppermute | solution.py:22
  75.5 15.9 %copy-start.2 = (bf16[344,4096]{1,0:T(8,128)(2,1)S(1)}, bf16[344,4096]{1,0:T(8,128)(2,1)}, u32[]{:S(2)}) copy-start(bf16[344,4096]{1,0:T(8,128)(2,1)} %param.8) | copy-start | bytes 8454148
  78.3 9.5 %collective-permute-start.12 = (bf16[2,16,4096]{2,1,0:T(8,128)(2,1)S(1)}, bf16[2,16,4096]{2,1,0:T(8,128)(2,1)S(1)}, u32[]{:S(2)}, u32[]{:S(2)}) collective-permute-start(bf16[2,16,4096]{2,1,0:T(8,128)(2,1)S(1)} %collective-permute-done.11), channel_id=1, source_target_pairs={{0,2},{2,4},{4,6},{6,8},{8,10},{10,12},{12,14},{14,16},{16,18},{18... | collective-permute-start | bytes 786440 | tf_op jit(solution)/shard_map/ppermute | solution.py:22
  81.2 9.5 %collective-permute-start.18 = (bf16[2,16,4096]{2,1,0:T(8,128)(2,1)S(1)}, bf16[2,16,4096]{2,1,0:T(8,128)(2,1)S(1)}, u32[]{:S(2)}, u32[]{:S(2)}) collective-permute-start(bf16[2,16,4096]{2,1,0:T(8,128)(2,1)S(1)} %collective-permute-done.17), channel_id=1, source_target_pairs={{0,2},{2,4},{4,6},{6,8},{8,10},{10,12},{12,14},{14,16},{16,18},{18... | collective-permute-start | bytes 786440 | tf_op jit(solution)/shard_map/ppermute | solution.py:22
  83.7 6.9 %copy-start.7 = (bf16[240,4096]{1,0:T(8,128)(2,1)}, bf16[240,4096]{1,0:T(8,128)(2,1)S(1)}, u32[]{:S(2)}) copy-start(bf16[240,4096]{1,0:T(8,128)(2,1)S(1)} %get-tuple-element.65) | copy-start | bytes 5898244
  83.8 6.9 %copy-start.9 = (bf16[240,4096]{1,0:T(8,128)(2,1)}, bf16[240,4096]{1,0:T(8,128)(2,1)S(1)}, u32[]{:S(2)}) copy-start(bf16[240,4096]{1,0:T(8,128)(2,1)S(1)} %get-tuple-element.66) | copy-start | bytes 5898244
  91.4 1.8 %copy-start.3 = (bf16[344,4096]{1,0:T(8,128)(2,1)S(1)}, bf16[344,4096]{1,0:T(8,128)(2,1)}, u32[]{:S(2)}) copy-start(bf16[344,4096]{1,0:T(8,128)(2,1)} %param.10) | copy-start | bytes 8454148
  92.1 3.5 %copy-start.8 = (bf16[240,4096]{1,0:T(8,128)(2,1)S(1)}, bf16[240,4096]{1,0:T(8,128)(2,1)}, u32[]{:S(2)}) copy-start(bf16[240,4096]{1,0:T(8,128)(2,1)} %copy-done.7) | copy-start | bytes 5898244
  95.6 1.8 %copy-start.10 = (bf16[240,4096]{1,0:T(8,128)(2,1)S(1)}, bf16[240,4096]{1,0:T(8,128)(2,1)}, u32[]{:S(2)}) copy-start(bf16[240,4096]{1,0:T(8,128)(2,1)} %copy-done.9) | copy-start | bytes 5898244
  101.0 1.0 copy-start.4
  101.0 1.0 copy-start.5
  101.0 1.1 copy-start.6
  106.8 9.6 %collective-permute-start.35 = (bf16[16,4096]{1,0:T(8,128)(2,1)S(1)}, bf16[16,4096]{1,0:T(8,128)(2,1)S(1)}, u32[]{:S(2)}, u32[]{:S(2)}) collective-permute-start(bf16[16,4096]{1,0:T(8,128)(2,1)S(1)} %get-tuple-element.56), channel_id=1, source_target_pairs={{2,0},{4,2},{6,4},{8,6},{10,8},{12,10},{14,12},{16,14},{18,16},{20... | collective-permute-start | bytes 393224 | tf_op jit(solution)/shard_map/ppermute | solution.py:22
  110.5 11.1 %collective-permute-start.22 = (bf16[16,4096]{1,0:T(8,128)(2,1)S(1)}, bf16[16,4096]{1,0:T(8,128)(2,1)S(1)}, u32[]{:S(2)}, u32[]{:S(2)}) collective-permute-start(bf16[16,4096]{1,0:T(8,128)(2,1)S(1)} %get-tuple-element.58), channel_id=1, source_target_pairs={{2,0},{4,2},{6,4},{8,6},{10,8},{12,10},{14,12},{16,14},{18,16},{20... | collective-permute-start | bytes 393224 | tf_op jit(solution)/shard_map/ppermute | solution.py:22
  112.4 12.3 %collective-permute-start.28 = (bf16[16,4096]{1,0:T(8,128)(2,1)S(1)}, bf16[16,4096]{1,0:T(8,128)(2,1)S(1)}, u32[]{:S(2)}, u32[]{:S(2)}) collective-permute-start(bf16[16,4096]{1,0:T(8,128)(2,1)S(1)} %get-tuple-element.57), channel_id=1, source_target_pairs={{2,0},{4,2},{6,4},{8,6},{10,8},{12,10},{14,12},{16,14},{18,16},{20... | collective-permute-start | bytes 393224 | tf_op jit(solution)/shard_map/ppermute | solution.py:22
  115.1 52.5 %collective-permute-start.41 = (bf16[24,4096]{1,0:T(8,128)(2,1)S(1)}, bf16[24,4096]{1,0:T(8,128)(2,1)S(1)}, u32[]{:S(2)}, u32[]{:S(2)}) collective-permute-start(bf16[24,4096]{1,0:T(8,128)(2,1)S(1)} %slice.306), channel_id=1, source_target_pairs={{1,0},{3,2},{5,4},{7,6},{9,8},{11,10},{13,12},{15,14},{17,16},{19,... | collective-permute-start | bytes 589832 | tf_op jit(solution)/shard_map/ppermute | solution.py:22
  116.4 10.2 %collective-permute-start.36 = (bf16[16,4096]{1,0:T(8,128)(2,1)S(1)}, bf16[16,4096]{1,0:T(8,128)(2,1)S(1)}, u32[]{:S(2)}, u32[]{:S(2)}) collective-permute-start(bf16[16,4096]{1,0:T(8,128)(2,1)S(1)} %add_convert_fusion.5), channel_id=1, source_target_pairs={{2,0},{23,1},{4,2},{1,3},{6,4},{3,5},{8,6},{5,7},{10,8},{7,9},{12,... | collective-permute-start | bytes 393224 | tf_op jit(solution)/shard_map/ppermute | solution.py:22
  121.6 8.1 %collective-permute-start.23 = (bf16[16,4096]{1,0:T(8,128)(2,1)S(1)}, bf16[16,4096]{1,0:T(8,128)(2,1)S(1)}, u32[]{:S(2)}, u32[]{:S(2)}) collective-permute-start(bf16[16,4096]{1,0:T(8,128)(2,1)S(1)} %add_convert_fusion.15), channel_id=1, source_target_pairs={{2,0},{23,1},{4,2},{1,3},{6,4},{3,5},{8,6},{5,7},{10,8},{7,9},{12,... | collective-permute-start | bytes 393224 | tf_op jit(solution)/shard_map/ppermute | solution.py:22
  124.7 9.7 %collective-permute-start.29 = (bf16[16,4096]{1,0:T(8,128)(2,1)S(1)}, bf16[16,4096]{1,0:T(8,128)(2,1)S(1)}, u32[]{:S(2)}, u32[]{:S(2)}) collective-permute-start(bf16[16,4096]{1,0:T(8,128)(2,1)S(1)} %add_convert_fusion.10), channel_id=1, source_target_pairs={{2,0},{23,1},{4,2},{1,3},{6,4},{3,5},{8,6},{5,7},{10,8},{7,9},{12,... | collective-permute-start | bytes 393224 | tf_op jit(solution)/shard_map/ppermute | solution.py:22
  126.7 9.9 %collective-permute-start.37 = (bf16[16,4096]{1,0:T(8,128)(2,1)S(1)}, bf16[16,4096]{1,0:T(8,128)(2,1)S(1)}, u32[]{:S(2)}, u32[]{:S(2)}) collective-permute-start(bf16[16,4096]{1,0:T(8,128)(2,1)S(1)} %add_convert_fusion.4), channel_id=1, source_target_pairs={{2,0},{23,1},{4,2},{1,3},{6,4},{3,5},{8,6},{5,7},{10,8},{7,9},{12,... | collective-permute-start | bytes 393224 | tf_op jit(solution)/shard_map/ppermute | solution.py:22
  129.7 8.8 %collective-permute-start.24 = (bf16[16,4096]{1,0:T(8,128)(2,1)S(1)}, bf16[16,4096]{1,0:T(8,128)(2,1)S(1)}, u32[]{:S(2)}, u32[]{:S(2)}) collective-permute-start(bf16[16,4096]{1,0:T(8,128)(2,1)S(1)} %add_convert_fusion.14), channel_id=1, source_target_pairs={{2,0},{23,1},{4,2},{1,3},{6,4},{3,5},{8,6},{5,7},{10,8},{7,9},{12,... | collective-permute-start | bytes 393224 | tf_op jit(solution)/shard_map/ppermute | solution.py:22
  134.5 8.1 %collective-permute-start.30 = (bf16[16,4096]{1,0:T(8,128)(2,1)S(1)}, bf16[16,4096]{1,0:T(8,128)(2,1)S(1)}, u32[]{:S(2)}, u32[]{:S(2)}) collective-permute-start(bf16[16,4096]{1,0:T(8,128)(2,1)S(1)} %add_convert_fusion.9), channel_id=1, source_target_pairs={{2,0},{23,1},{4,2},{1,3},{6,4},{3,5},{8,6},{5,7},{10,8},{7,9},{12,... | collective-permute-start | bytes 393224 | tf_op jit(solution)/shard_map/ppermute | solution.py:22
  136.6 9.6 %collective-permute-start.38 = (bf16[16,4096]{1,0:T(8,128)(2,1)S(1)}, bf16[16,4096]{1,0:T(8,128)(2,1)S(1)}, u32[]{:S(2)}, u32[]{:S(2)}) collective-permute-start(bf16[16,4096]{1,0:T(8,128)(2,1)S(1)} %add_convert_fusion.3), channel_id=1, source_target_pairs={{2,0},{23,1},{4,2},{1,3},{6,4},{3,5},{8,6},{5,7},{10,8},{7,9},{12,... | collective-permute-start | bytes 393224 | tf_op jit(solution)/shard_map/ppermute | solution.py:22
  138.6 10.7 %collective-permute-start.25 = (bf16[16,4096]{1,0:T(8,128)(2,1)S(1)}, bf16[16,4096]{1,0:T(8,128)(2,1)S(1)}, u32[]{:S(2)}, u32[]{:S(2)}) collective-permute-start(bf16[16,4096]{1,0:T(8,128)(2,1)S(1)} %add_convert_fusion.13), channel_id=1, source_target_pairs={{2,0},{23,1},{4,2},{1,3},{6,4},{3,5},{8,6},{5,7},{10,8},{7,9},{12,... | collective-permute-start | bytes 393224 | tf_op jit(solution)/shard_map/ppermute | solution.py:22
  142.6 8.7 %collective-permute-start.31 = (bf16[16,4096]{1,0:T(8,128)(2,1)S(1)}, bf16[16,4096]{1,0:T(8,128)(2,1)S(1)}, u32[]{:S(2)}, u32[]{:S(2)}) collective-permute-start(bf16[16,4096]{1,0:T(8,128)(2,1)S(1)} %add_convert_fusion.8), channel_id=1, source_target_pairs={{2,0},{23,1},{4,2},{1,3},{6,4},{3,5},{8,6},{5,7},{10,8},{7,9},{12,... | collective-permute-start | bytes 393224 | tf_op jit(solution)/shard_map/ppermute | solution.py:22
  146.2 8.1 %collective-permute-start.39 = (bf16[16,4096]{1,0:T(8,128)(2,1)S(1)}, bf16[16,4096]{1,0:T(8,128)(2,1)S(1)}, u32[]{:S(2)}, u32[]{:S(2)}) collective-permute-start(bf16[16,4096]{1,0:T(8,128)(2,1)S(1)} %add_convert_fusion.2), channel_id=1, source_target_pairs={{2,0},{23,1},{4,2},{1,3},{6,4},{3,5},{8,6},{5,7},{10,8},{7,9},{12,... | collective-permute-start | bytes 393224 | tf_op jit(solution)/shard_map/ppermute | solution.py:22
  149.3 7.2 %collective-permute-start.26 = (bf16[16,4096]{1,0:T(8,128)(2,1)S(1)}, bf16[16,4096]{1,0:T(8,128)(2,1)S(1)}, u32[]{:S(2)}, u32[]{:S(2)}) collective-permute-start(bf16[16,4096]{1,0:T(8,128)(2,1)S(1)} %add_convert_fusion.12), channel_id=1, source_target_pairs={{2,0},{23,1},{4,2},{1,3},{6,4},{3,5},{8,6},{5,7},{10,8},{7,9},{12,... | collective-permute-start | bytes 393224 | tf_op jit(solution)/shard_map/ppermute | solution.py:22
  151.3 9.8 %collective-permute-start.32 = (bf16[16,4096]{1,0:T(8,128)(2,1)S(1)}, bf16[16,4096]{1,0:T(8,128)(2,1)S(1)}, u32[]{:S(2)}, u32[]{:S(2)}) collective-permute-start(bf16[16,4096]{1,0:T(8,128)(2,1)S(1)} %add_convert_fusion.7), channel_id=1, source_target_pairs={{2,0},{23,1},{4,2},{1,3},{6,4},{3,5},{8,6},{5,7},{10,8},{7,9},{12,... | collective-permute-start | bytes 393224 | tf_op jit(solution)/shard_map/ppermute | solution.py:22
  154.3 16.7 %collective-permute-start.40 = (bf16[16,4096]{1,0:T(8,128)(2,1)S(1)}, bf16[16,4096]{1,0:T(8,128)(2,1)S(1)}, u32[]{:S(2)}, u32[]{:S(2)}) collective-permute-start(bf16[16,4096]{1,0:T(8,128)(2,1)S(1)} %add_convert_fusion.1), channel_id=1, source_target_pairs={{2,1},{23,0},{4,3},{1,2},{6,5},{3,4},{8,7},{5,6},{10,9},{7,8},{12,... | collective-permute-start | bytes 393224 | tf_op jit(solution)/shard_map/ppermute | solution.py:22
  156.6 14.5 %collective-permute-start.27 = (bf16[16,4096]{1,0:T(8,128)(2,1)S(1)}, bf16[16,4096]{1,0:T(8,128)(2,1)S(1)}, u32[]{:S(2)}, u32[]{:S(2)}) collective-permute-start(bf16[16,4096]{1,0:T(8,128)(2,1)S(1)} %add_convert_fusion.11), channel_id=1, source_target_pairs={{2,0},{23,1},{4,2},{1,3},{6,4},{3,5},{8,6},{5,7},{10,8},{7,9},{12,... | collective-permute-start | bytes 393224 | tf_op jit(solution)/shard_map/ppermute | solution.py:22
  161.2 6.3 %collective-permute-start.33 = (bf16[8,4096]{1,0:T(8,128)(2,1)S(1)}, bf16[8,4096]{1,0:T(8,128)(2,1)S(1)}, u32[]{:S(2)}, u32[]{:S(2)}) collective-permute-start(bf16[8,4096]{1,0:T(8,128)(2,1)S(1)} %get-tuple-element.96), channel_id=1, source_target_pairs={{2,0},{23,1},{4,2},{1,3},{6,4},{3,5},{8,6},{5,7},{10,8},{7,9},{12,... | collective-permute-start | bytes 196616 | tf_op jit(solution)/shard_map/ppermute | solution.py:22
  164.3 6.8 %collective-permute-start.34 = (bf16[8,4096]{1,0:T(8,128)(2,1)S(1)}, bf16[8,4096]{1,0:T(8,128)(2,1)S(1)}, u32[]{:S(2)}, u32[]{:S(2)}) collective-permute-start(bf16[8,4096]{1,0:T(8,128)(2,1)S(1)} %get-tuple-element.95), channel_id=1, source_target_pairs={{2,1},{23,0},{4,3},{1,2},{6,5},{3,4},{8,7},{5,6},{10,9},{7,8},{12,... | collective-permute-start | bytes 196616 | tf_op jit(solution)/shard_map/ppermute | solution.py:22

commit v5 on v2

--- a/solution.py
+++ b/solution.py
@@ -35,6 +35,8 @@
     home = [(target, source) for source, target in out]
     out_far = [(source, target) for source, target in out if source % CORES == 0]
     home_far = [(target, source) for source, target in out_far]
+    home_cross = [(source, target ^ 1) for source, target in home]
+    to_first = [(i + 1, i) for i in range(0, members, CORES)]
 
     mine = jnp.stack((kept_input, kept_grad), axis=0)
     other = hop(mine, sibling)
@@ -50,7 +52,10 @@
     def terms(pieces):
         inputs = jnp.concatenate([piece[0] for piece in pieces], axis=0)
         out_grads = jnp.concatenate([piece[1] for piece in pieces], axis=0)
-        preact = lax.dot_general(inputs, up, contract, preferred_element_type=jnp.float32) + bias
+        preact = lax.optimization_barrier(
+            lax.dot_general(inputs, up, contract, preferred_element_type=jnp.float32)
+            + bias
+        )
         down_grad = lax.dot_general(out_grads, down, contract, preferred_element_type=jnp.float32)
         pre_grad = (gelu_slope(preact) * down_grad).astype(jnp.bfloat16)
         pre_grad = lax.optimization_barrier(pre_grad)
@@ -67,29 +72,27 @@
     chain_other[steps] = jnp.where(core == 0, chain_other[steps], other)
 
     arrivals = [piece for pair in zip(chain_mine[1:steps], chain_other[1:steps]) for piece in pair]
-    near = terms(arrivals)
-    far_pieces, near = lax.optimization_barrier(
-        ([chain_mine[steps], chain_other[steps]], near)
-    )
-    far = terms(far_pieces)
-    for_mine = near[0::2] + far[:1]
-    for_other = near[1::2] + far[1:]
+    near = lax.optimization_barrier(terms(arrivals[:-1]))
+    (far_mine,) = terms(chain_mine[steps:])
+    late_other, far_other = lax.optimization_barrier(terms([arrivals[-1], chain_other[steps]]))
+    for_mine = near[0::2] + [far_mine]
+    for_other = near[1::2] + [late_other, far_other]
 
     def add(moved, part):
         return (moved.astype(jnp.float32) + part.astype(jnp.float32)).astype(jnp.bfloat16)
 
+    sum_mine = hop(for_mine[-1], home_far)
     sum_other = hop(for_other[-1], home_far)
-    sum_mine = hop(for_mine[-1], home_far)
     for step in range(2, steps + 1):
-        sum_other = hop(add(sum_other, for_other[steps - step]), home)
+        crossing = home_cross if step == steps else home
         sum_mine = hop(add(sum_mine, for_mine[steps - step]), home)
-    kept_here = core == 1
-    sum_other = sum_other.astype(jnp.float32) + jnp.where(kept_here, for_other[-1], 0.0)
-    from_sibling = hop(sum_other.astype(jnp.bfloat16), sibling)
+        sum_other = hop(add(sum_other, for_other[steps - step]), crossing)
+    kept = jnp.where(core == 1, for_mine[-1], 0.0).astype(jnp.float32)
+    joined = hop(for_other[-1], to_first)
     branch = (
         sum_mine.astype(jnp.float32)
-        + jnp.where(kept_here, for_mine[-1], 0.0).astype(jnp.float32)
-        + from_sibling.astype(jnp.float32)
+        + sum_other.astype(jnp.float32)
+        + (kept + joined.astype(jnp.float32))
     ).astype(jnp.bfloat16)
     usable = jnp.arange(slots, dtype=jnp.int32) < kept_count[0]
     summed = kept_grad.astype(jnp.float32) + branch.astype(jnp.float32)

time: 163 us -> 180 us (1.10)
  the two profiles are of different devices: /device:TPU:1 before, /device:TPU:58 now
where the time goes in v5:
time: 180 us; the launch traced here: 179 us
  starting transfers between devices  83.4 us (46%)
  waiting for transfers between devices  68.9 us (38%)
  matrix products  14.1 us (8%)
  other arithmetic  7.93 us (4%)
  local copies, waits for them, and re-layouts  3.1 us (2%)
    ppermute x29, starting transfers between devices, hop(): return lax.ppermute(block, 'tensor', pairs)  83.4 us
    ppermute x29, waiting for transfers between devices, hop(): return lax.ppermute(block, 'tensor', pairs)  68.9 us
    dot_general x3, matrix products, terms(): lax.dot_general(out_grads, down, contract, preferred_element_type=jnp.flo...  5.29 us
    dot_general x3, matrix products, terms(): lax.dot_general(inputs, up, contract, preferred_element_type=jnp.float32)  5.24 us
    concatenate x3, other arithmetic, both(): return lax.optimization_barrier(jnp.concatenate([block, theirs], axis=0))  3.78 us
  transfers between devices with their start and end apart: 29, of which 17 were waited for; matrix products, arithmetic and copies ran while one was open for 8% of the time, Pallas kernels for 0%

profile of v5, /device:TPU:58, one launch (start us, length us, event | category | flops | bytes accessed | tf_op | source)
XLA Modules:
  0.0 178.9 jit_solution(17517503796920263720)
XLA Ops:
  0.0 1.8 %pad_maximum_fusion.2 = bf16[2,24,4096]{2,1,0:T(8,128)(2,1)} fusion(bf16[1,24,4096]{2,1,0:T(8,128)(2,1)} %bitcast.104, bf16[1,24,4096]{2,1,0:T(8,128)(2,1)} %bitcast.106), kind=kLoop, calls=%fused_computation.19 | loop fusion | flops 196608 | bytes 786432 | tf_op jit(solution)/shard_map/stack | solution.py:41
  1.8 1.9 %collective-permute-start.10 = (bf16[2,24,4096]{2,1,0:T(8,128)(2,1)}, bf16[2,24,4096]{2,1,0:T(8,128)(2,1)}, u32[]{:S(2)}, u32[]{:S(2)}) collective-permute-start(bf16[2,24,4096]{2,1,0:T(8,128)(2,1)} %pad_maximum_fusion.2), channel_id=1, source_target_pairs={{0,1},{1,0},{2,3},{3,2},{4,5},{5,4},{6,7},{7,6},{8,9},{9,8},{10,11... | collective-permute-start | bytes 1179656 | tf_op jit(solution)/shard_map/ppermute | solution.py:21
  3.7 4.3 %collective-permute-start = (bf16[2,24,4096]{2,1,0:T(8,128)(2,1)}, bf16[2,24,4096]{2,1,0:T(8,128)(2,1)S(1)}, u32[]{:S(2)}, u32[]{:S(2)}) collective-permute-start(bf16[2,24,4096]{2,1,0:T(8,128)(2,1)} %pad_maximum_fusion.2), channel_id=1, source_target_pairs={{0,2},{1,23},{2,4},{3,1},{4,6},{5,3},{6,8},{7,5},{8,10},{9,7},{10,... | collective-permute-start | bytes 1179656 | tf_op jit(solution)/shard_map/ppermute | solution.py:21
  8.0 12.4 %collective-permute-start.6 = (bf16[344,4096]{1,0:T(8,128)(2,1)}, bf16[344,4096]{1,0:T(8,128)(2,1)S(1)}, u32[]{:S(2)}, u32[]{:S(2)}) collective-permute-start(bf16[344,4096]{1,0:T(8,128)(2,1)} %param.8), channel_id=1, source_target_pairs={{0,1},{1,0},{2,3},{3,2},{4,5},{5,4},{6,7},{7,6},{8,9},{9,8},{10,11... | collective-permute-start | bytes 8454152 | tf_op jit(solution)/shard_map/ppermute | solution.py:21
  20.5 1.9 %collective-permute-start.7 = (bf16[344]{0:T(512)(128)(2,1)}, bf16[344]{0:T(512)(128)(2,1)S(1)}, u32[]{:S(2)}, u32[]{:S(2)}) collective-permute-start(bf16[344]{0:T(512)(128)(2,1)} %param.9), channel_id=1, source_target_pairs={{0,1},{1,0},{2,3},{3,2},{4,5},{5,4},{6,7},{7,6},{8,9},{9,8},{10,11... | collective-permute-start | bytes 2072 | tf_op jit(solution)/shard_map/ppermute | solution.py:21
  22.4 2.4 %collective-permute-start.8 = (bf16[344,4096]{1,0:T(8,128)(2,1)}, bf16[344,4096]{1,0:T(8,128)(2,1)}, u32[]{:S(2)}, u32[]{:S(2)}) collective-permute-start(bf16[344,4096]{1,0:T(8,128)(2,1)} %param.10), channel_id=1, source_target_pairs={{0,1},{1,0},{2,3},{3,2},{4,5},{5,4},{6,7},{7,6},{8,9},{9,8},{10,11... | collective-permute-start | bytes 8454152 | tf_op jit(solution)/shard_map/ppermute | solution.py:21
  24.8 0.6 collective-permute-done.7
  25.5 0.8 pad_maximum_fusion.3
  26.2 1.9 %collective-permute-start.11 = (bf16[2,24,4096]{2,1,0:T(8,128)(2,1)}, bf16[2,24,4096]{2,1,0:T(8,128)(2,1)S(1)}, u32[]{:S(2)}, u32[]{:S(2)}) collective-permute-start(bf16[2,24,4096]{2,1,0:T(8,128)(2,1)} %collective-permute-done.10), channel_id=1, source_target_pairs={{0,2},{1,23},{2,4},{3,1},{4,6},{5,3},{6,8},{7,5},{8,10},{9,7},{10,... | collective-permute-start | bytes 1179656 | tf_op jit(solution)/shard_map/ppermute | solution.py:21
  28.1 1.9 %collective-permute-start.1 = (bf16[2,24,4096]{2,1,0:T(8,128)(2,1)S(1)}, bf16[2,24,4096]{2,1,0:T(8,128)(2,1)S(1)}, u32[]{:S(2)}, u32[]{:S(2)}) collective-permute-start(bf16[2,24,4096]{2,1,0:T(8,128)(2,1)S(1)} %collective-permute-done), channel_id=1, source_target_pairs={{0,2},{1,23},{2,4},{3,1},{4,6},{5,3},{6,8},{7,5},{8,10},{9,7},{10,... | collective-permute-start | bytes 1179656 | tf_op jit(solution)/shard_map/ppermute | solution.py:21
  30.1 7.2 %collective-permute-done.11 = bf16[2,24,4096]{2,1,0:T(8,128)(2,1)S(1)} collective-permute-done((bf16[2,24,4096]{2,1,0:T(8,128)(2,1)}, bf16[2,24,4096]{2,1,0:T(8,128)(2,1)S(1)}, u32[]{:S(2)}, u32[]{:S(2)}) %collective-permute-start.11) | collective-permute-done | bytes 393248 | tf_op jit(solution)/shard_map/ppermute | solution.py:21
  37.3 1.9 %collective-permute-start.12 = (bf16[2,24,4096]{2,1,0:T(8,128)(2,1)S(1)}, bf16[2,24,4096]{2,1,0:T(8,128)(2,1)S(1)}, u32[]{:S(2)}, u32[]{:S(2)}) collective-permute-start(bf16[2,24,4096]{2,1,0:T(8,128)(2,1)S(1)} %collective-permute-done.11), channel_id=1, source_target_pairs={{0,2},{1,23},{2,4},{3,1},{4,6},{5,3},{6,8},{7,5},{8,10},{9,7},{10,... | collective-permute-start | bytes 1179656 | tf_op jit(solution)/shard_map/ppermute | solution.py:21
  39.2 2.3 %collective-permute-done.1 = bf16[2,24,4096]{2,1,0:T(8,128)(2,1)S(1)} collective-permute-done((bf16[2,24,4096]{2,1,0:T(8,128)(2,1)S(1)}, bf16[2,24,4096]{2,1,0:T(8,128)(2,1)S(1)}, u32[]{:S(2)}, u32[]{:S(2)}) %collective-permute-start.1) | collective-permute-done | bytes 393248 | tf_op jit(solution)/shard_map/ppermute | solution.py:21
  41.5 1.9 %collective-permute-start.2 = (bf16[2,24,4096]{2,1,0:T(8,128)(2,1)S(1)}, bf16[2,24,4096]{2,1,0:T(8,128)(2,1)S(1)}, u32[]{:S(2)}, u32[]{:S(2)}) collective-permute-start(bf16[2,24,4096]{2,1,0:T(8,128)(2,1)S(1)} %collective-permute-done.1), channel_id=1, source_target_pairs={{0,2},{1,23},{2,4},{3,1},{4,6},{5,3},{6,8},{7,5},{8,10},{9,7},{10,... | collective-permute-start | bytes 1179656 | tf_op jit(solution)/shard_map/ppermute | solution.py:21
  43.5 4.7 %collective-permute-done.12 = bf16[2,24,4096]{2,1,0:T(8,128)(2,1)S(1)} collective-permute-done((bf16[2,24,4096]{2,1,0:T(8,128)(2,1)S(1)}, bf16[2,24,4096]{2,1,0:T(8,128)(2,1)S(1)}, u32[]{:S(2)}, u32[]{:S(2)}) %collective-permute-start.12) | collective-permute-done | bytes 393248 | tf_op jit(solution)/shard_map/ppermute | solution.py:21
  48.2 1.9 %collective-permute-start.13 = (bf16[2,24,4096]{2,1,0:T(8,128)(2,1)S(1)}, bf16[2,24,4096]{2,1,0:T(8,128)(2,1)S(1)}, u32[]{:S(2)}, u32[]{:S(2)}) collective-permute-start(bf16[2,24,4096]{2,1,0:T(8,128)(2,1)S(1)} %collective-permute-done.12), channel_id=1, source_target_pairs={{0,2},{1,23},{2,4},{3,1},{4,6},{5,3},{6,8},{7,5},{8,10},{9,7},{10,... | collective-permute-start | bytes 1179656 | tf_op jit(solution)/shard_map/ppermute | solution.py:21
  50.1 2.3 %collective-permute-done.2 = bf16[2,24,4096]{2,1,0:T(8,128)(2,1)S(1)} collective-permute-done((bf16[2,24,4096]{2,1,0:T(8,128)(2,1)S(1)}, bf16[2,24,4096]{2,1,0:T(8,128)(2,1)S(1)}, u32[]{:S(2)}, u32[]{:S(2)}) %collective-permute-start.2) | collective-permute-done | bytes 393248 | tf_op jit(solution)/shard_map/ppermute | solution.py:21
  52.4 1.9 %collective-permute-start.3 = (bf16[2,24,4096]{2,1,0:T(8,128)(2,1)S(1)}, bf16[2,24,4096]{2,1,0:T(8,128)(2,1)S(1)}, u32[]{:S(2)}, u32[]{:S(2)}) collective-permute-start(bf16[2,24,4096]{2,1,0:T(8,128)(2,1)S(1)} %collective-permute-done.2), channel_id=1, source_target_pairs={{0,2},{1,23},{2,4},{3,1},{4,6},{5,3},{6,8},{7,5},{8,10},{9,7},{10,... | collective-permute-start | bytes 1179656 | tf_op jit(solution)/shard_map/ppermute | solution.py:21
  54.4 4.6 %collective-permute-done.13 = bf16[2,24,4096]{2,1,0:T(8,128)(2,1)S(1)} collective-permute-done((bf16[2,24,4096]{2,1,0:T(8,128)(2,1)S(1)}, bf16[2,24,4096]{2,1,0:T(8,128)(2,1)S(1)}, u32[]{:S(2)}, u32[]{:S(2)}) %collective-permute-start.13) | collective-permute-done | bytes 393248 | tf_op jit(solution)/shard_map/ppermute | solution.py:21
  59.0 1.9 %collective-permute-start.14 = (bf16[2,24,4096]{2,1,0:T(8,128)(2,1)S(1)}, bf16[2,24,4096]{2,1,0:T(8,128)(2,1)S(1)}, u32[]{:S(2)}, u32[]{:S(2)}) collective-permute-start(bf16[2,24,4096]{2,1,0:T(8,128)(2,1)S(1)} %collective-permute-done.13), channel_id=1, source_target_pairs={{0,2},{1,23},{2,4},{3,1},{4,6},{5,3},{6,8},{7,5},{8,10},{9,7},{10,... | collective-permute-start | bytes 1179656 | tf_op jit(solution)/shard_map/ppermute | solution.py:21
  61.0 2.3 %collective-permute-done.3 = bf16[2,24,4096]{2,1,0:T(8,128)(2,1)S(1)} collective-permute-done((bf16[2,24,4096]{2,1,0:T(8,128)(2,1)S(1)}, bf16[2,24,4096]{2,1,0:T(8,128)(2,1)S(1)}, u32[]{:S(2)}, u32[]{:S(2)}) %collective-permute-start.3) | collective-permute-done | bytes 393248 | tf_op jit(solution)/shard_map/ppermute | solution.py:21
  63.3 1.9 %collective-permute-start.4 = (bf16[2,24,4096]{2,1,0:T(8,128)(2,1)S(1)}, bf16[2,24,4096]{2,1,0:T(8,128)(2,1)S(1)}, u32[]{:S(2)}, u32[]{:S(2)}) collective-permute-start(bf16[2,24,4096]{2,1,0:T(8,128)(2,1)S(1)} %collective-permute-done.3), channel_id=1, source_target_pairs={{0,2},{1,23},{2,4},{3,1},{4,6},{5,3},{6,8},{7,5},{8,10},{9,7},{10,... | collective-permute-start | bytes 1179656 | tf_op jit(solution)/shard_map/ppermute | solution.py:21
  65.2 8.9 %collective-permute-done.4 = bf16[2,24,4096]{2,1,0:T(8,128)(2,1)S(1)} collective-permute-done((bf16[2,24,4096]{2,1,0:T(8,128)(2,1)S(1)}, bf16[2,24,4096]{2,1,0:T(8,128)(2,1)S(1)}, u32[]{:S(2)}, u32[]{:S(2)}) %collective-permute-start.4) | collective-permute-done | bytes 393248 | tf_op jit(solution)/shard_map/ppermute | solution.py:21
  74.1 1.9 %collective-permute-start.5 = (bf16[2,24,4096]{2,1,0:T(8,128)(2,1)S(1)}, bf16[2,24,4096]{2,1,0:T(8,128)(2,1)S(1)}, u32[]{:S(2)}, u32[]{:S(2)}) collective-permute-start(bf16[2,24,4096]{2,1,0:T(8,128)(2,1)S(1)} %collective-permute-done.4), channel_id=1, source_target_pairs={{0,2},{2,4},{4,6},{6,8},{8,10},{10,12},{12,14},{14,16},{16,18},{18... | collective-permute-start | bytes 1179656 | tf_op jit(solution)/shard_map/ppermute | solution.py:21
  76.1 1.9 %collective-permute-start.20 = (bf16[2,24,4096]{2,1,0:T(8,128)(2,1)S(1)}, bf16[2,24,4096]{2,1,0:T(8,128)(2,1)S(1)}, u32[]{:S(2)}, u32[]{:S(2)}) collective-permute-start(bf16[2,24,4096]{2,1,0:T(8,128)(2,1)S(1)} %collective-permute-done.14), channel_id=1, source_target_pairs={{0,2},{1,23},{2,4},{3,1},{4,6},{5,3},{6,8},{7,5},{8,10},{9,7},{10,... | collective-permute-start | bytes 1179656 | tf_op jit(solution)/shard_map/ppermute | solution.py:21
  78.1 11.1 %collective-permute-done.20 = bf16[2,24,4096]{2,1,0:T(8,128)(2,1)S(1)} collective-permute-done((bf16[2,24,4096]{2,1,0:T(8,128)(2,1)S(1)}, bf16[2,24,4096]{2,1,0:T(8,128)(2,1)S(1)}, u32[]{:S(2)}, u32[]{:S(2)}) %collective-permute-start.20) | collective-permute-done | bytes 393248 | tf_op jit(solution)/shard_map/ppermute | solution.py:21
  89.2 1.9 %collective-permute-start.21 = (bf16[2,24,4096]{2,1,0:T(8,128)(2,1)S(1)}, bf16[2,24,4096]{2,1,0:T(8,128)(2,1)S(1)}, u32[]{:S(2)}, u32[]{:S(2)}) collective-permute-start(bf16[2,24,4096]{2,1,0:T(8,128)(2,1)S(1)} %collective-permute-done.20), channel_id=1, source_target_pairs={{0,2},{2,4},{4,6},{6,8},{8,10},{10,12},{12,14},{14,16},{16,18},{18... | collective-permute-start | bytes 1179656 | tf_op jit(solution)/shard_map/ppermute | solution.py:21
  91.2 0.8 slice_bitcast_fusion.3
  92.0 8.1 %collective-permute-done.21 = bf16[2,24,4096]{2,1,0:T(8,128)(2,1)S(1)} collective-permute-done((bf16[2,24,4096]{2,1,0:T(8,128)(2,1)S(1)}, bf16[2,24,4096]{2,1,0:T(8,128)(2,1)S(1)}, u32[]{:S(2)}, u32[]{:S(2)}) %collective-permute-start.21) | collective-permute-done | bytes 393248 | tf_op jit(solution)/shard_map/ppermute | solution.py:21
  100.1 0.8 slice_bitcast_fusion.2
  100.9 0.7 pad_maximum_fusion
  101.6 1.1 copy-done.1
  102.7 2.4 %pad_maximum_fusion.1 = bf16[688,4096]{1,0:T(8,128)(2,1)S(1)} fusion(bf16[344,4096]{1,0:T(8,128)(2,1)} %collective-permute-done.8, bf16[344,4096]{1,0:T(8,128)(2,1)S(1)} %copy-done.1), kind=kLoop, calls=%fused_computation.1 | loop fusion | flops 11272192 | bytes 11272192 | tf_op jit(solution)/shard_map/concatenate | solution.py:46
  105.1 1.7 convolution_add_fusion.1
  106.9 1.7 fusion.1
  108.7 1.1 convolution_convert_fusion.1
  109.8 1.9 %collective-permute-start.22 = (bf16[24,4096]{1,0:T(8,128)(2,1)S(1)}, bf16[24,4096]{1,0:T(8,128)(2,1)S(1)}, u32[]{:S(2)}, u32[]{:S(2)}) collective-permute-start(bf16[24,4096]{1,0:T(8,128)(2,1)S(1)} %get-tuple-element.21), channel_id=1, source_target_pairs={{2,0},{4,2},{6,4},{8,6},{10,8},{12,10},{14,12},{16,14},{18,16},{20... | collective-permute-start | bytes 589832 | tf_op jit(solution)/shard_map/ppermute | solution.py:21
  111.7 1.5 collective-permute-start.28
  113.2 1.9 %convolution_add_fusion = f32[216,688]{1,0:T(8,128)S(1)} fusion(bf16[216,4096]{1,0:T(8,128)(2,1)S(1)} %copy-done.9, bf16[688,4096]{1,0:T(8,128)(2,1)S(1)} %pad_maximum_fusion, f32[688]{0:T(1024)S(1)} %convert_element_type.138), kind=kOutput, calls=%fused_computation.6 | convolution fusion | flops 1217545344 | bytes 8002752 | tf_op jit(solution)/shard_map/dot_general | solution.py:56
  115.2 2.0 %fusion = bf16[216,688]{1,0:T(8,128)(2,1)S(1)} fusion(bf16[216,4096]{1,0:T(8,128)(2,1)S(1)} %copy-done.11, bf16[688,4096]{1,0:T(8,128)(2,1)S(1)} %pad_maximum_fusion.1, f32[216,688]{1,0:T(8,128)S(1)} %convolution_add_fusion), kind=kOutput, calls=%fused_computation.7 | convolution fusion | flops 1218882816 | bytes 8297216 | tf_op jit(solution)/shard_map/dot_general | solution.py:59
  117.1 1.6 convolution_convert_fusion
  118.8 1.6 convolution_add_fusion.2
  120.3 1.6 fusion.2
  121.9 0.9 convolution_convert_fusion.2
  122.8 1.9 %collective-permute-start.9 = (bf16[24,4096]{1,0:T(8,128)(2,1)S(1)}, bf16[24,4096]{1,0:T(8,128)(2,1)S(1)}, u32[]{:S(2)}, u32[]{:S(2)}) collective-permute-start(bf16[24,4096]{1,0:T(8,128)(2,1)S(1)} %convolution_convert_fusion.2), channel_id=1, source_target_pairs={{2,0},{4,2},{6,4},{8,6},{10,8},{12,10},{14,12},{16,14},{18,16},{20... | collective-permute-start | bytes 589832 | tf_op jit(solution)/shard_map/ppermute | solution.py:21
  124.7 0.1 fusion.41
  124.9 5.5 %collective-permute-done.9 = bf16[24,4096]{1,0:T(8,128)(2,1)S(1)} collective-permute-done((bf16[24,4096]{1,0:T(8,128)(2,1)S(1)}, bf16[24,4096]{1,0:T(8,128)(2,1)S(1)}, u32[]{:S(2)}, u32[]{:S(2)}) %collective-permute-start.9) | collective-permute-done | bytes 196640 | tf_op jit(solution)/shard_map/ppermute | solution.py:21
  130.4 3.1 %collective-permute-start.15 = (bf16[24,4096]{1,0:T(8,128)(2,1)S(1)}, bf16[24,4096]{1,0:T(8,128)(2,1)S(1)}, u32[]{:S(2)}, u32[]{:S(2)}) collective-permute-start(bf16[24,4096]{1,0:T(8,128)(2,1)S(1)} %add_convert_fusion.10), channel_id=1, source_target_pairs={{2,0},{23,1},{4,2},{1,3},{6,4},{3,5},{8,6},{5,7},{10,8},{7,9},{12,... | collective-permute-start | bytes 589832 | tf_op jit(solution)/shard_map/ppermute | solution.py:21
  133.6 1.9 %collective-permute-start.23 = (bf16[24,4096]{1,0:T(8,128)(2,1)S(1)}, bf16[24,4096]{1,0:T(8,128)(2,1)S(1)}, u32[]{:S(2)}, u32[]{:S(2)}) collective-permute-start(bf16[24,4096]{1,0:T(8,128)(2,1)S(1)} %add_convert_fusion.5), channel_id=1, source_target_pairs={{2,0},{23,1},{4,2},{1,3},{6,4},{3,5},{8,6},{5,7},{10,8},{7,9},{12,... | collective-permute-start | bytes 589832 | tf_op jit(solution)/shard_map/ppermute | solution.py:21
  135.6 2.4 %collective-permute-done.15 = bf16[24,4096]{1,0:T(8,128)(2,1)S(1)} collective-permute-done((bf16[24,4096]{1,0:T(8,128)(2,1)S(1)}, bf16[24,4096]{1,0:T(8,128)(2,1)S(1)}, u32[]{:S(2)}, u32[]{:S(2)}) %collective-permute-start.15) | collective-permute-done | bytes 196640 | tf_op jit(solution)/shard_map/ppermute | solution.py:21
  138.0 4.3 %collective-permute-start.16 = (bf16[24,4096]{1,0:T(8,128)(2,1)S(1)}, bf16[24,4096]{1,0:T(8,128)(2,1)S(1)}, u32[]{:S(2)}, u32[]{:S(2)}) collective-permute-start(bf16[24,4096]{1,0:T(8,128)(2,1)S(1)} %add_convert_fusion.9), channel_id=1, source_target_pairs={{2,0},{23,1},{4,2},{1,3},{6,4},{3,5},{8,6},{5,7},{10,8},{7,9},{12,... | collective-permute-start | bytes 589832 | tf_op jit(solution)/shard_map/ppermute | solution.py:21
  142.5 2.0 %collective-permute-start.24 = (bf16[24,4096]{1,0:T(8,128)(2,1)S(1)}, bf16[24,4096]{1,0:T(8,128)(2,1)S(1)}, u32[]{:S(2)}, u32[]{:S(2)}) collective-permute-start(bf16[24,4096]{1,0:T(8,128)(2,1)S(1)} %add_convert_fusion.4), channel_id=1, source_target_pairs={{2,0},{23,1},{4,2},{1,3},{6,4},{3,5},{8,6},{5,7},{10,8},{7,9},{12,... | collective-permute-start | bytes 589832 | tf_op jit(solution)/shard_map/ppermute | solution.py:21
  144.5 1.1 collective-permute-done.16
  145.7 5.6 %collective-permute-start.17 = (bf16[24,4096]{1,0:T(8,128)(2,1)S(1)}, bf16[24,4096]{1,0:T(8,128)(2,1)S(1)}, u32[]{:S(2)}, u32[]{:S(2)}) collective-permute-start(bf16[24,4096]{1,0:T(8,128)(2,1)S(1)} %add_convert_fusion.8), channel_id=1, source_target_pairs={{2,0},{23,1},{4,2},{1,3},{6,4},{3,5},{8,6},{5,7},{10,8},{7,9},{12,... | collective-permute-start | bytes 589832 | tf_op jit(solution)/shard_map/ppermute | solution.py:21
  151.3 2.0 %collective-permute-start.25 = (bf16[24,4096]{1,0:T(8,128)(2,1)S(1)}, bf16[24,4096]{1,0:T(8,128)(2,1)S(1)}, u32[]{:S(2)}, u32[]{:S(2)}) collective-permute-start(bf16[24,4096]{1,0:T(8,128)(2,1)S(1)} %add_convert_fusion.3), channel_id=1, source_target_pairs={{2,0},{23,1},{4,2},{1,3},{6,4},{3,5},{8,6},{5,7},{10,8},{7,9},{12,... | collective-permute-start | bytes 589832 | tf_op jit(solution)/shard_map/ppermute | solution.py:21
  153.3 1.1 collective-permute-done.17
  154.4 5.6 %collective-permute-start.18 = (bf16[24,4096]{1,0:T(8,128)(2,1)S(1)}, bf16[24,4096]{1,0:T(8,128)(2,1)S(1)}, u32[]{:S(2)}, u32[]{:S(2)}) collective-permute-start(bf16[24,4096]{1,0:T(8,128)(2,1)S(1)} %add_convert_fusion.7), channel_id=1, source_target_pairs={{2,0},{23,1},{4,2},{1,3},{6,4},{3,5},{8,6},{5,7},{10,8},{7,9},{12,... | collective-permute-start | bytes 589832 | tf_op jit(solution)/shard_map/ppermute | solution.py:21
  160.1 2.0 %collective-permute-start.26 = (bf16[24,4096]{1,0:T(8,128)(2,1)S(1)}, bf16[24,4096]{1,0:T(8,128)(2,1)S(1)}, u32[]{:S(2)}, u32[]{:S(2)}) collective-permute-start(bf16[24,4096]{1,0:T(8,128)(2,1)S(1)} %add_convert_fusion.2), channel_id=1, source_target_pairs={{2,0},{23,1},{4,2},{1,3},{6,4},{3,5},{8,6},{5,7},{10,8},{7,9},{12,... | collective-permute-start | bytes 589832 | tf_op jit(solution)/shard_map/ppermute | solution.py:21
  162.1 1.1 collective-permute-done.18
  163.3 5.6 %collective-permute-start.19 = (bf16[24,4096]{1,0:T(8,128)(2,1)S(1)}, bf16[24,4096]{1,0:T(8,128)(2,1)S(1)}, u32[]{:S(2)}, u32[]{:S(2)}) collective-permute-start(bf16[24,4096]{1,0:T(8,128)(2,1)S(1)} %add_convert_fusion.6), channel_id=1, source_target_pairs={{2,0},{23,1},{4,2},{1,3},{6,4},{3,5},{8,6},{5,7},{10,8},{7,9},{12,... | collective-permute-start | bytes 589832 | tf_op jit(solution)/shard_map/ppermute | solution.py:21
  168.9 1.9 %collective-permute-start.27 = (bf16[24,4096]{1,0:T(8,128)(2,1)S(1)}, bf16[24,4096]{1,0:T(8,128)(2,1)S(1)}, u32[]{:S(2)}, u32[]{:S(2)}) collective-permute-start(bf16[24,4096]{1,0:T(8,128)(2,1)S(1)} %add_convert_fusion.1), channel_id=1, source_target_pairs={{2,1},{23,0},{4,3},{1,2},{6,5},{3,4},{8,7},{5,6},{10,9},{7,8},{12,... | collective-permute-start | bytes 589832 | tf_op jit(solution)/shard_map/ppermute | solution.py:21
  171.5 0.5 collective-permute-done.19
  172.0 5.1 %collective-permute-done.27 = bf16[24,4096]{1,0:T(8,128)(2,1)S(1)} collective-permute-done((bf16[24,4096]{1,0:T(8,128)(2,1)S(1)}, bf16[24,4096]{1,0:T(8,128)(2,1)S(1)}, u32[]{:S(2)}, u32[]{:S(2)}) %collective-permute-start.27) | collective-permute-done | bytes 196640 | tf_op jit(solution)/shard_map/ppermute | solution.py:21
  177.1 1.8 select_convert_fusion
  (59 shorter events, 1.0 us)
Async XLA Ops:
  1.8 24.4 %collective-permute-start.10 = (bf16[2,24,4096]{2,1,0:T(8,128)(2,1)}, bf16[2,24,4096]{2,1,0:T(8,128)(2,1)}, u32[]{:S(2)}, u32[]{:S(2)}) collective-permute-start(bf16[2,24,4096]{2,1,0:T(8,128)(2,1)} %pad_maximum_fusion.2), channel_id=1, source_target_pairs={{0,1},{1,0},{2,3},{3,2},{4,5},{5,4},{6,7},{7,6},{8,9},{9,8},{10,11... | collective-permute-start | bytes 1179656 | tf_op jit(solution)/shard_map/ppermute | solution.py:21
  3.7 24.4 %collective-permute-start = (bf16[2,24,4096]{2,1,0:T(8,128)(2,1)}, bf16[2,24,4096]{2,1,0:T(8,128)(2,1)S(1)}, u32[]{:S(2)}, u32[]{:S(2)}) collective-permute-start(bf16[2,24,4096]{2,1,0:T(8,128)(2,1)} %pad_maximum_fusion.2), channel_id=1, source_target_pairs={{0,2},{1,23},{2,4},{3,1},{4,6},{5,3},{6,8},{7,5},{8,10},{9,7},{10,... | collective-permute-start | bytes 1179656 | tf_op jit(solution)/shard_map/ppermute | solution.py:21
  8.0 92.9 %collective-permute-start.6 = (bf16[344,4096]{1,0:T(8,128)(2,1)}, bf16[344,4096]{1,0:T(8,128)(2,1)S(1)}, u32[]{:S(2)}, u32[]{:S(2)}) collective-permute-start(bf16[344,4096]{1,0:T(8,128)(2,1)} %param.8), channel_id=1, source_target_pairs={{0,1},{1,0},{2,3},{3,2},{4,5},{5,4},{6,7},{7,6},{8,9},{9,8},{10,11... | collective-permute-start | bytes 8454152 | tf_op jit(solution)/shard_map/ppermute | solution.py:21
  20.5 5.0 %collective-permute-start.7 = (bf16[344]{0:T(512)(128)(2,1)}, bf16[344]{0:T(512)(128)(2,1)S(1)}, u32[]{:S(2)}, u32[]{:S(2)}) collective-permute-start(bf16[344]{0:T(512)(128)(2,1)} %param.9), channel_id=1, source_target_pairs={{0,1},{1,0},{2,3},{3,2},{4,5},{5,4},{6,7},{7,6},{8,9},{9,8},{10,11... | collective-permute-start | bytes 2072 | tf_op jit(solution)/shard_map/ppermute | solution.py:21
  22.4 79.2 %collective-permute-start.8 = (bf16[344,4096]{1,0:T(8,128)(2,1)}, bf16[344,4096]{1,0:T(8,128)(2,1)}, u32[]{:S(2)}, u32[]{:S(2)}) collective-permute-start(bf16[344,4096]{1,0:T(8,128)(2,1)} %param.10), channel_id=1, source_target_pairs={{0,1},{1,0},{2,3},{3,2},{4,5},{5,4},{6,7},{7,6},{8,9},{9,8},{10,11... | collective-permute-start | bytes 8454152 | tf_op jit(solution)/shard_map/ppermute | solution.py:21
  26.2 11.1 %collective-permute-start.11 = (bf16[2,24,4096]{2,1,0:T(8,128)(2,1)}, bf16[2,24,4096]{2,1,0:T(8,128)(2,1)S(1)}, u32[]{:S(2)}, u32[]{:S(2)}) collective-permute-start(bf16[2,24,4096]{2,1,0:T(8,128)(2,1)} %collective-permute-done.10), channel_id=1, source_target_pairs={{0,2},{1,23},{2,4},{3,1},{4,6},{5,3},{6,8},{7,5},{8,10},{9,7},{10,... | collective-permute-start | bytes 1179656 | tf_op jit(solution)/shard_map/ppermute | solution.py:21
  28.1 13.4 %collective-permute-start.1 = (bf16[2,24,4096]{2,1,0:T(8,128)(2,1)S(1)}, bf16[2,24,4096]{2,1,0:T(8,128)(2,1)S(1)}, u32[]{:S(2)}, u32[]{:S(2)}) collective-permute-start(bf16[2,24,4096]{2,1,0:T(8,128)(2,1)S(1)} %collective-permute-done), channel_id=1, source_target_pairs={{0,2},{1,23},{2,4},{3,1},{4,6},{5,3},{6,8},{7,5},{8,10},{9,7},{10,... | collective-permute-start | bytes 1179656 | tf_op jit(solution)/shard_map/ppermute | solution.py:21
  37.3 10.9 %collective-permute-start.12 = (bf16[2,24,4096]{2,1,0:T(8,128)(2,1)S(1)}, bf16[2,24,4096]{2,1,0:T(8,128)(2,1)S(1)}, u32[]{:S(2)}, u32[]{:S(2)}) collective-permute-start(bf16[2,24,4096]{2,1,0:T(8,128)(2,1)S(1)} %collective-permute-done.11), channel_id=1, source_target_pairs={{0,2},{1,23},{2,4},{3,1},{4,6},{5,3},{6,8},{7,5},{8,10},{9,7},{10,... | collective-permute-start | bytes 1179656 | tf_op jit(solution)/shard_map/ppermute | solution.py:21
  41.5 10.9 %collective-permute-start.2 = (bf16[2,24,4096]{2,1,0:T(8,128)(2,1)S(1)}, bf16[2,24,4096]{2,1,0:T(8,128)(2,1)S(1)}, u32[]{:S(2)}, u32[]{:S(2)}) collective-permute-start(bf16[2,24,4096]{2,1,0:T(8,128)(2,1)S(1)} %collective-permute-done.1), channel_id=1, source_target_pairs={{0,2},{1,23},{2,4},{3,1},{4,6},{5,3},{6,8},{7,5},{8,10},{9,7},{10,... | collective-permute-start | bytes 1179656 | tf_op jit(solution)/shard_map/ppermute | solution.py:21
  48.2 10.9 %collective-permute-start.13 = (bf16[2,24,4096]{2,1,0:T(8,128)(2,1)S(1)}, bf16[2,24,4096]{2,1,0:T(8,128)(2,1)S(1)}, u32[]{:S(2)}, u32[]{:S(2)}) collective-permute-start(bf16[2,24,4096]{2,1,0:T(8,128)(2,1)S(1)} %collective-permute-done.12), channel_id=1, source_target_pairs={{0,2},{1,23},{2,4},{3,1},{4,6},{5,3},{6,8},{7,5},{8,10},{9,7},{10,... | collective-permute-start | bytes 1179656 | tf_op jit(solution)/shard_map/ppermute | solution.py:21
  52.4 10.9 %collective-permute-start.3 = (bf16[2,24,4096]{2,1,0:T(8,128)(2,1)S(1)}, bf16[2,24,4096]{2,1,0:T(8,128)(2,1)S(1)}, u32[]{:S(2)}, u32[]{:S(2)}) collective-permute-start(bf16[2,24,4096]{2,1,0:T(8,128)(2,1)S(1)} %collective-permute-done.2), channel_id=1, source_target_pairs={{0,2},{1,23},{2,4},{3,1},{4,6},{5,3},{6,8},{7,5},{8,10},{9,7},{10,... | collective-permute-start | bytes 1179656 | tf_op jit(solution)/shard_map/ppermute | solution.py:21
  54.4 36.8 %copy-start.2 = (bf16[24,4096]{1,0:T(8,128)(2,1)S(1)}, bf16[24,4096]{1,0:T(8,128)(2,1)}, u32[]{:S(2)}) copy-start(bf16[24,4096]{1,0:T(8,128)(2,1)} %param.7) | copy-start | bytes 589828
  54.4 36.8 %copy-start.5 = (bf16[24,4096]{1,0:T(8,128)(2,1)S(1)}, bf16[24,4096]{1,0:T(8,128)(2,1)}, u32[]{:S(2)}) copy-start(bf16[24,4096]{1,0:T(8,128)(2,1)} %param.6) | copy-start | bytes 589828
  59.0 17.0 %collective-permute-start.14 = (bf16[2,24,4096]{2,1,0:T(8,128)(2,1)S(1)}, bf16[2,24,4096]{2,1,0:T(8,128)(2,1)S(1)}, u32[]{:S(2)}, u32[]{:S(2)}) collective-permute-start(bf16[2,24,4096]{2,1,0:T(8,128)(2,1)S(1)} %collective-permute-done.13), channel_id=1, source_target_pairs={{0,2},{1,23},{2,4},{3,1},{4,6},{5,3},{6,8},{7,5},{8,10},{9,7},{10,... | collective-permute-start | bytes 1179656 | tf_op jit(solution)/shard_map/ppermute | solution.py:21
  63.3 10.9 %collective-permute-start.4 = (bf16[2,24,4096]{2,1,0:T(8,128)(2,1)S(1)}, bf16[2,24,4096]{2,1,0:T(8,128)(2,1)S(1)}, u32[]{:S(2)}, u32[]{:S(2)}) collective-permute-start(bf16[2,24,4096]{2,1,0:T(8,128)(2,1)S(1)} %collective-permute-done.3), channel_id=1, source_target_pairs={{0,2},{1,23},{2,4},{3,1},{4,6},{5,3},{6,8},{7,5},{8,10},{9,7},{10,... | collective-permute-start | bytes 1179656 | tf_op jit(solution)/shard_map/ppermute | solution.py:21
  74.1 17.0 %collective-permute-start.5 = (bf16[2,24,4096]{2,1,0:T(8,128)(2,1)S(1)}, bf16[2,24,4096]{2,1,0:T(8,128)(2,1)S(1)}, u32[]{:S(2)}, u32[]{:S(2)}) collective-permute-start(bf16[2,24,4096]{2,1,0:T(8,128)(2,1)S(1)} %collective-permute-done.4), channel_id=1, source_target_pairs={{0,2},{2,4},{4,6},{6,8},{8,10},{10,12},{12,14},{14,16},{16,18},{18... | collective-permute-start | bytes 1179656 | tf_op jit(solution)/shard_map/ppermute | solution.py:21
  76.1 13.2 %collective-permute-start.20 = (bf16[2,24,4096]{2,1,0:T(8,128)(2,1)S(1)}, bf16[2,24,4096]{2,1,0:T(8,128)(2,1)S(1)}, u32[]{:S(2)}, u32[]{:S(2)}) collective-permute-start(bf16[2,24,4096]{2,1,0:T(8,128)(2,1)S(1)} %collective-permute-done.14), channel_id=1, source_target_pairs={{0,2},{1,23},{2,4},{3,1},{4,6},{5,3},{6,8},{7,5},{8,10},{9,7},{10,... | collective-permute-start | bytes 1179656 | tf_op jit(solution)/shard_map/ppermute | solution.py:21
  78.1 22.9 %copy-start.8 = (bf16[216,4096]{1,0:T(8,128)(2,1)}, bf16[216,4096]{1,0:T(8,128)(2,1)S(1)}, u32[]{:S(2)}) copy-start(bf16[216,4096]{1,0:T(8,128)(2,1)S(1)} %get-tuple-element.36) | copy-start | bytes 5308420
  78.1 22.8 %copy-start.10 = (bf16[216,4096]{1,0:T(8,128)(2,1)}, bf16[216,4096]{1,0:T(8,128)(2,1)S(1)}, u32[]{:S(2)}) copy-start(bf16[216,4096]{1,0:T(8,128)(2,1)S(1)} %get-tuple-element.37) | copy-start | bytes 5308420
  78.1 22.8 %copy-start = (bf16[344,4096]{1,0:T(8,128)(2,1)S(1)}, bf16[344,4096]{1,0:T(8,128)(2,1)}, u32[]{:S(2)}) copy-start(bf16[344,4096]{1,0:T(8,128)(2,1)} %param.8) | copy-start | bytes 8454148
  89.2 10.9 %collective-permute-start.21 = (bf16[2,24,4096]{2,1,0:T(8,128)(2,1)S(1)}, bf16[2,24,4096]{2,1,0:T(8,128)(2,1)S(1)}, u32[]{:S(2)}, u32[]{:S(2)}) collective-permute-start(bf16[2,24,4096]{2,1,0:T(8,128)(2,1)S(1)} %collective-permute-done.20), channel_id=1, source_target_pairs={{0,2},{2,4},{4,6},{6,8},{8,10},{10,12},{12,14},{14,16},{16,18},{18... | collective-permute-start | bytes 1179656 | tf_op jit(solution)/shard_map/ppermute | solution.py:21
  100.9 1.8 %copy-start.1 = (bf16[344,4096]{1,0:T(8,128)(2,1)S(1)}, bf16[344,4096]{1,0:T(8,128)(2,1)}, u32[]{:S(2)}) copy-start(bf16[344,4096]{1,0:T(8,128)(2,1)} %param.10) | copy-start | bytes 8454148
  101.6 3.5 %copy-start.6 = (bf16[24,4096]{1,0:T(8,128)(2,1)S(1)}, bf16[24,4096]{1,0:T(8,128)(2,1)}, u32[]{:S(2)}) copy-start(bf16[24,4096]{1,0:T(8,128)(2,1)} %get-tuple-element.56) | copy-start | bytes 589828
  101.6 3.5 %copy-start.7 = (bf16[24,4096]{1,0:T(8,128)(2,1)S(1)}, bf16[24,4096]{1,0:T(8,128)(2,1)}, u32[]{:S(2)}) copy-start(bf16[24,4096]{1,0:T(8,128)(2,1)} %get-tuple-element.58) | copy-start | bytes 589828
  105.1 1.8 copy-start.3
  105.1 1.8 copy-start.4
  108.6 4.6 %copy-start.9 = (bf16[216,4096]{1,0:T(8,128)(2,1)S(1)}, bf16[216,4096]{1,0:T(8,128)(2,1)}, u32[]{:S(2)}) copy-start(bf16[216,4096]{1,0:T(8,128)(2,1)} %copy-done.8) | copy-start | bytes 5308420
  109.8 23.8 %collective-permute-start.22 = (bf16[24,4096]{1,0:T(8,128)(2,1)S(1)}, bf16[24,4096]{1,0:T(8,128)(2,1)S(1)}, u32[]{:S(2)}, u32[]{:S(2)}) collective-permute-start(bf16[24,4096]{1,0:T(8,128)(2,1)S(1)} %get-tuple-element.21), channel_id=1, source_target_pairs={{2,0},{4,2},{6,4},{8,6},{10,8},{12,10},{14,12},{16,14},{18,16},{20... | collective-permute-start | bytes 589832 | tf_op jit(solution)/shard_map/ppermute | solution.py:21
  111.7 59.8 %collective-permute-start.28 = (bf16[24,4096]{1,0:T(8,128)(2,1)S(1)}, bf16[24,4096]{1,0:T(8,128)(2,1)}, u32[]{:S(2)}, u32[]{:S(2)}) collective-permute-start(bf16[24,4096]{1,0:T(8,128)(2,1)S(1)} %get-tuple-element.21), channel_id=1, source_target_pairs={{1,0},{3,2},{5,4},{7,6},{9,8},{11,10},{13,12},{15,14},{17,16},{19,... | collective-permute-start | bytes 589832 | tf_op jit(solution)/shard_map/ppermute | solution.py:21
  113.2 2.0 %copy-start.11 = (bf16[216,4096]{1,0:T(8,128)(2,1)S(1)}, bf16[216,4096]{1,0:T(8,128)(2,1)}, u32[]{:S(2)}) copy-start(bf16[216,4096]{1,0:T(8,128)(2,1)} %copy-done.10) | copy-start | bytes 5308420
  122.8 7.6 %collective-permute-start.9 = (bf16[24,4096]{1,0:T(8,128)(2,1)S(1)}, bf16[24,4096]{1,0:T(8,128)(2,1)S(1)}, u32[]{:S(2)}, u32[]{:S(2)}) collective-permute-start(bf16[24,4096]{1,0:T(8,128)(2,1)S(1)} %convolution_convert_fusion.2), channel_id=1, source_target_pairs={{2,0},{4,2},{6,4},{8,6},{10,8},{12,10},{14,12},{16,14},{18,16},{20... | collective-permute-start | bytes 589832 | tf_op jit(solution)/shard_map/ppermute | solution.py:21
  130.4 7.6 %collective-permute-start.15 = (bf16[24,4096]{1,0:T(8,128)(2,1)S(1)}, bf16[24,4096]{1,0:T(8,128)(2,1)S(1)}, u32[]{:S(2)}, u32[]{:S(2)}) collective-permute-start(bf16[24,4096]{1,0:T(8,128)(2,1)S(1)} %add_convert_fusion.10), channel_id=1, source_target_pairs={{2,0},{23,1},{4,2},{1,3},{6,4},{3,5},{8,6},{5,7},{10,8},{7,9},{12,... | collective-permute-start | bytes 589832 | tf_op jit(solution)/shard_map/ppermute | solution.py:21
  133.6 8.8 %collective-permute-start.23 = (bf16[24,4096]{1,0:T(8,128)(2,1)S(1)}, bf16[24,4096]{1,0:T(8,128)(2,1)S(1)}, u32[]{:S(2)}, u32[]{:S(2)}) collective-permute-start(bf16[24,4096]{1,0:T(8,128)(2,1)S(1)} %add_convert_fusion.5), channel_id=1, source_target_pairs={{2,0},{23,1},{4,2},{1,3},{6,4},{3,5},{8,6},{5,7},{10,8},{7,9},{12,... | collective-permute-start | bytes 589832 | tf_op jit(solution)/shard_map/ppermute | solution.py:21
  138.0 7.6 %collective-permute-start.16 = (bf16[24,4096]{1,0:T(8,128)(2,1)S(1)}, bf16[24,4096]{1,0:T(8,128)(2,1)S(1)}, u32[]{:S(2)}, u32[]{:S(2)}) collective-permute-start(bf16[24,4096]{1,0:T(8,128)(2,1)S(1)} %add_convert_fusion.9), channel_id=1, source_target_pairs={{2,0},{23,1},{4,2},{1,3},{6,4},{3,5},{8,6},{5,7},{10,8},{7,9},{12,... | collective-permute-start | bytes 589832 | tf_op jit(solution)/shard_map/ppermute | solution.py:21
  142.5 8.8 %collective-permute-start.24 = (bf16[24,4096]{1,0:T(8,128)(2,1)S(1)}, bf16[24,4096]{1,0:T(8,128)(2,1)S(1)}, u32[]{:S(2)}, u32[]{:S(2)}) collective-permute-start(bf16[24,4096]{1,0:T(8,128)(2,1)S(1)} %add_convert_fusion.4), channel_id=1, source_target_pairs={{2,0},{23,1},{4,2},{1,3},{6,4},{3,5},{8,6},{5,7},{10,8},{7,9},{12,... | collective-permute-start | bytes 589832 | tf_op jit(solution)/shard_map/ppermute | solution.py:21
  145.7 8.7 %collective-permute-start.17 = (bf16[24,4096]{1,0:T(8,128)(2,1)S(1)}, bf16[24,4096]{1,0:T(8,128)(2,1)S(1)}, u32[]{:S(2)}, u32[]{:S(2)}) collective-permute-start(bf16[24,4096]{1,0:T(8,128)(2,1)S(1)} %add_convert_fusion.8), channel_id=1, source_target_pairs={{2,0},{23,1},{4,2},{1,3},{6,4},{3,5},{8,6},{5,7},{10,8},{7,9},{12,... | collective-permute-start | bytes 589832 | tf_op jit(solution)/shard_map/ppermute | solution.py:21
  151.3 8.8 %collective-permute-start.25 = (bf16[24,4096]{1,0:T(8,128)(2,1)S(1)}, bf16[24,4096]{1,0:T(8,128)(2,1)S(1)}, u32[]{:S(2)}, u32[]{:S(2)}) collective-permute-start(bf16[24,4096]{1,0:T(8,128)(2,1)S(1)} %add_convert_fusion.3), channel_id=1, source_target_pairs={{2,0},{23,1},{4,2},{1,3},{6,4},{3,5},{8,6},{5,7},{10,8},{7,9},{12,... | collective-permute-start | bytes 589832 | tf_op jit(solution)/shard_map/ppermute | solution.py:21
  154.4 8.8 %collective-permute-start.18 = (bf16[24,4096]{1,0:T(8,128)(2,1)S(1)}, bf16[24,4096]{1,0:T(8,128)(2,1)S(1)}, u32[]{:S(2)}, u32[]{:S(2)}) collective-permute-start(bf16[24,4096]{1,0:T(8,128)(2,1)S(1)} %add_convert_fusion.7), channel_id=1, source_target_pairs={{2,0},{23,1},{4,2},{1,3},{6,4},{3,5},{8,6},{5,7},{10,8},{7,9},{12,... | collective-permute-start | bytes 589832 | tf_op jit(solution)/shard_map/ppermute | solution.py:21
  160.1 8.8 %collective-permute-start.26 = (bf16[24,4096]{1,0:T(8,128)(2,1)S(1)}, bf16[24,4096]{1,0:T(8,128)(2,1)S(1)}, u32[]{:S(2)}, u32[]{:S(2)}) collective-permute-start(bf16[24,4096]{1,0:T(8,128)(2,1)S(1)} %add_convert_fusion.2), channel_id=1, source_target_pairs={{2,0},{23,1},{4,2},{1,3},{6,4},{3,5},{8,6},{5,7},{10,8},{7,9},{12,... | collective-permute-start | bytes 589832 | tf_op jit(solution)/shard_map/ppermute | solution.py:21
  163.3 8.8 %collective-permute-start.19 = (bf16[24,4096]{1,0:T(8,128)(2,1)S(1)}, bf16[24,4096]{1,0:T(8,128)(2,1)S(1)}, u32[]{:S(2)}, u32[]{:S(2)}) collective-permute-start(bf16[24,4096]{1,0:T(8,128)(2,1)S(1)} %add_convert_fusion.6), channel_id=1, source_target_pairs={{2,0},{23,1},{4,2},{1,3},{6,4},{3,5},{8,6},{5,7},{10,8},{7,9},{12,... | collective-permute-start | bytes 589832 | tf_op jit(solution)/shard_map/ppermute | solution.py:21
  168.9 8.2 %collective-permute-start.27 = (bf16[24,4096]{1,0:T(8,128)(2,1)S(1)}, bf16[24,4096]{1,0:T(8,128)(2,1)S(1)}, u32[]{:S(2)}, u32[]{:S(2)}) collective-permute-start(bf16[24,4096]{1,0:T(8,128)(2,1)S(1)} %add_convert_fusion.1), channel_id=1, source_target_pairs={{2,1},{23,0},{4,3},{1,2},{6,5},{3,4},{8,7},{5,6},{10,9},{7,8},{12,... | collective-permute-start | bytes 589832 | tf_op jit(solution)/shard_map/ppermute | solution.py:21

commit v6 on v3

--- a/solution.py
+++ b/solution.py
@@ -35,10 +35,10 @@
     home = [(target, source) for source, target in out]
     out_far = [(source, target) for source, target in out if source % CORES == 0]
     home_far = [(target, source) for source, target in out_far]
+    home_cross = [(source, target ^ 1) for source, target in home]
     out_cross = [(source ^ 1, target) for source, target in out]
-    home_cross = [(target, source) for source, target in out_cross]
-    to_second = [(i, i + 1) for i in range(0, members, CORES)]
-    to_first = [(target, source) for source, target in to_second]
+    to_first = [(i + 1, i) for i in range(0, members, CORES)]
+    to_second = [(target, source) for source, target in to_first]
 
     mine = jnp.stack((kept_input, kept_grad), axis=0)
     other = hop(mine, to_second)
@@ -54,7 +54,10 @@
     def terms(pieces):
         inputs = jnp.concatenate([piece[0] for piece in pieces], axis=0)
         out_grads = jnp.concatenate([piece[1] for piece in pieces], axis=0)
-        preact = lax.dot_general(inputs, up, contract, preferred_element_type=jnp.float32) + bias
+        preact = lax.optimization_barrier(
+            lax.dot_general(inputs, up, contract, preferred_element_type=jnp.float32)
+            + bias
+        )
         down_grad = lax.dot_general(out_grads, down, contract, preferred_element_type=jnp.float32)
         pre_grad = (gelu_slope(preact) * down_grad).astype(jnp.bfloat16)
         pre_grad = lax.optimization_barrier(pre_grad)
@@ -72,13 +75,13 @@
     chain_other[steps] = jnp.where(core == 0, chain_other[steps], other)
 
     arrivals = [piece for pair in zip(chain_mine[1:steps], chain_other[1:steps]) for piece in pair]
-    near = terms(arrivals)
+    near = terms(arrivals[:-1])
     far_pieces, near = lax.optimization_barrier(
-        ([chain_mine[steps], chain_other[steps]], near)
+        ([arrivals[-1], chain_mine[steps], chain_other[steps]], near)
     )
     far = terms(far_pieces)
-    for_mine = near[0::2] + far[:1]
-    for_other = near[1::2] + far[1:]
+    for_mine = near[0::2] + far[1:2]
+    for_other = near[1::2] + far[0::2]
 
     def add(moved, part):
         return (moved.astype(jnp.float32) + part.astype(jnp.float32)).astype(jnp.bfloat16)

time: 167 us -> 168 us (level)
  the two profiles are of different devices: /device:TPU:46 before, /device:TPU:52 now
where the time goes in v6:
time: 168 us; the launch traced here: 167 us
  starting transfers between devices  89.2 us (53%)
  waiting for transfers between devices  54.3 us (32%)
  matrix products  12.1 us (7%)
  other arithmetic  7.63 us (5%)
  local copies, waits for them, and re-layouts  2.48 us (1%)
    ppermute x29, starting transfers between devices, hop(): return lax.ppermute(block, 'tensor', pairs)  89.2 us
    ppermute x29, waiting for transfers between devices, hop(): return lax.ppermute(block, 'tensor', pairs)  54.3 us
    dot_general x2, matrix products, terms(): lax.dot_general(out_grads, down, contract, preferred_element_type=jnp.flo...  4.84 us
    dot_general x2, matrix products, terms(): lax.dot_general(inputs, up, contract, preferred_element_type=jnp.float32)  4.58 us
    concatenate x3, other arithmetic, both(): return lax.optimization_barrier(jnp.concatenate([block, theirs], axis=0))  3.64 us
  transfers between devices with their start and end apart: 29, of which 13 were waited for; matrix products, arithmetic and copies ran while one was open for 4% of the time, Pallas kernels for 0%

profile of v6, /device:TPU:52, one launch (start us, length us, event | category | flops | bytes accessed | tf_op | source)
XLA Modules:
  0.0 167.1 jit_solution(17556578391276729738)
XLA Ops:
  0.0 1.8 %pad_maximum_fusion.2 = bf16[2,24,4096]{2,1,0:T(8,128)(2,1)} fusion(bf16[1,24,4096]{2,1,0:T(8,128)(2,1)} %bitcast.98, bf16[1,24,4096]{2,1,0:T(8,128)(2,1)} %bitcast.100), kind=kLoop, calls=%fused_computation.25 | loop fusion | flops 196608 | bytes 786432 | tf_op jit(solution)/shard_map/stack | solution.py:43
  1.8 4.3 %collective-permute-start.5 = (bf16[2,24,4096]{2,1,0:T(8,128)(2,1)}, bf16[2,24,4096]{2,1,0:T(8,128)(2,1)}, u32[]{:S(2)}, u32[]{:S(2)}) collective-permute-start(bf16[2,24,4096]{2,1,0:T(8,128)(2,1)} %pad_maximum_fusion.2), channel_id=1, source_target_pairs={{0,2},{1,23},{2,4},{3,1},{4,6},{5,3},{6,8},{7,5},{8,10},{9,7},{10,... | collective-permute-start | bytes 1179656 | tf_op jit(solution)/shard_map/ppermute | solution.py:21
  6.1 11.9 %collective-permute-start = (bf16[2,24,4096]{2,1,0:T(8,128)(2,1)}, bf16[2,24,4096]{2,1,0:T(8,128)(2,1)S(1)}, u32[]{:S(2)}, u32[]{:S(2)}) collective-permute-start(bf16[2,24,4096]{2,1,0:T(8,128)(2,1)} %pad_maximum_fusion.2), channel_id=1, source_target_pairs={{1,2},{0,23},{3,4},{2,1},{5,6},{4,3},{7,8},{6,5},{9,10},{8,7},{11,... | collective-permute-start | bytes 1179656 | tf_op jit(solution)/shard_map/ppermute | solution.py:21
  18.0 2.5 %collective-permute-start.12 = (bf16[2,24,4096]{2,1,0:T(8,128)(2,1)}, bf16[2,24,4096]{2,1,0:T(8,128)(2,1)}, u32[]{:S(2)}, u32[]{:S(2)}) collective-permute-start(bf16[2,24,4096]{2,1,0:T(8,128)(2,1)} %pad_maximum_fusion.2), channel_id=1, source_target_pairs={{0,1},{2,3},{4,5},{6,7},{8,9},{10,11},{12,13},{14,15},{16,17},{18,... | collective-permute-start | bytes 1179656 | tf_op jit(solution)/shard_map/ppermute | solution.py:21
  20.5 1.9 %collective-permute-start.13 = (bf16[344,4096]{1,0:T(8,128)(2,1)}, bf16[344,4096]{1,0:T(8,128)(2,1)S(1)}, u32[]{:S(2)}, u32[]{:S(2)}) collective-permute-start(bf16[344,4096]{1,0:T(8,128)(2,1)} %param.8), channel_id=1, source_target_pairs={{0,1},{1,0},{2,3},{3,2},{4,5},{5,4},{6,7},{7,6},{8,9},{9,8},{10,11... | collective-permute-start | bytes 8454152 | tf_op jit(solution)/shard_map/ppermute | solution.py:21
  22.5 2.4 %collective-permute-start.14 = (bf16[344]{0:T(512)(128)(2,1)}, bf16[344]{0:T(512)(128)(2,1)S(1)}, u32[]{:S(2)}, u32[]{:S(2)}) collective-permute-start(bf16[344]{0:T(512)(128)(2,1)} %param.9), channel_id=1, source_target_pairs={{0,1},{1,0},{2,3},{3,2},{4,5},{5,4},{6,7},{7,6},{8,9},{9,8},{10,11... | collective-permute-start | bytes 2072 | tf_op jit(solution)/shard_map/ppermute | solution.py:21
  24.9 2.9 %collective-permute-done.14 = bf16[344]{0:T(512)(128)(2,1)S(1)} collective-permute-done((bf16[344]{0:T(512)(128)(2,1)}, bf16[344]{0:T(512)(128)(2,1)S(1)}, u32[]{:S(2)}, u32[]{:S(2)}) %collective-permute-start.14) | collective-permute-done | bytes 720 | tf_op jit(solution)/shard_map/ppermute | solution.py:21
  27.8 2.0 %collective-permute-start.15 = (bf16[344,4096]{1,0:T(8,128)(2,1)}, bf16[344,4096]{1,0:T(8,128)(2,1)}, u32[]{:S(2)}, u32[]{:S(2)}) collective-permute-start(bf16[344,4096]{1,0:T(8,128)(2,1)} %param.10), channel_id=1, source_target_pairs={{0,1},{1,0},{2,3},{3,2},{4,5},{5,4},{6,7},{7,6},{8,9},{9,8},{10,11... | collective-permute-start | bytes 8454152 | tf_op jit(solution)/shard_map/ppermute | solution.py:21
  29.9 0.8 pad_maximum_fusion.3
  30.6 1.0 fusion.37
  31.7 2.9 %collective-permute-start.6 = (bf16[2,24,4096]{2,1,0:T(8,128)(2,1)}, bf16[2,24,4096]{2,1,0:T(8,128)(2,1)S(1)}, u32[]{:S(2)}, u32[]{:S(2)}) collective-permute-start(bf16[2,24,4096]{2,1,0:T(8,128)(2,1)} %collective-permute-done.5), channel_id=1, source_target_pairs={{0,2},{1,23},{2,4},{3,1},{4,6},{5,3},{6,8},{7,5},{8,10},{9,7},{10,... | collective-permute-start | bytes 1179656 | tf_op jit(solution)/shard_map/ppermute | solution.py:21
  34.6 1.9 %collective-permute-start.1 = (bf16[2,24,4096]{2,1,0:T(8,128)(2,1)S(1)}, bf16[2,24,4096]{2,1,0:T(8,128)(2,1)S(1)}, u32[]{:S(2)}, u32[]{:S(2)}) collective-permute-start(bf16[2,24,4096]{2,1,0:T(8,128)(2,1)S(1)} %collective-permute-done), channel_id=1, source_target_pairs={{0,2},{1,23},{2,4},{3,1},{4,6},{5,3},{6,8},{7,5},{8,10},{9,7},{10,... | collective-permute-start | bytes 1179656 | tf_op jit(solution)/shard_map/ppermute | solution.py:21
  36.6 6.2 %collective-permute-done.6 = bf16[2,24,4096]{2,1,0:T(8,128)(2,1)S(1)} collective-permute-done((bf16[2,24,4096]{2,1,0:T(8,128)(2,1)}, bf16[2,24,4096]{2,1,0:T(8,128)(2,1)S(1)}, u32[]{:S(2)}, u32[]{:S(2)}) %collective-permute-start.6) | collective-permute-done | bytes 393248 | tf_op jit(solution)/shard_map/ppermute | solution.py:21
  42.8 1.9 %collective-permute-start.7 = (bf16[2,24,4096]{2,1,0:T(8,128)(2,1)S(1)}, bf16[2,24,4096]{2,1,0:T(8,128)(2,1)S(1)}, u32[]{:S(2)}, u32[]{:S(2)}) collective-permute-start(bf16[2,24,4096]{2,1,0:T(8,128)(2,1)S(1)} %collective-permute-done.6), channel_id=1, source_target_pairs={{0,2},{1,23},{2,4},{3,1},{4,6},{5,3},{6,8},{7,5},{8,10},{9,7},{10,... | collective-permute-start | bytes 1179656 | tf_op jit(solution)/shard_map/ppermute | solution.py:21
  44.7 2.3 %collective-permute-done.1 = bf16[2,24,4096]{2,1,0:T(8,128)(2,1)S(1)} collective-permute-done((bf16[2,24,4096]{2,1,0:T(8,128)(2,1)S(1)}, bf16[2,24,4096]{2,1,0:T(8,128)(2,1)S(1)}, u32[]{:S(2)}, u32[]{:S(2)}) %collective-permute-start.1) | collective-permute-done | bytes 393248 | tf_op jit(solution)/shard_map/ppermute | solution.py:21
  47.0 1.9 %collective-permute-start.2 = (bf16[2,24,4096]{2,1,0:T(8,128)(2,1)S(1)}, bf16[2,24,4096]{2,1,0:T(8,128)(2,1)S(1)}, u32[]{:S(2)}, u32[]{:S(2)}) collective-permute-start(bf16[2,24,4096]{2,1,0:T(8,128)(2,1)S(1)} %collective-permute-done.1), channel_id=1, source_target_pairs={{0,2},{1,23},{2,4},{3,1},{4,6},{5,3},{6,8},{7,5},{8,10},{9,7},{10,... | collective-permute-start | bytes 1179656 | tf_op jit(solution)/shard_map/ppermute | solution.py:21
  49.0 4.7 %collective-permute-done.7 = bf16[2,24,4096]{2,1,0:T(8,128)(2,1)S(1)} collective-permute-done((bf16[2,24,4096]{2,1,0:T(8,128)(2,1)S(1)}, bf16[2,24,4096]{2,1,0:T(8,128)(2,1)S(1)}, u32[]{:S(2)}, u32[]{:S(2)}) %collective-permute-start.7) | collective-permute-done | bytes 393248 | tf_op jit(solution)/shard_map/ppermute | solution.py:21
  53.7 1.9 %collective-permute-start.8 = (bf16[2,24,4096]{2,1,0:T(8,128)(2,1)S(1)}, bf16[2,24,4096]{2,1,0:T(8,128)(2,1)S(1)}, u32[]{:S(2)}, u32[]{:S(2)}) collective-permute-start(bf16[2,24,4096]{2,1,0:T(8,128)(2,1)S(1)} %collective-permute-done.7), channel_id=1, source_target_pairs={{0,2},{1,23},{2,4},{3,1},{4,6},{5,3},{6,8},{7,5},{8,10},{9,7},{10,... | collective-permute-start | bytes 1179656 | tf_op jit(solution)/shard_map/ppermute | solution.py:21
  55.6 2.3 %collective-permute-done.2 = bf16[2,24,4096]{2,1,0:T(8,128)(2,1)S(1)} collective-permute-done((bf16[2,24,4096]{2,1,0:T(8,128)(2,1)S(1)}, bf16[2,24,4096]{2,1,0:T(8,128)(2,1)S(1)}, u32[]{:S(2)}, u32[]{:S(2)}) %collective-permute-start.2) | collective-permute-done | bytes 393248 | tf_op jit(solution)/shard_map/ppermute | solution.py:21
  57.9 1.9 %collective-permute-start.3 = (bf16[2,24,4096]{2,1,0:T(8,128)(2,1)S(1)}, bf16[2,24,4096]{2,1,0:T(8,128)(2,1)S(1)}, u32[]{:S(2)}, u32[]{:S(2)}) collective-permute-start(bf16[2,24,4096]{2,1,0:T(8,128)(2,1)S(1)} %collective-permute-done.2), channel_id=1, source_target_pairs={{0,2},{1,23},{2,4},{3,1},{4,6},{5,3},{6,8},{7,5},{8,10},{9,7},{10,... | collective-permute-start | bytes 1179656 | tf_op jit(solution)/shard_map/ppermute | solution.py:21
  59.8 0.0 copy-start.2
  59.9 4.6 %collective-permute-done.8 = bf16[2,24,4096]{2,1,0:T(8,128)(2,1)S(1)} collective-permute-done((bf16[2,24,4096]{2,1,0:T(8,128)(2,1)S(1)}, bf16[2,24,4096]{2,1,0:T(8,128)(2,1)S(1)}, u32[]{:S(2)}, u32[]{:S(2)}) %collective-permute-start.8) | collective-permute-done | bytes 393248 | tf_op jit(solution)/shard_map/ppermute | solution.py:21
  64.5 1.9 %collective-permute-start.9 = (bf16[2,24,4096]{2,1,0:T(8,128)(2,1)S(1)}, bf16[2,24,4096]{2,1,0:T(8,128)(2,1)S(1)}, u32[]{:S(2)}, u32[]{:S(2)}) collective-permute-start(bf16[2,24,4096]{2,1,0:T(8,128)(2,1)S(1)} %collective-permute-done.8), channel_id=1, source_target_pairs={{0,2},{1,23},{2,4},{3,1},{4,6},{5,3},{6,8},{7,5},{8,10},{9,7},{10,... | collective-permute-start | bytes 1179656 | tf_op jit(solution)/shard_map/ppermute | solution.py:21
  66.4 2.3 %collective-permute-done.3 = bf16[2,24,4096]{2,1,0:T(8,128)(2,1)S(1)} collective-permute-done((bf16[2,24,4096]{2,1,0:T(8,128)(2,1)S(1)}, bf16[2,24,4096]{2,1,0:T(8,128)(2,1)S(1)}, u32[]{:S(2)}, u32[]{:S(2)}) %collective-permute-start.3) | collective-permute-done | bytes 393248 | tf_op jit(solution)/shard_map/ppermute | solution.py:21
  68.7 1.9 %collective-permute-start.4 = (bf16[2,24,4096]{2,1,0:T(8,128)(2,1)S(1)}, bf16[2,24,4096]{2,1,0:T(8,128)(2,1)S(1)}, u32[]{:S(2)}, u32[]{:S(2)}) collective-permute-start(bf16[2,24,4096]{2,1,0:T(8,128)(2,1)S(1)} %collective-permute-done.3), channel_id=1, source_target_pairs={{0,2},{1,23},{2,4},{3,1},{4,6},{5,3},{6,8},{7,5},{8,10},{9,7},{10,... | collective-permute-start | bytes 1179656 | tf_op jit(solution)/shard_map/ppermute | solution.py:21
  70.7 0.0 copy-start
  70.7 8.9 %collective-permute-done.4 = bf16[2,24,4096]{2,1,0:T(8,128)(2,1)S(1)} collective-permute-done((bf16[2,24,4096]{2,1,0:T(8,128)(2,1)S(1)}, bf16[2,24,4096]{2,1,0:T(8,128)(2,1)S(1)}, u32[]{:S(2)}, u32[]{:S(2)}) %collective-permute-start.4) | collective-permute-done | bytes 393248 | tf_op jit(solution)/shard_map/ppermute | solution.py:21
  79.6 1.9 %collective-permute-start.11 = (bf16[2,24,4096]{2,1,0:T(8,128)(2,1)S(1)}, bf16[2,24,4096]{2,1,0:T(8,128)(2,1)S(1)}, u32[]{:S(2)}, u32[]{:S(2)}) collective-permute-start(bf16[2,24,4096]{2,1,0:T(8,128)(2,1)S(1)} %collective-permute-done.4), channel_id=1, source_target_pairs={{0,2},{2,4},{4,6},{6,8},{8,10},{10,12},{12,14},{14,16},{16,18},{18... | collective-permute-start | bytes 1179656 | tf_op jit(solution)/shard_map/ppermute | solution.py:21
  81.5 1.9 %collective-permute-start.10 = (bf16[2,24,4096]{2,1,0:T(8,128)(2,1)S(1)}, bf16[2,24,4096]{2,1,0:T(8,128)(2,1)S(1)}, u32[]{:S(2)}, u32[]{:S(2)}) collective-permute-start(bf16[2,24,4096]{2,1,0:T(8,128)(2,1)S(1)} %collective-permute-done.9), channel_id=1, source_target_pairs={{0,2},{2,4},{4,6},{6,8},{8,10},{10,12},{12,14},{14,16},{16,18},{18... | collective-permute-start | bytes 1179656 | tf_op jit(solution)/shard_map/ppermute | solution.py:21
  83.5 11.2 %collective-permute-done.10 = bf16[2,24,4096]{2,1,0:T(8,128)(2,1)S(1)} collective-permute-done((bf16[2,24,4096]{2,1,0:T(8,128)(2,1)S(1)}, bf16[2,24,4096]{2,1,0:T(8,128)(2,1)S(1)}, u32[]{:S(2)}, u32[]{:S(2)}) %collective-permute-start.10) | collective-permute-done | bytes 393248 | tf_op jit(solution)/shard_map/ppermute | solution.py:21
  94.7 0.1 broadcast_select_fusion.1
  94.8 0.8 broadcast_select_fusion
  95.6 0.6 pad_maximum_fusion
  96.2 0.0 copy-start.1
  96.2 2.8 %convolution_add_fusion = f32[216,688]{1,0:T(8,128)} fusion(bf16[216,4096]{1,0:T(8,128)(2,1)S(1)} %get-tuple-element.46, bf16[688,4096]{1,0:T(8,128)(2,1)S(1)} %pad_maximum_fusion, f32[688]{0:T(1024)S(1)} %convert_element_type.132), kind=kOutput, calls=%fused_computation.5 | convolution fusion | flops 1217545344 | bytes 8002752 | tf_op jit(solution)/shard_map/dot_general | solution.py:58
  99.0 2.3 %pad_maximum_fusion.1 = bf16[688,4096]{1,0:T(8,128)(2,1)S(1)} fusion(bf16[344,4096]{1,0:T(8,128)(2,1)} %collective-permute-done.15, bf16[344,4096]{1,0:T(8,128)(2,1)S(1)} %copy-done.1), kind=kLoop, calls=%fused_computation.1 | loop fusion | flops 11272192 | bytes 11272192 | tf_op jit(solution)/shard_map/concatenate | solution.py:48
  101.3 0.0 copy-done.8
  101.3 3.0 %fusion = bf16[216,688]{1,0:T(8,128)(2,1)S(1)} fusion(bf16[216,4096]{1,0:T(8,128)(2,1)S(1)} %copy-done.8, bf16[688,4096]{1,0:T(8,128)(2,1)S(1)} %pad_maximum_fusion.1, f32[216,688]{1,0:T(8,128)} %convolution_add_fusion), kind=kOutput, calls=%fused_computation.6 | convolution fusion | flops 1218882816 | bytes 8297216 | tf_op jit(solution)/shard_map/dot_general | solution.py:61
  104.3 1.6 convolution_convert_fusion
  106.0 0.2 fusion.40
  106.2 0.8 copy-done.6
  107.0 0.1 copy-done.3
  107.1 0.1 slice_bitcast_fusion.21
  107.1 1.8 %convolution_add_fusion.1 = f32[72,688]{1,0:T(8,128)S(1)} fusion(bf16[688,4096]{1,0:T(8,128)(2,1)S(1)} %pad_maximum_fusion, bf16[24,4096]{1,0:T(8,128)(2,1)S(1)} %get-tuple-element.44, bf16[24,4096]{1,0:T(8,128)(2,1)S(1)} %get-tuple-element.65, bf16[24,4096]{1,0:T(8,128)(2,1)S(1)} %get-tuple-element.40, f32[688]{0:T(1024)S(1)} %convert_element_type.132), kind=kOutput, calls=%fused_computation.8 | convolution fusion | flops 407617920 | bytes 6426816 | tf_op jit(solution)/shard_map/dot_general | solution.py:58
  108.9 1.8 %fusion.1 = bf16[72,688]{1,0:T(8,128)(2,1)S(1)} fusion(bf16[688,4096]{1,0:T(8,128)(2,1)S(1)} %pad_maximum_fusion.1, bf16[24,4096]{1,0:T(8,128)(2,1)S(1)} %get-tuple-element.45, bf16[24,4096]{1,0:T(8,128)(2,1)S(1)} %get-tuple-element.64, bf16[24,4096]{1,0:T(8,128)(2,1)S(1)} %get-tuple-element.41, f32[72,688]{1,0:T(8,128)S(1)} %convolution_add_fusion.1), kind=kOutput, calls=%fused_computation.9 | convolution fusion | flops 408063744 | bytes 6523136 | tf_op jit(solution)/shard_map/dot_general | solution.py:61
  110.8 1.1 convolution_convert_fusion.1
  111.9 1.9 %collective-permute-start.16 = (bf16[24,4096]{1,0:T(8,128)(2,1)S(1)}, bf16[24,4096]{1,0:T(8,128)(2,1)S(1)}, u32[]{:S(2)}, u32[]{:S(2)}) collective-permute-start(bf16[24,4096]{1,0:T(8,128)(2,1)S(1)} %get-tuple-element.38), channel_id=1, source_target_pairs={{2,0},{4,2},{6,4},{8,6},{10,8},{12,10},{14,12},{16,14},{18,16},{20... | collective-permute-start | bytes 589832 | tf_op jit(solution)/shard_map/ppermute | solution.py:21
  113.9 1.9 %collective-permute-start.22 = (bf16[24,4096]{1,0:T(8,128)(2,1)S(1)}, bf16[24,4096]{1,0:T(8,128)(2,1)S(1)}, u32[]{:S(2)}, u32[]{:S(2)}) collective-permute-start(bf16[24,4096]{1,0:T(8,128)(2,1)S(1)} %get-tuple-element.39), channel_id=1, source_target_pairs={{2,0},{4,2},{6,4},{8,6},{10,8},{12,10},{14,12},{16,14},{18,16},{20... | collective-permute-start | bytes 589832 | tf_op jit(solution)/shard_map/ppermute | solution.py:21
  115.8 1.3 collective-permute-start.28
  117.1 2.4 %collective-permute-done.16 = bf16[24,4096]{1,0:T(8,128)(2,1)S(1)} collective-permute-done((bf16[24,4096]{1,0:T(8,128)(2,1)S(1)}, bf16[24,4096]{1,0:T(8,128)(2,1)S(1)}, u32[]{:S(2)}, u32[]{:S(2)}) %collective-permute-start.16) | collective-permute-done | bytes 196640 | tf_op jit(solution)/shard_map/ppermute | solution.py:21
  119.5 3.1 %collective-permute-start.17 = (bf16[24,4096]{1,0:T(8,128)(2,1)S(1)}, bf16[24,4096]{1,0:T(8,128)(2,1)S(1)}, u32[]{:S(2)}, u32[]{:S(2)}) collective-permute-start(bf16[24,4096]{1,0:T(8,128)(2,1)S(1)} %add_convert_fusion.10), channel_id=1, source_target_pairs={{2,0},{23,1},{4,2},{1,3},{6,4},{3,5},{8,6},{5,7},{10,8},{7,9},{12,... | collective-permute-start | bytes 589832 | tf_op jit(solution)/shard_map/ppermute | solution.py:21
  122.7 3.4 %collective-permute-start.23 = (bf16[24,4096]{1,0:T(8,128)(2,1)S(1)}, bf16[24,4096]{1,0:T(8,128)(2,1)S(1)}, u32[]{:S(2)}, u32[]{:S(2)}) collective-permute-start(bf16[24,4096]{1,0:T(8,128)(2,1)S(1)} %add_convert_fusion.5), channel_id=1, source_target_pairs={{2,0},{23,1},{4,2},{1,3},{6,4},{3,5},{8,6},{5,7},{10,8},{7,9},{12,... | collective-permute-start | bytes 589832 | tf_op jit(solution)/shard_map/ppermute | solution.py:21
  126.2 0.9 collective-permute-done.17
  127.2 4.3 %collective-permute-start.18 = (bf16[24,4096]{1,0:T(8,128)(2,1)S(1)}, bf16[24,4096]{1,0:T(8,128)(2,1)S(1)}, u32[]{:S(2)}, u32[]{:S(2)}) collective-permute-start(bf16[24,4096]{1,0:T(8,128)(2,1)S(1)} %add_convert_fusion.9), channel_id=1, source_target_pairs={{2,0},{23,1},{4,2},{1,3},{6,4},{3,5},{8,6},{5,7},{10,8},{7,9},{12,... | collective-permute-start | bytes 589832 | tf_op jit(solution)/shard_map/ppermute | solution.py:21
  131.6 3.4 %collective-permute-start.24 = (bf16[24,4096]{1,0:T(8,128)(2,1)S(1)}, bf16[24,4096]{1,0:T(8,128)(2,1)S(1)}, u32[]{:S(2)}, u32[]{:S(2)}) collective-permute-start(bf16[24,4096]{1,0:T(8,128)(2,1)S(1)} %add_convert_fusion.4), channel_id=1, source_target_pairs={{2,0},{23,1},{4,2},{1,3},{6,4},{3,5},{8,6},{5,7},{10,8},{7,9},{12,... | collective-permute-start | bytes 589832 | tf_op jit(solution)/shard_map/ppermute | solution.py:21
  135.1 5.3 %collective-permute-start.19 = (bf16[24,4096]{1,0:T(8,128)(2,1)S(1)}, bf16[24,4096]{1,0:T(8,128)(2,1)S(1)}, u32[]{:S(2)}, u32[]{:S(2)}) collective-permute-start(bf16[24,4096]{1,0:T(8,128)(2,1)S(1)} %add_convert_fusion.8), channel_id=1, source_target_pairs={{2,0},{23,1},{4,2},{1,3},{6,4},{3,5},{8,6},{5,7},{10,8},{7,9},{12,... | collective-permute-start | bytes 589832 | tf_op jit(solution)/shard_map/ppermute | solution.py:21
  140.4 3.4 %collective-permute-start.25 = (bf16[24,4096]{1,0:T(8,128)(2,1)S(1)}, bf16[24,4096]{1,0:T(8,128)(2,1)S(1)}, u32[]{:S(2)}, u32[]{:S(2)}) collective-permute-start(bf16[24,4096]{1,0:T(8,128)(2,1)S(1)} %add_convert_fusion.3), channel_id=1, source_target_pairs={{2,0},{23,1},{4,2},{1,3},{6,4},{3,5},{8,6},{5,7},{10,8},{7,9},{12,... | collective-permute-start | bytes 589832 | tf_op jit(solution)/shard_map/ppermute | solution.py:21
  143.9 5.3 %collective-permute-start.20 = (bf16[24,4096]{1,0:T(8,128)(2,1)S(1)}, bf16[24,4096]{1,0:T(8,128)(2,1)S(1)}, u32[]{:S(2)}, u32[]{:S(2)}) collective-permute-start(bf16[24,4096]{1,0:T(8,128)(2,1)S(1)} %add_convert_fusion.7), channel_id=1, source_target_pairs={{2,0},{23,1},{4,2},{1,3},{6,4},{3,5},{8,6},{5,7},{10,8},{7,9},{12,... | collective-permute-start | bytes 589832 | tf_op jit(solution)/shard_map/ppermute | solution.py:21
  149.2 3.4 %collective-permute-start.26 = (bf16[24,4096]{1,0:T(8,128)(2,1)S(1)}, bf16[24,4096]{1,0:T(8,128)(2,1)S(1)}, u32[]{:S(2)}, u32[]{:S(2)}) collective-permute-start(bf16[24,4096]{1,0:T(8,128)(2,1)S(1)} %add_convert_fusion.2), channel_id=1, source_target_pairs={{2,0},{23,1},{4,2},{1,3},{6,4},{3,5},{8,6},{5,7},{10,8},{7,9},{12,... | collective-permute-start | bytes 589832 | tf_op jit(solution)/shard_map/ppermute | solution.py:21
  152.7 5.3 %collective-permute-start.21 = (bf16[24,4096]{1,0:T(8,128)(2,1)S(1)}, bf16[24,4096]{1,0:T(8,128)(2,1)S(1)}, u32[]{:S(2)}, u32[]{:S(2)}) collective-permute-start(bf16[24,4096]{1,0:T(8,128)(2,1)S(1)} %add_convert_fusion.6), channel_id=1, source_target_pairs={{2,0},{23,1},{4,2},{1,3},{6,4},{3,5},{8,6},{5,7},{10,8},{7,9},{12,... | collective-permute-start | bytes 589832 | tf_op jit(solution)/shard_map/ppermute | solution.py:21
  158.1 1.9 %collective-permute-start.27 = (bf16[24,4096]{1,0:T(8,128)(2,1)S(1)}, bf16[24,4096]{1,0:T(8,128)(2,1)S(1)}, u32[]{:S(2)}, u32[]{:S(2)}) collective-permute-start(bf16[24,4096]{1,0:T(8,128)(2,1)S(1)} %add_convert_fusion.1), channel_id=1, source_target_pairs={{2,1},{23,0},{4,3},{1,2},{6,5},{3,4},{8,7},{5,6},{10,9},{7,8},{12,... | collective-permute-start | bytes 589832 | tf_op jit(solution)/shard_map/ppermute | solution.py:21
  160.7 0.5 collective-permute-done.21
  161.2 5.1 %collective-permute-done.27 = bf16[24,4096]{1,0:T(8,128)(2,1)S(1)} collective-permute-done((bf16[24,4096]{1,0:T(8,128)(2,1)S(1)}, bf16[24,4096]{1,0:T(8,128)(2,1)S(1)}, u32[]{:S(2)}, u32[]{:S(2)}) %collective-permute-start.27) | collective-permute-done | bytes 196640 | tf_op jit(solution)/shard_map/ppermute | solution.py:21
  166.3 0.8 select_convert_fusion
  (50 shorter events, 0.9 us)
Async XLA Ops:
  1.8 28.8 %collective-permute-start.5 = (bf16[2,24,4096]{2,1,0:T(8,128)(2,1)}, bf16[2,24,4096]{2,1,0:T(8,128)(2,1)}, u32[]{:S(2)}, u32[]{:S(2)}) collective-permute-start(bf16[2,24,4096]{2,1,0:T(8,128)(2,1)} %pad_maximum_fusion.2), channel_id=1, source_target_pairs={{0,2},{1,23},{2,4},{3,1},{4,6},{5,3},{6,8},{7,5},{8,10},{9,7},{10,... | collective-permute-start | bytes 1179656 | tf_op jit(solution)/shard_map/ppermute | solution.py:21
  6.1 28.5 %collective-permute-start = (bf16[2,24,4096]{2,1,0:T(8,128)(2,1)}, bf16[2,24,4096]{2,1,0:T(8,128)(2,1)S(1)}, u32[]{:S(2)}, u32[]{:S(2)}) collective-permute-start(bf16[2,24,4096]{2,1,0:T(8,128)(2,1)} %pad_maximum_fusion.2), channel_id=1, source_target_pairs={{1,2},{0,23},{3,4},{2,1},{5,6},{4,3},{7,8},{6,5},{9,10},{8,7},{11,... | collective-permute-start | bytes 1179656 | tf_op jit(solution)/shard_map/ppermute | solution.py:21
  18.0 76.7 %collective-permute-start.12 = (bf16[2,24,4096]{2,1,0:T(8,128)(2,1)}, bf16[2,24,4096]{2,1,0:T(8,128)(2,1)}, u32[]{:S(2)}, u32[]{:S(2)}) collective-permute-start(bf16[2,24,4096]{2,1,0:T(8,128)(2,1)} %pad_maximum_fusion.2), channel_id=1, source_target_pairs={{0,1},{2,3},{4,5},{6,7},{8,9},{10,11},{12,13},{14,15},{16,17},{18,... | collective-permute-start | bytes 1179656 | tf_op jit(solution)/shard_map/ppermute | solution.py:21
  20.5 75.0 %collective-permute-start.13 = (bf16[344,4096]{1,0:T(8,128)(2,1)}, bf16[344,4096]{1,0:T(8,128)(2,1)S(1)}, u32[]{:S(2)}, u32[]{:S(2)}) collective-permute-start(bf16[344,4096]{1,0:T(8,128)(2,1)} %param.8), channel_id=1, source_target_pairs={{0,1},{1,0},{2,3},{3,2},{4,5},{5,4},{6,7},{7,6},{8,9},{9,8},{10,11... | collective-permute-start | bytes 8454152 | tf_op jit(solution)/shard_map/ppermute | solution.py:21
  22.5 5.4 %collective-permute-start.14 = (bf16[344]{0:T(512)(128)(2,1)}, bf16[344]{0:T(512)(128)(2,1)S(1)}, u32[]{:S(2)}, u32[]{:S(2)}) collective-permute-start(bf16[344]{0:T(512)(128)(2,1)} %param.9), channel_id=1, source_target_pairs={{0,1},{1,0},{2,3},{3,2},{4,5},{5,4},{6,7},{7,6},{8,9},{9,8},{10,11... | collective-permute-start | bytes 2072 | tf_op jit(solution)/shard_map/ppermute | solution.py:21
  27.8 71.2 %collective-permute-start.15 = (bf16[344,4096]{1,0:T(8,128)(2,1)}, bf16[344,4096]{1,0:T(8,128)(2,1)}, u32[]{:S(2)}, u32[]{:S(2)}) collective-permute-start(bf16[344,4096]{1,0:T(8,128)(2,1)} %param.10), channel_id=1, source_target_pairs={{0,1},{1,0},{2,3},{3,2},{4,5},{5,4},{6,7},{7,6},{8,9},{9,8},{10,11... | collective-permute-start | bytes 8454152 | tf_op jit(solution)/shard_map/ppermute | solution.py:21
  31.7 11.1 %collective-permute-start.6 = (bf16[2,24,4096]{2,1,0:T(8,128)(2,1)}, bf16[2,24,4096]{2,1,0:T(8,128)(2,1)S(1)}, u32[]{:S(2)}, u32[]{:S(2)}) collective-permute-start(bf16[2,24,4096]{2,1,0:T(8,128)(2,1)} %collective-permute-done.5), channel_id=1, source_target_pairs={{0,2},{1,23},{2,4},{3,1},{4,6},{5,3},{6,8},{7,5},{8,10},{9,7},{10,... | collective-permute-start | bytes 1179656 | tf_op jit(solution)/shard_map/ppermute | solution.py:21
  34.6 12.4 %collective-permute-start.1 = (bf16[2,24,4096]{2,1,0:T(8,128)(2,1)S(1)}, bf16[2,24,4096]{2,1,0:T(8,128)(2,1)S(1)}, u32[]{:S(2)}, u32[]{:S(2)}) collective-permute-start(bf16[2,24,4096]{2,1,0:T(8,128)(2,1)S(1)} %collective-permute-done), channel_id=1, source_target_pairs={{0,2},{1,23},{2,4},{3,1},{4,6},{5,3},{6,8},{7,5},{8,10},{9,7},{10,... | collective-permute-start | bytes 1179656 | tf_op jit(solution)/shard_map/ppermute | solution.py:21
  42.8 10.9 %collective-permute-start.7 = (bf16[2,24,4096]{2,1,0:T(8,128)(2,1)S(1)}, bf16[2,24,4096]{2,1,0:T(8,128)(2,1)S(1)}, u32[]{:S(2)}, u32[]{:S(2)}) collective-permute-start(bf16[2,24,4096]{2,1,0:T(8,128)(2,1)S(1)} %collective-permute-done.6), channel_id=1, source_target_pairs={{0,2},{1,23},{2,4},{3,1},{4,6},{5,3},{6,8},{7,5},{8,10},{9,7},{10,... | collective-permute-start | bytes 1179656 | tf_op jit(solution)/shard_map/ppermute | solution.py:21
  47.0 10.9 %collective-permute-start.2 = (bf16[2,24,4096]{2,1,0:T(8,128)(2,1)S(1)}, bf16[2,24,4096]{2,1,0:T(8,128)(2,1)S(1)}, u32[]{:S(2)}, u32[]{:S(2)}) collective-permute-start(bf16[2,24,4096]{2,1,0:T(8,128)(2,1)S(1)} %collective-permute-done.1), channel_id=1, source_target_pairs={{0,2},{1,23},{2,4},{3,1},{4,6},{5,3},{6,8},{7,5},{8,10},{9,7},{10,... | collective-permute-start | bytes 1179656 | tf_op jit(solution)/shard_map/ppermute | solution.py:21
  53.7 10.9 %collective-permute-start.8 = (bf16[2,24,4096]{2,1,0:T(8,128)(2,1)S(1)}, bf16[2,24,4096]{2,1,0:T(8,128)(2,1)S(1)}, u32[]{:S(2)}, u32[]{:S(2)}) collective-permute-start(bf16[2,24,4096]{2,1,0:T(8,128)(2,1)S(1)} %collective-permute-done.7), channel_id=1, source_target_pairs={{0,2},{1,23},{2,4},{3,1},{4,6},{5,3},{6,8},{7,5},{8,10},{9,7},{10,... | collective-permute-start | bytes 1179656 | tf_op jit(solution)/shard_map/ppermute | solution.py:21
  57.9 10.9 %collective-permute-start.3 = (bf16[2,24,4096]{2,1,0:T(8,128)(2,1)S(1)}, bf16[2,24,4096]{2,1,0:T(8,128)(2,1)S(1)}, u32[]{:S(2)}, u32[]{:S(2)}) collective-permute-start(bf16[2,24,4096]{2,1,0:T(8,128)(2,1)S(1)} %collective-permute-done.2), channel_id=1, source_target_pairs={{0,2},{1,23},{2,4},{3,1},{4,6},{5,3},{6,8},{7,5},{8,10},{9,7},{10,... | collective-permute-start | bytes 1179656 | tf_op jit(solution)/shard_map/ppermute | solution.py:21
  59.8 34.9 %copy-start.2 = (bf16[24,4096]{1,0:T(8,128)(2,1)S(1)}, bf16[24,4096]{1,0:T(8,128)(2,1)}, u32[]{:S(2)}) copy-start(bf16[24,4096]{1,0:T(8,128)(2,1)} %param.7) | copy-start | bytes 589828
  59.8 34.9 %copy-start.4 = (bf16[24,4096]{1,0:T(8,128)(2,1)S(1)}, bf16[24,4096]{1,0:T(8,128)(2,1)}, u32[]{:S(2)}) copy-start(bf16[24,4096]{1,0:T(8,128)(2,1)} %param.6) | copy-start | bytes 589828
  64.5 17.0 %collective-permute-start.9 = (bf16[2,24,4096]{2,1,0:T(8,128)(2,1)S(1)}, bf16[2,24,4096]{2,1,0:T(8,128)(2,1)S(1)}, u32[]{:S(2)}, u32[]{:S(2)}) collective-permute-start(bf16[2,24,4096]{2,1,0:T(8,128)(2,1)S(1)} %collective-permute-done.8), channel_id=1, source_target_pairs={{0,2},{1,23},{2,4},{3,1},{4,6},{5,3},{6,8},{7,5},{8,10},{9,7},{10,... | collective-permute-start | bytes 1179656 | tf_op jit(solution)/shard_map/ppermute | solution.py:21
  68.7 10.9 %collective-permute-start.4 = (bf16[2,24,4096]{2,1,0:T(8,128)(2,1)S(1)}, bf16[2,24,4096]{2,1,0:T(8,128)(2,1)S(1)}, u32[]{:S(2)}, u32[]{:S(2)}) collective-permute-start(bf16[2,24,4096]{2,1,0:T(8,128)(2,1)S(1)} %collective-permute-done.3), channel_id=1, source_target_pairs={{0,2},{1,23},{2,4},{3,1},{4,6},{5,3},{6,8},{7,5},{8,10},{9,7},{10,... | collective-permute-start | bytes 1179656 | tf_op jit(solution)/shard_map/ppermute | solution.py:21
  70.7 24.9 %copy-start = (bf16[344,4096]{1,0:T(8,128)(2,1)S(1)}, bf16[344,4096]{1,0:T(8,128)(2,1)}, u32[]{:S(2)}) copy-start(bf16[344,4096]{1,0:T(8,128)(2,1)} %param.8) | copy-start | bytes 8454148
  79.6 16.6 %copy-start.5 = (bf16[2,24,4096]{2,1,0:T(8,128)(2,1)}, bf16[2,24,4096]{2,1,0:T(8,128)(2,1)S(1)}, u32[]{:S(2)}) copy-start(bf16[2,24,4096]{2,1,0:T(8,128)(2,1)S(1)} %collective-permute-done.4) | copy-start | bytes 1179652
  79.6 15.2 %collective-permute-start.11 = (bf16[2,24,4096]{2,1,0:T(8,128)(2,1)S(1)}, bf16[2,24,4096]{2,1,0:T(8,128)(2,1)S(1)}, u32[]{:S(2)}, u32[]{:S(2)}) collective-permute-start(bf16[2,24,4096]{2,1,0:T(8,128)(2,1)S(1)} %collective-permute-done.4), channel_id=1, source_target_pairs={{0,2},{2,4},{4,6},{6,8},{8,10},{10,12},{12,14},{14,16},{16,18},{18... | collective-permute-start | bytes 1179656 | tf_op jit(solution)/shard_map/ppermute | solution.py:21
  81.5 13.2 %collective-permute-start.10 = (bf16[2,24,4096]{2,1,0:T(8,128)(2,1)S(1)}, bf16[2,24,4096]{2,1,0:T(8,128)(2,1)S(1)}, u32[]{:S(2)}, u32[]{:S(2)}) collective-permute-start(bf16[2,24,4096]{2,1,0:T(8,128)(2,1)S(1)} %collective-permute-done.9), channel_id=1, source_target_pairs={{0,2},{2,4},{4,6},{6,8},{8,10},{10,12},{12,14},{14,16},{16,18},{18... | collective-permute-start | bytes 1179656 | tf_op jit(solution)/shard_map/ppermute | solution.py:21
  83.5 12.1 %copy-start.7 = (bf16[216,4096]{1,0:T(8,128)(2,1)}, bf16[216,4096]{1,0:T(8,128)(2,1)S(1)}, u32[]{:S(2)}) copy-start(bf16[216,4096]{1,0:T(8,128)(2,1)S(1)} %get-tuple-element.47) | copy-start | bytes 5308420
  96.2 2.8 %copy-start.1 = (bf16[344,4096]{1,0:T(8,128)(2,1)S(1)}, bf16[344,4096]{1,0:T(8,128)(2,1)}, u32[]{:S(2)}) copy-start(bf16[344,4096]{1,0:T(8,128)(2,1)} %param.10) | copy-start | bytes 8454148
  99.0 2.3 %copy-start.8 = (bf16[216,4096]{1,0:T(8,128)(2,1)S(1)}, bf16[216,4096]{1,0:T(8,128)(2,1)}, u32[]{:S(2)}) copy-start(bf16[216,4096]{1,0:T(8,128)(2,1)} %copy-done.7) | copy-start | bytes 5308420
  105.9 1.0 copy-start.6
  106.0 1.1 copy-start.3
  111.9 7.6 %collective-permute-start.16 = (bf16[24,4096]{1,0:T(8,128)(2,1)S(1)}, bf16[24,4096]{1,0:T(8,128)(2,1)S(1)}, u32[]{:S(2)}, u32[]{:S(2)}) collective-permute-start(bf16[24,4096]{1,0:T(8,128)(2,1)S(1)} %get-tuple-element.38), channel_id=1, source_target_pairs={{2,0},{4,2},{6,4},{8,6},{10,8},{12,10},{14,12},{16,14},{18,16},{20... | collective-permute-start | bytes 589832 | tf_op jit(solution)/shard_map/ppermute | solution.py:21
  113.9 8.8 %collective-permute-start.22 = (bf16[24,4096]{1,0:T(8,128)(2,1)S(1)}, bf16[24,4096]{1,0:T(8,128)(2,1)S(1)}, u32[]{:S(2)}, u32[]{:S(2)}) collective-permute-start(bf16[24,4096]{1,0:T(8,128)(2,1)S(1)} %get-tuple-element.39), channel_id=1, source_target_pairs={{2,0},{4,2},{6,4},{8,6},{10,8},{12,10},{14,12},{16,14},{18,16},{20... | collective-permute-start | bytes 589832 | tf_op jit(solution)/shard_map/ppermute | solution.py:21
  115.8 44.9 %collective-permute-start.28 = (bf16[24,4096]{1,0:T(8,128)(2,1)S(1)}, bf16[24,4096]{1,0:T(8,128)(2,1)S(1)}, u32[]{:S(2)}, u32[]{:S(2)}) collective-permute-start(bf16[24,4096]{1,0:T(8,128)(2,1)S(1)} %get-tuple-element.39), channel_id=1, source_target_pairs={{1,0},{3,2},{5,4},{7,6},{9,8},{11,10},{13,12},{15,14},{17,16},{19,... | collective-permute-start | bytes 589832 | tf_op jit(solution)/shard_map/ppermute | solution.py:21
  119.5 7.6 %collective-permute-start.17 = (bf16[24,4096]{1,0:T(8,128)(2,1)S(1)}, bf16[24,4096]{1,0:T(8,128)(2,1)S(1)}, u32[]{:S(2)}, u32[]{:S(2)}) collective-permute-start(bf16[24,4096]{1,0:T(8,128)(2,1)S(1)} %add_convert_fusion.10), channel_id=1, source_target_pairs={{2,0},{23,1},{4,2},{1,3},{6,4},{3,5},{8,6},{5,7},{10,8},{7,9},{12,... | collective-permute-start | bytes 589832 | tf_op jit(solution)/shard_map/ppermute | solution.py:21
  122.7 8.8 %collective-permute-start.23 = (bf16[24,4096]{1,0:T(8,128)(2,1)S(1)}, bf16[24,4096]{1,0:T(8,128)(2,1)S(1)}, u32[]{:S(2)}, u32[]{:S(2)}) collective-permute-start(bf16[24,4096]{1,0:T(8,128)(2,1)S(1)} %add_convert_fusion.5), channel_id=1, source_target_pairs={{2,0},{23,1},{4,2},{1,3},{6,4},{3,5},{8,6},{5,7},{10,8},{7,9},{12,... | collective-permute-start | bytes 589832 | tf_op jit(solution)/shard_map/ppermute | solution.py:21
  127.2 7.8 %collective-permute-start.18 = (bf16[24,4096]{1,0:T(8,128)(2,1)S(1)}, bf16[24,4096]{1,0:T(8,128)(2,1)S(1)}, u32[]{:S(2)}, u32[]{:S(2)}) collective-permute-start(bf16[24,4096]{1,0:T(8,128)(2,1)S(1)} %add_convert_fusion.9), channel_id=1, source_target_pairs={{2,0},{23,1},{4,2},{1,3},{6,4},{3,5},{8,6},{5,7},{10,8},{7,9},{12,... | collective-permute-start | bytes 589832 | tf_op jit(solution)/shard_map/ppermute | solution.py:21
  131.6 8.8 %collective-permute-start.24 = (bf16[24,4096]{1,0:T(8,128)(2,1)S(1)}, bf16[24,4096]{1,0:T(8,128)(2,1)S(1)}, u32[]{:S(2)}, u32[]{:S(2)}) collective-permute-start(bf16[24,4096]{1,0:T(8,128)(2,1)S(1)} %add_convert_fusion.4), channel_id=1, source_target_pairs={{2,0},{23,1},{4,2},{1,3},{6,4},{3,5},{8,6},{5,7},{10,8},{7,9},{12,... | collective-permute-start | bytes 589832 | tf_op jit(solution)/shard_map/ppermute | solution.py:21
  135.1 8.8 %collective-permute-start.19 = (bf16[24,4096]{1,0:T(8,128)(2,1)S(1)}, bf16[24,4096]{1,0:T(8,128)(2,1)S(1)}, u32[]{:S(2)}, u32[]{:S(2)}) collective-permute-start(bf16[24,4096]{1,0:T(8,128)(2,1)S(1)} %add_convert_fusion.8), channel_id=1, source_target_pairs={{2,0},{23,1},{4,2},{1,3},{6,4},{3,5},{8,6},{5,7},{10,8},{7,9},{12,... | collective-permute-start | bytes 589832 | tf_op jit(solution)/shard_map/ppermute | solution.py:21
  140.4 8.8 %collective-permute-start.25 = (bf16[24,4096]{1,0:T(8,128)(2,1)S(1)}, bf16[24,4096]{1,0:T(8,128)(2,1)S(1)}, u32[]{:S(2)}, u32[]{:S(2)}) collective-permute-start(bf16[24,4096]{1,0:T(8,128)(2,1)S(1)} %add_convert_fusion.3), channel_id=1, source_target_pairs={{2,0},{23,1},{4,2},{1,3},{6,4},{3,5},{8,6},{5,7},{10,8},{7,9},{12,... | collective-permute-start | bytes 589832 | tf_op jit(solution)/shard_map/ppermute | solution.py:21
  143.9 8.8 %collective-permute-start.20 = (bf16[24,4096]{1,0:T(8,128)(2,1)S(1)}, bf16[24,4096]{1,0:T(8,128)(2,1)S(1)}, u32[]{:S(2)}, u32[]{:S(2)}) collective-permute-start(bf16[24,4096]{1,0:T(8,128)(2,1)S(1)} %add_convert_fusion.7), channel_id=1, source_target_pairs={{2,0},{23,1},{4,2},{1,3},{6,4},{3,5},{8,6},{5,7},{10,8},{7,9},{12,... | collective-permute-start | bytes 589832 | tf_op jit(solution)/shard_map/ppermute | solution.py:21
  149.2 8.8 %collective-permute-start.26 = (bf16[24,4096]{1,0:T(8,128)(2,1)S(1)}, bf16[24,4096]{1,0:T(8,128)(2,1)S(1)}, u32[]{:S(2)}, u32[]{:S(2)}) collective-permute-start(bf16[24,4096]{1,0:T(8,128)(2,1)S(1)} %add_convert_fusion.2), channel_id=1, source_target_pairs={{2,0},{23,1},{4,2},{1,3},{6,4},{3,5},{8,6},{5,7},{10,8},{7,9},{12,... | collective-permute-start | bytes 589832 | tf_op jit(solution)/shard_map/ppermute | solution.py:21
  152.7 8.4 %collective-permute-start.21 = (bf16[24,4096]{1,0:T(8,128)(2,1)S(1)}, bf16[24,4096]{1,0:T(8,128)(2,1)S(1)}, u32[]{:S(2)}, u32[]{:S(2)}) collective-permute-start(bf16[24,4096]{1,0:T(8,128)(2,1)S(1)} %add_convert_fusion.6), channel_id=1, source_target_pairs={{2,0},{23,1},{4,2},{1,3},{6,4},{3,5},{8,6},{5,7},{10,8},{7,9},{12,... | collective-permute-start | bytes 589832 | tf_op jit(solution)/shard_map/ppermute | solution.py:21
  158.1 8.2 %collective-permute-start.27 = (bf16[24,4096]{1,0:T(8,128)(2,1)S(1)}, bf16[24,4096]{1,0:T(8,128)(2,1)S(1)}, u32[]{:S(2)}, u32[]{:S(2)}) collective-permute-start(bf16[24,4096]{1,0:T(8,128)(2,1)S(1)} %add_convert_fusion.1), channel_id=1, source_target_pairs={{2,1},{23,0},{4,3},{1,2},{6,5},{3,4},{8,7},{5,6},{10,9},{7,8},{12,... | collective-permute-start | bytes 589832 | tf_op jit(solution)/shard_map/ppermute | solution.py:21

commit v7 on v6

--- a/solution.py
+++ b/solution.py
@@ -36,12 +36,10 @@
     out_far = [(source, target) for source, target in out if source % CORES == 0]
     home_far = [(target, source) for source, target in out_far]
     home_cross = [(source, target ^ 1) for source, target in home]
-    out_cross = [(source ^ 1, target) for source, target in out]
     to_first = [(i + 1, i) for i in range(0, members, CORES)]
-    to_second = [(target, source) for source, target in to_first]
 
     mine = jnp.stack((kept_input, kept_grad), axis=0)
-    other = hop(mine, to_second)
+    other = hop(mine, sibling)
 
     def both(block):
         theirs = hop(block, sibling)
@@ -65,12 +63,11 @@
         partials = partials.astype(jnp.bfloat16)
         return [partials[i * slots : (i + 1) * slots] for i in range(len(pieces))]
 
-    chain_mine, chain_other = [mine], [mine]
+    chain_mine, chain_other = [mine], [other]
     for step in range(1, steps + 1):
         pairs = out if step < steps else out_far
         chain_mine.append(hop(chain_mine[-1], pairs))
-        crossing = out_cross if step == 1 else pairs
-        chain_other.append(hop(chain_other[-1], crossing))
+        chain_other.append(hop(chain_other[-1], pairs))
     chain_mine[steps] = jnp.where(core == 0, chain_mine[steps], mine)
     chain_other[steps] = jnp.where(core == 0, chain_other[steps], other)
 

time: 168 us -> 163 us (0.970)
  the two profiles are of different devices: /device:TPU:52 before, /device:TPU:56 now
where the time goes in v7:
time: 163 us; the launch traced here: 162 us
  starting transfers between devices  83.4 us (51%)
  waiting for transfers between devices  58.1 us (36%)
  matrix products  10.2 us (6%)
  other arithmetic  7.9 us (5%)
    ppermute x29, starting transfers between devices, hop(): return lax.ppermute(block, 'tensor', pairs)  83.4 us
    ppermute x29, waiting for transfers between devices, hop(): return lax.ppermute(block, 'tensor', pairs)  58.1 us
    concatenate x3, other arithmetic, both(): return lax.optimization_barrier(jnp.concatenate([block, theirs], axis=0))  3.9 us
    dot_general x2, matrix products, terms(): lax.dot_general(out_grads, down, contract, preferred_element_type=jnp.flo...  3.75 us
    dot_general x2, matrix products, terms(): lax.dot_general(inputs, up, contract, preferred_element_type=jnp.float32)  3.72 us
  transfers between devices with their start and end apart: 29, of which 19 were waited for; matrix products, arithmetic and copies ran while one was open for 3% of the time, Pallas kernels for 0%

profile of v7, /device:TPU:56, one launch (start us, length us, event | category | flops | bytes accessed | tf_op | source)
XLA Modules:
  0.0 162.3 jit_solution(11063729770922940011)
XLA Ops:
  0.0 1.8 %pad_maximum_fusion.2 = bf16[2,24,4096]{2,1,0:T(8,128)(2,1)} fusion(bf16[1,24,4096]{2,1,0:T(8,128)(2,1)} %bitcast.98, bf16[1,24,4096]{2,1,0:T(8,128)(2,1)} %bitcast.100), kind=kLoop, calls=%fused_computation.25 | loop fusion | flops 196608 | bytes 786432 | tf_op jit(solution)/shard_map/stack | solution.py:41
  1.8 1.9 %collective-permute-start = (bf16[2,24,4096]{2,1,0:T(8,128)(2,1)}, bf16[2,24,4096]{2,1,0:T(8,128)(2,1)}, u32[]{:S(2)}, u32[]{:S(2)}) collective-permute-start(bf16[2,24,4096]{2,1,0:T(8,128)(2,1)} %pad_maximum_fusion.2), channel_id=1, source_target_pairs={{0,1},{1,0},{2,3},{3,2},{4,5},{5,4},{6,7},{7,6},{8,9},{9,8},{10,11... | collective-permute-start | bytes 1179656 | tf_op jit(solution)/shard_map/ppermute | solution.py:21
  3.7 4.3 %collective-permute-start.6 = (bf16[2,24,4096]{2,1,0:T(8,128)(2,1)}, bf16[2,24,4096]{2,1,0:T(8,128)(2,1)S(1)}, u32[]{:S(2)}, u32[]{:S(2)}) collective-permute-start(bf16[2,24,4096]{2,1,0:T(8,128)(2,1)} %pad_maximum_fusion.2), channel_id=1, source_target_pairs={{0,2},{1,23},{2,4},{3,1},{4,6},{5,3},{6,8},{7,5},{8,10},{9,7},{10,... | collective-permute-start | bytes 1179656 | tf_op jit(solution)/shard_map/ppermute | solution.py:21
  8.0 12.4 %collective-permute-start.13 = (bf16[344,4096]{1,0:T(8,128)(2,1)}, bf16[344,4096]{1,0:T(8,128)(2,1)S(1)}, u32[]{:S(2)}, u32[]{:S(2)}) collective-permute-start(bf16[344,4096]{1,0:T(8,128)(2,1)} %param.8), channel_id=1, source_target_pairs={{0,1},{1,0},{2,3},{3,2},{4,5},{5,4},{6,7},{7,6},{8,9},{9,8},{10,11... | collective-permute-start | bytes 8454152 | tf_op jit(solution)/shard_map/ppermute | solution.py:21
  20.5 1.9 %collective-permute-start.14 = (bf16[344]{0:T(512)(128)(2,1)}, bf16[344]{0:T(512)(128)(2,1)S(1)}, u32[]{:S(2)}, u32[]{:S(2)}) collective-permute-start(bf16[344]{0:T(512)(128)(2,1)} %param.9), channel_id=1, source_target_pairs={{0,1},{1,0},{2,3},{3,2},{4,5},{5,4},{6,7},{7,6},{8,9},{9,8},{10,11... | collective-permute-start | bytes 2072 | tf_op jit(solution)/shard_map/ppermute | solution.py:21
  22.4 2.4 %collective-permute-start.15 = (bf16[344,4096]{1,0:T(8,128)(2,1)}, bf16[344,4096]{1,0:T(8,128)(2,1)}, u32[]{:S(2)}, u32[]{:S(2)}) collective-permute-start(bf16[344,4096]{1,0:T(8,128)(2,1)} %param.10), channel_id=1, source_target_pairs={{0,1},{1,0},{2,3},{3,2},{4,5},{5,4},{6,7},{7,6},{8,9},{9,8},{10,11... | collective-permute-start | bytes 8454152 | tf_op jit(solution)/shard_map/ppermute | solution.py:21
  24.8 0.6 collective-permute-done.14
  25.5 0.8 pad_maximum_fusion.3
  26.2 1.9 %collective-permute-start.1 = (bf16[2,24,4096]{2,1,0:T(8,128)(2,1)}, bf16[2,24,4096]{2,1,0:T(8,128)(2,1)S(1)}, u32[]{:S(2)}, u32[]{:S(2)}) collective-permute-start(bf16[2,24,4096]{2,1,0:T(8,128)(2,1)} %collective-permute-done), channel_id=1, source_target_pairs={{0,2},{1,23},{2,4},{3,1},{4,6},{5,3},{6,8},{7,5},{8,10},{9,7},{10,... | collective-permute-start | bytes 1179656 | tf_op jit(solution)/shard_map/ppermute | solution.py:21
  28.2 1.9 %collective-permute-start.7 = (bf16[2,24,4096]{2,1,0:T(8,128)(2,1)S(1)}, bf16[2,24,4096]{2,1,0:T(8,128)(2,1)S(1)}, u32[]{:S(2)}, u32[]{:S(2)}) collective-permute-start(bf16[2,24,4096]{2,1,0:T(8,128)(2,1)S(1)} %collective-permute-done.6), channel_id=1, source_target_pairs={{0,2},{1,23},{2,4},{3,1},{4,6},{5,3},{6,8},{7,5},{8,10},{9,7},{10,... | collective-permute-start | bytes 1179656 | tf_op jit(solution)/shard_map/ppermute | solution.py:21
  30.1 7.2 %collective-permute-done.1 = bf16[2,24,4096]{2,1,0:T(8,128)(2,1)S(1)} collective-permute-done((bf16[2,24,4096]{2,1,0:T(8,128)(2,1)}, bf16[2,24,4096]{2,1,0:T(8,128)(2,1)S(1)}, u32[]{:S(2)}, u32[]{:S(2)}) %collective-permute-start.1) | collective-permute-done | bytes 393248 | tf_op jit(solution)/shard_map/ppermute | solution.py:21
  37.3 1.9 %collective-permute-start.2 = (bf16[2,24,4096]{2,1,0:T(8,128)(2,1)S(1)}, bf16[2,24,4096]{2,1,0:T(8,128)(2,1)S(1)}, u32[]{:S(2)}, u32[]{:S(2)}) collective-permute-start(bf16[2,24,4096]{2,1,0:T(8,128)(2,1)S(1)} %collective-permute-done.1), channel_id=1, source_target_pairs={{0,2},{1,23},{2,4},{3,1},{4,6},{5,3},{6,8},{7,5},{8,10},{9,7},{10,... | collective-permute-start | bytes 1179656 | tf_op jit(solution)/shard_map/ppermute | solution.py:21
  39.2 2.3 %collective-permute-done.7 = bf16[2,24,4096]{2,1,0:T(8,128)(2,1)S(1)} collective-permute-done((bf16[2,24,4096]{2,1,0:T(8,128)(2,1)S(1)}, bf16[2,24,4096]{2,1,0:T(8,128)(2,1)S(1)}, u32[]{:S(2)}, u32[]{:S(2)}) %collective-permute-start.7) | collective-permute-done | bytes 393248 | tf_op jit(solution)/shard_map/ppermute | solution.py:21
  41.5 1.9 %collective-permute-start.8 = (bf16[2,24,4096]{2,1,0:T(8,128)(2,1)S(1)}, bf16[2,24,4096]{2,1,0:T(8,128)(2,1)S(1)}, u32[]{:S(2)}, u32[]{:S(2)}) collective-permute-start(bf16[2,24,4096]{2,1,0:T(8,128)(2,1)S(1)} %collective-permute-done.7), channel_id=1, source_target_pairs={{0,2},{1,23},{2,4},{3,1},{4,6},{5,3},{6,8},{7,5},{8,10},{9,7},{10,... | collective-permute-start | bytes 1179656 | tf_op jit(solution)/shard_map/ppermute | solution.py:21
  43.5 4.7 %collective-permute-done.2 = bf16[2,24,4096]{2,1,0:T(8,128)(2,1)S(1)} collective-permute-done((bf16[2,24,4096]{2,1,0:T(8,128)(2,1)S(1)}, bf16[2,24,4096]{2,1,0:T(8,128)(2,1)S(1)}, u32[]{:S(2)}, u32[]{:S(2)}) %collective-permute-start.2) | collective-permute-done | bytes 393248 | tf_op jit(solution)/shard_map/ppermute | solution.py:21
  48.2 1.9 %collective-permute-start.3 = (bf16[2,24,4096]{2,1,0:T(8,128)(2,1)S(1)}, bf16[2,24,4096]{2,1,0:T(8,128)(2,1)S(1)}, u32[]{:S(2)}, u32[]{:S(2)}) collective-permute-start(bf16[2,24,4096]{2,1,0:T(8,128)(2,1)S(1)} %collective-permute-done.2), channel_id=1, source_target_pairs={{0,2},{1,23},{2,4},{3,1},{4,6},{5,3},{6,8},{7,5},{8,10},{9,7},{10,... | collective-permute-start | bytes 1179656 | tf_op jit(solution)/shard_map/ppermute | solution.py:21
  50.1 2.3 %collective-permute-done.8 = bf16[2,24,4096]{2,1,0:T(8,128)(2,1)S(1)} collective-permute-done((bf16[2,24,4096]{2,1,0:T(8,128)(2,1)S(1)}, bf16[2,24,4096]{2,1,0:T(8,128)(2,1)S(1)}, u32[]{:S(2)}, u32[]{:S(2)}) %collective-permute-start.8) | collective-permute-done | bytes 393248 | tf_op jit(solution)/shard_map/ppermute | solution.py:21
  52.4 1.9 %collective-permute-start.9 = (bf16[2,24,4096]{2,1,0:T(8,128)(2,1)S(1)}, bf16[2,24,4096]{2,1,0:T(8,128)(2,1)S(1)}, u32[]{:S(2)}, u32[]{:S(2)}) collective-permute-start(bf16[2,24,4096]{2,1,0:T(8,128)(2,1)S(1)} %collective-permute-done.8), channel_id=1, source_target_pairs={{0,2},{1,23},{2,4},{3,1},{4,6},{5,3},{6,8},{7,5},{8,10},{9,7},{10,... | collective-permute-start | bytes 1179656 | tf_op jit(solution)/shard_map/ppermute | solution.py:21
  54.4 4.6 %collective-permute-done.3 = bf16[2,24,4096]{2,1,0:T(8,128)(2,1)S(1)} collective-permute-done((bf16[2,24,4096]{2,1,0:T(8,128)(2,1)S(1)}, bf16[2,24,4096]{2,1,0:T(8,128)(2,1)S(1)}, u32[]{:S(2)}, u32[]{:S(2)}) %collective-permute-start.3) | collective-permute-done | bytes 393248 | tf_op jit(solution)/shard_map/ppermute | solution.py:21
  59.1 1.9 %collective-permute-start.4 = (bf16[2,24,4096]{2,1,0:T(8,128)(2,1)S(1)}, bf16[2,24,4096]{2,1,0:T(8,128)(2,1)S(1)}, u32[]{:S(2)}, u32[]{:S(2)}) collective-permute-start(bf16[2,24,4096]{2,1,0:T(8,128)(2,1)S(1)} %collective-permute-done.3), channel_id=1, source_target_pairs={{0,2},{1,23},{2,4},{3,1},{4,6},{5,3},{6,8},{7,5},{8,10},{9,7},{10,... | collective-permute-start | bytes 1179656 | tf_op jit(solution)/shard_map/ppermute | solution.py:21
  61.0 2.3 %collective-permute-done.9 = bf16[2,24,4096]{2,1,0:T(8,128)(2,1)S(1)} collective-permute-done((bf16[2,24,4096]{2,1,0:T(8,128)(2,1)S(1)}, bf16[2,24,4096]{2,1,0:T(8,128)(2,1)S(1)}, u32[]{:S(2)}, u32[]{:S(2)}) %collective-permute-start.9) | collective-permute-done | bytes 393248 | tf_op jit(solution)/shard_map/ppermute | solution.py:21
  63.3 1.9 %collective-permute-start.10 = (bf16[2,24,4096]{2,1,0:T(8,128)(2,1)S(1)}, bf16[2,24,4096]{2,1,0:T(8,128)(2,1)S(1)}, u32[]{:S(2)}, u32[]{:S(2)}) collective-permute-start(bf16[2,24,4096]{2,1,0:T(8,128)(2,1)S(1)} %collective-permute-done.9), channel_id=1, source_target_pairs={{0,2},{1,23},{2,4},{3,1},{4,6},{5,3},{6,8},{7,5},{8,10},{9,7},{10,... | collective-permute-start | bytes 1179656 | tf_op jit(solution)/shard_map/ppermute | solution.py:21
  65.3 4.7 %collective-permute-done.4 = bf16[2,24,4096]{2,1,0:T(8,128)(2,1)S(1)} collective-permute-done((bf16[2,24,4096]{2,1,0:T(8,128)(2,1)S(1)}, bf16[2,24,4096]{2,1,0:T(8,128)(2,1)S(1)}, u32[]{:S(2)}, u32[]{:S(2)}) %collective-permute-start.4) | collective-permute-done | bytes 393248 | tf_op jit(solution)/shard_map/ppermute | solution.py:21
  69.9 1.9 %collective-permute-start.5 = (bf16[2,24,4096]{2,1,0:T(8,128)(2,1)S(1)}, bf16[2,24,4096]{2,1,0:T(8,128)(2,1)S(1)}, u32[]{:S(2)}, u32[]{:S(2)}) collective-permute-start(bf16[2,24,4096]{2,1,0:T(8,128)(2,1)S(1)} %collective-permute-done.4), channel_id=1, source_target_pairs={{0,2},{1,23},{2,4},{3,1},{4,6},{5,3},{6,8},{7,5},{8,10},{9,7},{10,... | collective-permute-start | bytes 1179656 | tf_op jit(solution)/shard_map/ppermute | solution.py:21
  71.8 2.3 %collective-permute-done.10 = bf16[2,24,4096]{2,1,0:T(8,128)(2,1)S(1)} collective-permute-done((bf16[2,24,4096]{2,1,0:T(8,128)(2,1)S(1)}, bf16[2,24,4096]{2,1,0:T(8,128)(2,1)S(1)}, u32[]{:S(2)}, u32[]{:S(2)}) %collective-permute-start.10) | collective-permute-done | bytes 393248 | tf_op jit(solution)/shard_map/ppermute | solution.py:21
  74.1 1.9 %collective-permute-start.11 = (bf16[2,24,4096]{2,1,0:T(8,128)(2,1)S(1)}, bf16[2,24,4096]{2,1,0:T(8,128)(2,1)S(1)}, u32[]{:S(2)}, u32[]{:S(2)}) collective-permute-start(bf16[2,24,4096]{2,1,0:T(8,128)(2,1)S(1)} %collective-permute-done.10), channel_id=1, source_target_pairs={{0,2},{2,4},{4,6},{6,8},{8,10},{10,12},{12,14},{14,16},{16,18},{18... | collective-permute-start | bytes 1179656 | tf_op jit(solution)/shard_map/ppermute | solution.py:21
  76.1 4.6 %collective-permute-done.5 = bf16[2,24,4096]{2,1,0:T(8,128)(2,1)S(1)} collective-permute-done((bf16[2,24,4096]{2,1,0:T(8,128)(2,1)S(1)}, bf16[2,24,4096]{2,1,0:T(8,128)(2,1)S(1)}, u32[]{:S(2)}, u32[]{:S(2)}) %collective-permute-start.5) | collective-permute-done | bytes 393248 | tf_op jit(solution)/shard_map/ppermute | solution.py:21
  80.8 1.9 %collective-permute-start.12 = (bf16[2,24,4096]{2,1,0:T(8,128)(2,1)S(1)}, bf16[2,24,4096]{2,1,0:T(8,128)(2,1)S(1)}, u32[]{:S(2)}, u32[]{:S(2)}) collective-permute-start(bf16[2,24,4096]{2,1,0:T(8,128)(2,1)S(1)} %collective-permute-done.5), channel_id=1, source_target_pairs={{0,2},{2,4},{4,6},{6,8},{8,10},{10,12},{12,14},{14,16},{16,18},{18... | collective-permute-start | bytes 1179656 | tf_op jit(solution)/shard_map/ppermute | solution.py:21
  82.7 2.3 %collective-permute-done.11 = bf16[2,24,4096]{2,1,0:T(8,128)(2,1)S(1)} collective-permute-done((bf16[2,24,4096]{2,1,0:T(8,128)(2,1)S(1)}, bf16[2,24,4096]{2,1,0:T(8,128)(2,1)S(1)}, u32[]{:S(2)}, u32[]{:S(2)}) %collective-permute-start.11) | collective-permute-done | bytes 393248 | tf_op jit(solution)/shard_map/ppermute | solution.py:21
  85.0 0.1 broadcast_select_fusion.1
  85.1 6.6 %collective-permute-done.12 = bf16[2,24,4096]{2,1,0:T(8,128)(2,1)S(1)} collective-permute-done((bf16[2,24,4096]{2,1,0:T(8,128)(2,1)S(1)}, bf16[2,24,4096]{2,1,0:T(8,128)(2,1)S(1)}, u32[]{:S(2)}, u32[]{:S(2)}) %collective-permute-start.12) | collective-permute-done | bytes 393248 | tf_op jit(solution)/shard_map/ppermute | solution.py:21
  91.7 0.8 broadcast_select_fusion
  92.5 0.7 pad_maximum_fusion
  93.2 1.9 %convolution_add_fusion = f32[216,688]{1,0:T(8,128)S(1)} fusion(bf16[216,4096]{1,0:T(8,128)(2,1)S(1)} %get-tuple-element.46, bf16[688,4096]{1,0:T(8,128)(2,1)S(1)} %pad_maximum_fusion, f32[688]{0:T(1024)S(1)} %convert_element_type.132), kind=kOutput, calls=%fused_computation.5 | convolution fusion | flops 1217545344 | bytes 8002752 | tf_op jit(solution)/shard_map/dot_general | solution.py:56
  95.1 2.5 %pad_maximum_fusion.1 = bf16[688,4096]{1,0:T(8,128)(2,1)S(1)} fusion(bf16[344,4096]{1,0:T(8,128)(2,1)} %collective-permute-done.15, bf16[344,4096]{1,0:T(8,128)(2,1)S(1)} %copy-done.1), kind=kLoop, calls=%fused_computation.1 | loop fusion | flops 11272192 | bytes 11272192 | tf_op jit(solution)/shard_map/concatenate | solution.py:46
  97.6 1.9 %fusion = bf16[216,688]{1,0:T(8,128)(2,1)S(1)} fusion(bf16[216,4096]{1,0:T(8,128)(2,1)S(1)} %copy-done.8, bf16[688,4096]{1,0:T(8,128)(2,1)S(1)} %pad_maximum_fusion.1, f32[216,688]{1,0:T(8,128)S(1)} %convolution_add_fusion), kind=kOutput, calls=%fused_computation.6 | convolution fusion | flops 1218882816 | bytes 8297216 | tf_op jit(solution)/shard_map/dot_general | solution.py:59
  99.6 1.6 convolution_convert_fusion
  101.2 0.1 fusion.40
  101.3 0.9 copy-done.6
  102.2 0.1 copy-done.3
  102.4 1.8 %convolution_add_fusion.1 = f32[72,688]{1,0:T(8,128)S(1)} fusion(bf16[688,4096]{1,0:T(8,128)(2,1)S(1)} %pad_maximum_fusion, bf16[24,4096]{1,0:T(8,128)(2,1)S(1)} %get-tuple-element.44, bf16[24,4096]{1,0:T(8,128)(2,1)S(1)} %get-tuple-element.65, bf16[24,4096]{1,0:T(8,128)(2,1)S(1)} %get-tuple-element.40, f32[688]{0:T(1024)S(1)} %convert_element_type.132), kind=kOutput, calls=%fused_computation.8 | convolution fusion | flops 407617920 | bytes 6426816 | tf_op jit(solution)/shard_map/dot_general | solution.py:56
  104.2 1.8 %fusion.1 = bf16[72,688]{1,0:T(8,128)(2,1)S(1)} fusion(bf16[688,4096]{1,0:T(8,128)(2,1)S(1)} %pad_maximum_fusion.1, bf16[24,4096]{1,0:T(8,128)(2,1)S(1)} %get-tuple-element.45, bf16[24,4096]{1,0:T(8,128)(2,1)S(1)} %get-tuple-element.64, bf16[24,4096]{1,0:T(8,128)(2,1)S(1)} %get-tuple-element.41, f32[72,688]{1,0:T(8,128)S(1)} %convolution_add_fusion.1), kind=kOutput, calls=%fused_computation.9 | convolution fusion | flops 408063744 | bytes 6523136 | tf_op jit(solution)/shard_map/dot_general | solution.py:59
  106.0 1.1 convolution_convert_fusion.1
  107.2 1.9 %collective-permute-start.16 = (bf16[24,4096]{1,0:T(8,128)(2,1)S(1)}, bf16[24,4096]{1,0:T(8,128)(2,1)S(1)}, u32[]{:S(2)}, u32[]{:S(2)}) collective-permute-start(bf16[24,4096]{1,0:T(8,128)(2,1)S(1)} %get-tuple-element.38), channel_id=1, source_target_pairs={{2,0},{4,2},{6,4},{8,6},{10,8},{12,10},{14,12},{16,14},{18,16},{20... | collective-permute-start | bytes 589832 | tf_op jit(solution)/shard_map/ppermute | solution.py:21
  109.1 1.9 %collective-permute-start.22 = (bf16[24,4096]{1,0:T(8,128)(2,1)S(1)}, bf16[24,4096]{1,0:T(8,128)(2,1)S(1)}, u32[]{:S(2)}, u32[]{:S(2)}) collective-permute-start(bf16[24,4096]{1,0:T(8,128)(2,1)S(1)} %get-tuple-element.39), channel_id=1, source_target_pairs={{2,0},{4,2},{6,4},{8,6},{10,8},{12,10},{14,12},{16,14},{18,16},{20... | collective-permute-start | bytes 589832 | tf_op jit(solution)/shard_map/ppermute | solution.py:21
  111.0 1.3 collective-permute-start.28
  112.3 2.4 %collective-permute-done.16 = bf16[24,4096]{1,0:T(8,128)(2,1)S(1)} collective-permute-done((bf16[24,4096]{1,0:T(8,128)(2,1)S(1)}, bf16[24,4096]{1,0:T(8,128)(2,1)S(1)}, u32[]{:S(2)}, u32[]{:S(2)}) %collective-permute-start.16) | collective-permute-done | bytes 196640 | tf_op jit(solution)/shard_map/ppermute | solution.py:21
  114.8 3.1 %collective-permute-start.17 = (bf16[24,4096]{1,0:T(8,128)(2,1)S(1)}, bf16[24,4096]{1,0:T(8,128)(2,1)S(1)}, u32[]{:S(2)}, u32[]{:S(2)}) collective-permute-start(bf16[24,4096]{1,0:T(8,128)(2,1)S(1)} %add_convert_fusion.10), channel_id=1, source_target_pairs={{2,0},{23,1},{4,2},{1,3},{6,4},{3,5},{8,6},{5,7},{10,8},{7,9},{12,... | collective-permute-start | bytes 589832 | tf_op jit(solution)/shard_map/ppermute | solution.py:21
  118.0 2.0 %collective-permute-start.23 = (bf16[24,4096]{1,0:T(8,128)(2,1)S(1)}, bf16[24,4096]{1,0:T(8,128)(2,1)S(1)}, u32[]{:S(2)}, u32[]{:S(2)}) collective-permute-start(bf16[24,4096]{1,0:T(8,128)(2,1)S(1)} %add_convert_fusion.5), channel_id=1, source_target_pairs={{2,0},{23,1},{4,2},{1,3},{6,4},{3,5},{8,6},{5,7},{10,8},{7,9},{12,... | collective-permute-start | bytes 589832 | tf_op jit(solution)/shard_map/ppermute | solution.py:21
  120.0 2.3 %collective-permute-done.17 = bf16[24,4096]{1,0:T(8,128)(2,1)S(1)} collective-permute-done((bf16[24,4096]{1,0:T(8,128)(2,1)S(1)}, bf16[24,4096]{1,0:T(8,128)(2,1)S(1)}, u32[]{:S(2)}, u32[]{:S(2)}) %collective-permute-start.17) | collective-permute-done | bytes 196640 | tf_op jit(solution)/shard_map/ppermute | solution.py:21
  122.4 4.3 %collective-permute-start.18 = (bf16[24,4096]{1,0:T(8,128)(2,1)S(1)}, bf16[24,4096]{1,0:T(8,128)(2,1)S(1)}, u32[]{:S(2)}, u32[]{:S(2)}) collective-permute-start(bf16[24,4096]{1,0:T(8,128)(2,1)S(1)} %add_convert_fusion.9), channel_id=1, source_target_pairs={{2,0},{23,1},{4,2},{1,3},{6,4},{3,5},{8,6},{5,7},{10,8},{7,9},{12,... | collective-permute-start | bytes 589832 | tf_op jit(solution)/shard_map/ppermute | solution.py:21
  126.8 2.0 %collective-permute-start.24 = (bf16[24,4096]{1,0:T(8,128)(2,1)S(1)}, bf16[24,4096]{1,0:T(8,128)(2,1)S(1)}, u32[]{:S(2)}, u32[]{:S(2)}) collective-permute-start(bf16[24,4096]{1,0:T(8,128)(2,1)S(1)} %add_convert_fusion.4), channel_id=1, source_target_pairs={{2,0},{23,1},{4,2},{1,3},{6,4},{3,5},{8,6},{5,7},{10,8},{7,9},{12,... | collective-permute-start | bytes 589832 | tf_op jit(solution)/shard_map/ppermute | solution.py:21
  128.8 1.1 collective-permute-done.18
  130.0 5.6 %collective-permute-start.19 = (bf16[24,4096]{1,0:T(8,128)(2,1)S(1)}, bf16[24,4096]{1,0:T(8,128)(2,1)S(1)}, u32[]{:S(2)}, u32[]{:S(2)}) collective-permute-start(bf16[24,4096]{1,0:T(8,128)(2,1)S(1)} %add_convert_fusion.8), channel_id=1, source_target_pairs={{2,0},{23,1},{4,2},{1,3},{6,4},{3,5},{8,6},{5,7},{10,8},{7,9},{12,... | collective-permute-start | bytes 589832 | tf_op jit(solution)/shard_map/ppermute | solution.py:21
  135.6 2.0 %collective-permute-start.25 = (bf16[24,4096]{1,0:T(8,128)(2,1)S(1)}, bf16[24,4096]{1,0:T(8,128)(2,1)S(1)}, u32[]{:S(2)}, u32[]{:S(2)}) collective-permute-start(bf16[24,4096]{1,0:T(8,128)(2,1)S(1)} %add_convert_fusion.3), channel_id=1, source_target_pairs={{2,0},{23,1},{4,2},{1,3},{6,4},{3,5},{8,6},{5,7},{10,8},{7,9},{12,... | collective-permute-start | bytes 589832 | tf_op jit(solution)/shard_map/ppermute | solution.py:21
  137.7 1.1 collective-permute-done.19
  138.8 5.6 %collective-permute-start.20 = (bf16[24,4096]{1,0:T(8,128)(2,1)S(1)}, bf16[24,4096]{1,0:T(8,128)(2,1)S(1)}, u32[]{:S(2)}, u32[]{:S(2)}) collective-permute-start(bf16[24,4096]{1,0:T(8,128)(2,1)S(1)} %add_convert_fusion.7), channel_id=1, source_target_pairs={{2,0},{23,1},{4,2},{1,3},{6,4},{3,5},{8,6},{5,7},{10,8},{7,9},{12,... | collective-permute-start | bytes 589832 | tf_op jit(solution)/shard_map/ppermute | solution.py:21
  144.5 2.0 %collective-permute-start.26 = (bf16[24,4096]{1,0:T(8,128)(2,1)S(1)}, bf16[24,4096]{1,0:T(8,128)(2,1)S(1)}, u32[]{:S(2)}, u32[]{:S(2)}) collective-permute-start(bf16[24,4096]{1,0:T(8,128)(2,1)S(1)} %add_convert_fusion.2), channel_id=1, source_target_pairs={{2,0},{23,1},{4,2},{1,3},{6,4},{3,5},{8,6},{5,7},{10,8},{7,9},{12,... | collective-permute-start | bytes 589832 | tf_op jit(solution)/shard_map/ppermute | solution.py:21
  146.5 1.1 collective-permute-done.20
  147.6 5.6 %collective-permute-start.21 = (bf16[24,4096]{1,0:T(8,128)(2,1)S(1)}, bf16[24,4096]{1,0:T(8,128)(2,1)S(1)}, u32[]{:S(2)}, u32[]{:S(2)}) collective-permute-start(bf16[24,4096]{1,0:T(8,128)(2,1)S(1)} %add_convert_fusion.6), channel_id=1, source_target_pairs={{2,0},{23,1},{4,2},{1,3},{6,4},{3,5},{8,6},{5,7},{10,8},{7,9},{12,... | collective-permute-start | bytes 589832 | tf_op jit(solution)/shard_map/ppermute | solution.py:21
  153.3 1.9 %collective-permute-start.27 = (bf16[24,4096]{1,0:T(8,128)(2,1)S(1)}, bf16[24,4096]{1,0:T(8,128)(2,1)S(1)}, u32[]{:S(2)}, u32[]{:S(2)}) collective-permute-start(bf16[24,4096]{1,0:T(8,128)(2,1)S(1)} %add_convert_fusion.1), channel_id=1, source_target_pairs={{2,1},{23,0},{4,3},{1,2},{6,5},{3,4},{8,7},{5,6},{10,9},{7,8},{12,... | collective-permute-start | bytes 589832 | tf_op jit(solution)/shard_map/ppermute | solution.py:21
  155.9 0.5 collective-permute-done.21
  156.4 5.1 %collective-permute-done.27 = bf16[24,4096]{1,0:T(8,128)(2,1)S(1)} collective-permute-done((bf16[24,4096]{1,0:T(8,128)(2,1)S(1)}, bf16[24,4096]{1,0:T(8,128)(2,1)S(1)}, u32[]{:S(2)}, u32[]{:S(2)}) %collective-permute-start.27) | collective-permute-done | bytes 196640 | tf_op jit(solution)/shard_map/ppermute | solution.py:21
  161.5 0.8 select_convert_fusion
  (50 shorter events, 0.9 us)
Async XLA Ops:
  1.8 24.4 %collective-permute-start = (bf16[2,24,4096]{2,1,0:T(8,128)(2,1)}, bf16[2,24,4096]{2,1,0:T(8,128)(2,1)}, u32[]{:S(2)}, u32[]{:S(2)}) collective-permute-start(bf16[2,24,4096]{2,1,0:T(8,128)(2,1)} %pad_maximum_fusion.2), channel_id=1, source_target_pairs={{0,1},{1,0},{2,3},{3,2},{4,5},{5,4},{6,7},{7,6},{8,9},{9,8},{10,11... | collective-permute-start | bytes 1179656 | tf_op jit(solution)/shard_map/ppermute | solution.py:21
  3.7 24.4 %collective-permute-start.6 = (bf16[2,24,4096]{2,1,0:T(8,128)(2,1)}, bf16[2,24,4096]{2,1,0:T(8,128)(2,1)S(1)}, u32[]{:S(2)}, u32[]{:S(2)}) collective-permute-start(bf16[2,24,4096]{2,1,0:T(8,128)(2,1)} %pad_maximum_fusion.2), channel_id=1, source_target_pairs={{0,2},{1,23},{2,4},{3,1},{4,6},{5,3},{6,8},{7,5},{8,10},{9,7},{10,... | collective-permute-start | bytes 1179656 | tf_op jit(solution)/shard_map/ppermute | solution.py:21
  8.0 84.5 %collective-permute-start.13 = (bf16[344,4096]{1,0:T(8,128)(2,1)}, bf16[344,4096]{1,0:T(8,128)(2,1)S(1)}, u32[]{:S(2)}, u32[]{:S(2)}) collective-permute-start(bf16[344,4096]{1,0:T(8,128)(2,1)} %param.8), channel_id=1, source_target_pairs={{0,1},{1,0},{2,3},{3,2},{4,5},{5,4},{6,7},{7,6},{8,9},{9,8},{10,11... | collective-permute-start | bytes 8454152 | tf_op jit(solution)/shard_map/ppermute | solution.py:21
  20.5 5.0 %collective-permute-start.14 = (bf16[344]{0:T(512)(128)(2,1)}, bf16[344]{0:T(512)(128)(2,1)S(1)}, u32[]{:S(2)}, u32[]{:S(2)}) collective-permute-start(bf16[344]{0:T(512)(128)(2,1)} %param.9), channel_id=1, source_target_pairs={{0,1},{1,0},{2,3},{3,2},{4,5},{5,4},{6,7},{7,6},{8,9},{9,8},{10,11... | collective-permute-start | bytes 2072 | tf_op jit(solution)/shard_map/ppermute | solution.py:21
  22.4 72.7 %collective-permute-start.15 = (bf16[344,4096]{1,0:T(8,128)(2,1)}, bf16[344,4096]{1,0:T(8,128)(2,1)}, u32[]{:S(2)}, u32[]{:S(2)}) collective-permute-start(bf16[344,4096]{1,0:T(8,128)(2,1)} %param.10), channel_id=1, source_target_pairs={{0,1},{1,0},{2,3},{3,2},{4,5},{5,4},{6,7},{7,6},{8,9},{9,8},{10,11... | collective-permute-start | bytes 8454152 | tf_op jit(solution)/shard_map/ppermute | solution.py:21
  26.2 11.1 %collective-permute-start.1 = (bf16[2,24,4096]{2,1,0:T(8,128)(2,1)}, bf16[2,24,4096]{2,1,0:T(8,128)(2,1)S(1)}, u32[]{:S(2)}, u32[]{:S(2)}) collective-permute-start(bf16[2,24,4096]{2,1,0:T(8,128)(2,1)} %collective-permute-done), channel_id=1, source_target_pairs={{0,2},{1,23},{2,4},{3,1},{4,6},{5,3},{6,8},{7,5},{8,10},{9,7},{10,... | collective-permute-start | bytes 1179656 | tf_op jit(solution)/shard_map/ppermute | solution.py:21
  28.2 13.4 %collective-permute-start.7 = (bf16[2,24,4096]{2,1,0:T(8,128)(2,1)S(1)}, bf16[2,24,4096]{2,1,0:T(8,128)(2,1)S(1)}, u32[]{:S(2)}, u32[]{:S(2)}) collective-permute-start(bf16[2,24,4096]{2,1,0:T(8,128)(2,1)S(1)} %collective-permute-done.6), channel_id=1, source_target_pairs={{0,2},{1,23},{2,4},{3,1},{4,6},{5,3},{6,8},{7,5},{8,10},{9,7},{10,... | collective-permute-start | bytes 1179656 | tf_op jit(solution)/shard_map/ppermute | solution.py:21
  37.3 10.9 %collective-permute-start.2 = (bf16[2,24,4096]{2,1,0:T(8,128)(2,1)S(1)}, bf16[2,24,4096]{2,1,0:T(8,128)(2,1)S(1)}, u32[]{:S(2)}, u32[]{:S(2)}) collective-permute-start(bf16[2,24,4096]{2,1,0:T(8,128)(2,1)S(1)} %collective-permute-done.1), channel_id=1, source_target_pairs={{0,2},{1,23},{2,4},{3,1},{4,6},{5,3},{6,8},{7,5},{8,10},{9,7},{10,... | collective-permute-start | bytes 1179656 | tf_op jit(solution)/shard_map/ppermute | solution.py:21
  41.5 10.9 %collective-permute-start.8 = (bf16[2,24,4096]{2,1,0:T(8,128)(2,1)S(1)}, bf16[2,24,4096]{2,1,0:T(8,128)(2,1)S(1)}, u32[]{:S(2)}, u32[]{:S(2)}) collective-permute-start(bf16[2,24,4096]{2,1,0:T(8,128)(2,1)S(1)} %collective-permute-done.7), channel_id=1, source_target_pairs={{0,2},{1,23},{2,4},{3,1},{4,6},{5,3},{6,8},{7,5},{8,10},{9,7},{10,... | collective-permute-start | bytes 1179656 | tf_op jit(solution)/shard_map/ppermute | solution.py:21
  48.2 10.9 %collective-permute-start.3 = (bf16[2,24,4096]{2,1,0:T(8,128)(2,1)S(1)}, bf16[2,24,4096]{2,1,0:T(8,128)(2,1)S(1)}, u32[]{:S(2)}, u32[]{:S(2)}) collective-permute-start(bf16[2,24,4096]{2,1,0:T(8,128)(2,1)S(1)} %collective-permute-done.2), channel_id=1, source_target_pairs={{0,2},{1,23},{2,4},{3,1},{4,6},{5,3},{6,8},{7,5},{8,10},{9,7},{10,... | collective-permute-start | bytes 1179656 | tf_op jit(solution)/shard_map/ppermute | solution.py:21
  52.4 10.9 %collective-permute-start.9 = (bf16[2,24,4096]{2,1,0:T(8,128)(2,1)S(1)}, bf16[2,24,4096]{2,1,0:T(8,128)(2,1)S(1)}, u32[]{:S(2)}, u32[]{:S(2)}) collective-permute-start(bf16[2,24,4096]{2,1,0:T(8,128)(2,1)S(1)} %collective-permute-done.8), channel_id=1, source_target_pairs={{0,2},{1,23},{2,4},{3,1},{4,6},{5,3},{6,8},{7,5},{8,10},{9,7},{10,... | collective-permute-start | bytes 1179656 | tf_op jit(solution)/shard_map/ppermute | solution.py:21
  54.4 30.6 %copy-start.2 = (bf16[24,4096]{1,0:T(8,128)(2,1)S(1)}, bf16[24,4096]{1,0:T(8,128)(2,1)}, u32[]{:S(2)}) copy-start(bf16[24,4096]{1,0:T(8,128)(2,1)} %param.7) | copy-start | bytes 589828
  54.4 30.6 %copy-start.4 = (bf16[24,4096]{1,0:T(8,128)(2,1)S(1)}, bf16[24,4096]{1,0:T(8,128)(2,1)}, u32[]{:S(2)}) copy-start(bf16[24,4096]{1,0:T(8,128)(2,1)} %param.6) | copy-start | bytes 589828
  59.1 10.9 %collective-permute-start.4 = (bf16[2,24,4096]{2,1,0:T(8,128)(2,1)S(1)}, bf16[2,24,4096]{2,1,0:T(8,128)(2,1)S(1)}, u32[]{:S(2)}, u32[]{:S(2)}) collective-permute-start(bf16[2,24,4096]{2,1,0:T(8,128)(2,1)S(1)} %collective-permute-done.3), channel_id=1, source_target_pairs={{0,2},{1,23},{2,4},{3,1},{4,6},{5,3},{6,8},{7,5},{8,10},{9,7},{10,... | collective-permute-start | bytes 1179656 | tf_op jit(solution)/shard_map/ppermute | solution.py:21
  63.3 10.9 %collective-permute-start.10 = (bf16[2,24,4096]{2,1,0:T(8,128)(2,1)S(1)}, bf16[2,24,4096]{2,1,0:T(8,128)(2,1)S(1)}, u32[]{:S(2)}, u32[]{:S(2)}) collective-permute-start(bf16[2,24,4096]{2,1,0:T(8,128)(2,1)S(1)} %collective-permute-done.9), channel_id=1, source_target_pairs={{0,2},{1,23},{2,4},{3,1},{4,6},{5,3},{6,8},{7,5},{8,10},{9,7},{10,... | collective-permute-start | bytes 1179656 | tf_op jit(solution)/shard_map/ppermute | solution.py:21
  69.9 10.9 %collective-permute-start.5 = (bf16[2,24,4096]{2,1,0:T(8,128)(2,1)S(1)}, bf16[2,24,4096]{2,1,0:T(8,128)(2,1)S(1)}, u32[]{:S(2)}, u32[]{:S(2)}) collective-permute-start(bf16[2,24,4096]{2,1,0:T(8,128)(2,1)S(1)} %collective-permute-done.4), channel_id=1, source_target_pairs={{0,2},{1,23},{2,4},{3,1},{4,6},{5,3},{6,8},{7,5},{8,10},{9,7},{10,... | collective-permute-start | bytes 1179656 | tf_op jit(solution)/shard_map/ppermute | solution.py:21
  74.1 10.9 %collective-permute-start.11 = (bf16[2,24,4096]{2,1,0:T(8,128)(2,1)S(1)}, bf16[2,24,4096]{2,1,0:T(8,128)(2,1)S(1)}, u32[]{:S(2)}, u32[]{:S(2)}) collective-permute-start(bf16[2,24,4096]{2,1,0:T(8,128)(2,1)S(1)} %collective-permute-done.10), channel_id=1, source_target_pairs={{0,2},{2,4},{4,6},{6,8},{8,10},{10,12},{12,14},{14,16},{16,18},{18... | collective-permute-start | bytes 1179656 | tf_op jit(solution)/shard_map/ppermute | solution.py:21
  76.1 16.4 %copy-start = (bf16[344,4096]{1,0:T(8,128)(2,1)S(1)}, bf16[344,4096]{1,0:T(8,128)(2,1)}, u32[]{:S(2)}) copy-start(bf16[344,4096]{1,0:T(8,128)(2,1)} %param.8) | copy-start | bytes 8454148
  76.1 16.3 %copy-start.7 = (bf16[216,4096]{1,0:T(8,128)(2,1)}, bf16[216,4096]{1,0:T(8,128)(2,1)S(1)}, u32[]{:S(2)}) copy-start(bf16[216,4096]{1,0:T(8,128)(2,1)S(1)} %get-tuple-element.47) | copy-start | bytes 5308420
  80.8 12.3 %copy-start.5 = (bf16[2,24,4096]{2,1,0:T(8,128)(2,1)}, bf16[2,24,4096]{2,1,0:T(8,128)(2,1)S(1)}, u32[]{:S(2)}) copy-start(bf16[2,24,4096]{2,1,0:T(8,128)(2,1)S(1)} %collective-permute-done.5) | copy-start | bytes 1179652
  80.8 10.9 %collective-permute-start.12 = (bf16[2,24,4096]{2,1,0:T(8,128)(2,1)S(1)}, bf16[2,24,4096]{2,1,0:T(8,128)(2,1)S(1)}, u32[]{:S(2)}, u32[]{:S(2)}) collective-permute-start(bf16[2,24,4096]{2,1,0:T(8,128)(2,1)S(1)} %collective-permute-done.5), channel_id=1, source_target_pairs={{0,2},{2,4},{4,6},{6,8},{8,10},{10,12},{12,14},{14,16},{16,18},{18... | collective-permute-start | bytes 1179656 | tf_op jit(solution)/shard_map/ppermute | solution.py:21
  93.1 2.0 %copy-start.1 = (bf16[344,4096]{1,0:T(8,128)(2,1)S(1)}, bf16[344,4096]{1,0:T(8,128)(2,1)}, u32[]{:S(2)}) copy-start(bf16[344,4096]{1,0:T(8,128)(2,1)} %param.10) | copy-start | bytes 8454148
  95.1 2.5 %copy-start.8 = (bf16[216,4096]{1,0:T(8,128)(2,1)S(1)}, bf16[216,4096]{1,0:T(8,128)(2,1)}, u32[]{:S(2)}) copy-start(bf16[216,4096]{1,0:T(8,128)(2,1)} %copy-done.7) | copy-start | bytes 5308420
  101.2 1.0 copy-start.6
  101.2 1.1 copy-start.3
  107.2 7.6 %collective-permute-start.16 = (bf16[24,4096]{1,0:T(8,128)(2,1)S(1)}, bf16[24,4096]{1,0:T(8,128)(2,1)S(1)}, u32[]{:S(2)}, u32[]{:S(2)}) collective-permute-start(bf16[24,4096]{1,0:T(8,128)(2,1)S(1)} %get-tuple-element.38), channel_id=1, source_target_pairs={{2,0},{4,2},{6,4},{8,6},{10,8},{12,10},{14,12},{16,14},{18,16},{20... | collective-permute-start | bytes 589832 | tf_op jit(solution)/shard_map/ppermute | solution.py:21
  109.1 8.8 %collective-permute-start.22 = (bf16[24,4096]{1,0:T(8,128)(2,1)S(1)}, bf16[24,4096]{1,0:T(8,128)(2,1)S(1)}, u32[]{:S(2)}, u32[]{:S(2)}) collective-permute-start(bf16[24,4096]{1,0:T(8,128)(2,1)S(1)} %get-tuple-element.39), channel_id=1, source_target_pairs={{2,0},{4,2},{6,4},{8,6},{10,8},{12,10},{14,12},{16,14},{18,16},{20... | collective-permute-start | bytes 589832 | tf_op jit(solution)/shard_map/ppermute | solution.py:21
  111.0 44.9 %collective-permute-start.28 = (bf16[24,4096]{1,0:T(8,128)(2,1)S(1)}, bf16[24,4096]{1,0:T(8,128)(2,1)S(1)}, u32[]{:S(2)}, u32[]{:S(2)}) collective-permute-start(bf16[24,4096]{1,0:T(8,128)(2,1)S(1)} %get-tuple-element.39), channel_id=1, source_target_pairs={{1,0},{3,2},{5,4},{7,6},{9,8},{11,10},{13,12},{15,14},{17,16},{19,... | collective-permute-start | bytes 589832 | tf_op jit(solution)/shard_map/ppermute | solution.py:21
  114.8 7.6 %collective-permute-start.17 = (bf16[24,4096]{1,0:T(8,128)(2,1)S(1)}, bf16[24,4096]{1,0:T(8,128)(2,1)S(1)}, u32[]{:S(2)}, u32[]{:S(2)}) collective-permute-start(bf16[24,4096]{1,0:T(8,128)(2,1)S(1)} %add_convert_fusion.10), channel_id=1, source_target_pairs={{2,0},{23,1},{4,2},{1,3},{6,4},{3,5},{8,6},{5,7},{10,8},{7,9},{12,... | collective-permute-start | bytes 589832 | tf_op jit(solution)/shard_map/ppermute | solution.py:21
  118.0 8.8 %collective-permute-start.23 = (bf16[24,4096]{1,0:T(8,128)(2,1)S(1)}, bf16[24,4096]{1,0:T(8,128)(2,1)S(1)}, u32[]{:S(2)}, u32[]{:S(2)}) collective-permute-start(bf16[24,4096]{1,0:T(8,128)(2,1)S(1)} %add_convert_fusion.5), channel_id=1, source_target_pairs={{2,0},{23,1},{4,2},{1,3},{6,4},{3,5},{8,6},{5,7},{10,8},{7,9},{12,... | collective-permute-start | bytes 589832 | tf_op jit(solution)/shard_map/ppermute | solution.py:21
  122.4 7.6 %collective-permute-start.18 = (bf16[24,4096]{1,0:T(8,128)(2,1)S(1)}, bf16[24,4096]{1,0:T(8,128)(2,1)S(1)}, u32[]{:S(2)}, u32[]{:S(2)}) collective-permute-start(bf16[24,4096]{1,0:T(8,128)(2,1)S(1)} %add_convert_fusion.9), channel_id=1, source_target_pairs={{2,0},{23,1},{4,2},{1,3},{6,4},{3,5},{8,6},{5,7},{10,8},{7,9},{12,... | collective-permute-start | bytes 589832 | tf_op jit(solution)/shard_map/ppermute | solution.py:21
  126.8 8.8 %collective-permute-start.24 = (bf16[24,4096]{1,0:T(8,128)(2,1)S(1)}, bf16[24,4096]{1,0:T(8,128)(2,1)S(1)}, u32[]{:S(2)}, u32[]{:S(2)}) collective-permute-start(bf16[24,4096]{1,0:T(8,128)(2,1)S(1)} %add_convert_fusion.4), channel_id=1, source_target_pairs={{2,0},{23,1},{4,2},{1,3},{6,4},{3,5},{8,6},{5,7},{10,8},{7,9},{12,... | collective-permute-start | bytes 589832 | tf_op jit(solution)/shard_map/ppermute | solution.py:21
  130.0 8.7 %collective-permute-start.19 = (bf16[24,4096]{1,0:T(8,128)(2,1)S(1)}, bf16[24,4096]{1,0:T(8,128)(2,1)S(1)}, u32[]{:S(2)}, u32[]{:S(2)}) collective-permute-start(bf16[24,4096]{1,0:T(8,128)(2,1)S(1)} %add_convert_fusion.8), channel_id=1, source_target_pairs={{2,0},{23,1},{4,2},{1,3},{6,4},{3,5},{8,6},{5,7},{10,8},{7,9},{12,... | collective-permute-start | bytes 589832 | tf_op jit(solution)/shard_map/ppermute | solution.py:21
  135.6 8.8 %collective-permute-start.25 = (bf16[24,4096]{1,0:T(8,128)(2,1)S(1)}, bf16[24,4096]{1,0:T(8,128)(2,1)S(1)}, u32[]{:S(2)}, u32[]{:S(2)}) collective-permute-start(bf16[24,4096]{1,0:T(8,128)(2,1)S(1)} %add_convert_fusion.3), channel_id=1, source_target_pairs={{2,0},{23,1},{4,2},{1,3},{6,4},{3,5},{8,6},{5,7},{10,8},{7,9},{12,... | collective-permute-start | bytes 589832 | tf_op jit(solution)/shard_map/ppermute | solution.py:21
  138.8 8.8 %collective-permute-start.20 = (bf16[24,4096]{1,0:T(8,128)(2,1)S(1)}, bf16[24,4096]{1,0:T(8,128)(2,1)S(1)}, u32[]{:S(2)}, u32[]{:S(2)}) collective-permute-start(bf16[24,4096]{1,0:T(8,128)(2,1)S(1)} %add_convert_fusion.7), channel_id=1, source_target_pairs={{2,0},{23,1},{4,2},{1,3},{6,4},{3,5},{8,6},{5,7},{10,8},{7,9},{12,... | collective-permute-start | bytes 589832 | tf_op jit(solution)/shard_map/ppermute | solution.py:21
  144.5 8.8 %collective-permute-start.26 = (bf16[24,4096]{1,0:T(8,128)(2,1)S(1)}, bf16[24,4096]{1,0:T(8,128)(2,1)S(1)}, u32[]{:S(2)}, u32[]{:S(2)}) collective-permute-start(bf16[24,4096]{1,0:T(8,128)(2,1)S(1)} %add_convert_fusion.2), channel_id=1, source_target_pairs={{2,0},{23,1},{4,2},{1,3},{6,4},{3,5},{8,6},{5,7},{10,8},{7,9},{12,... | collective-permute-start | bytes 589832 | tf_op jit(solution)/shard_map/ppermute | solution.py:21
  147.6 8.8 %collective-permute-start.21 = (bf16[24,4096]{1,0:T(8,128)(2,1)S(1)}, bf16[24,4096]{1,0:T(8,128)(2,1)S(1)}, u32[]{:S(2)}, u32[]{:S(2)}) collective-permute-start(bf16[24,4096]{1,0:T(8,128)(2,1)S(1)} %add_convert_fusion.6), channel_id=1, source_target_pairs={{2,0},{23,1},{4,2},{1,3},{6,4},{3,5},{8,6},{5,7},{10,8},{7,9},{12,... | collective-permute-start | bytes 589832 | tf_op jit(solution)/shard_map/ppermute | solution.py:21
  153.3 8.2 %collective-permute-start.27 = (bf16[24,4096]{1,0:T(8,128)(2,1)S(1)}, bf16[24,4096]{1,0:T(8,128)(2,1)S(1)}, u32[]{:S(2)}, u32[]{:S(2)}) collective-permute-start(bf16[24,4096]{1,0:T(8,128)(2,1)S(1)} %add_convert_fusion.1), channel_id=1, source_target_pairs={{2,1},{23,0},{4,3},{1,2},{6,5},{3,4},{8,7},{5,6},{10,9},{7,8},{12,... | collective-permute-start | bytes 589832 | tf_op jit(solution)/shard_map/ppermute | solution.py:21
